TPU v7x, 256 devices: a whole 4x4x8 slice. The times are simulated.
256 devices in a mesh: frame: 16 (over y_hi, x, core), head: 16 (over y_lo, z).
Axes of the slice: x: 4, y: 4 (y_hi: 2, y_lo: 2; y = y_hi * 2 + y_lo), z: 8, core: 2. Of those that a mesh axis runs over, the one named last changes fastest.
Arguments:
- queries: bfloat16 [32768, 2048], P('frame', 'head'), may hold values from -64 to 64
- keys: bfloat16 [32768, 2048], P('frame', 'head'), may hold values from -4 to 4
- values: bfloat16 [32768, 2048], P('frame', 'head'), may hold values from -6 to 6
- block_mask: int32 [16, 16, 32, 45], P('head', 'frame'), may hold values 0 or 1
- out_weight: bfloat16 [2048, 3072], P('head'), may hold values from -1 to 1
Outputs:
- projected: bfloat16 [32768, 3072], P(('frame', 'head'))
All inputs are finite; a program needn't handle non-finite values. No bound on the sum of `block_mask` on one device may be relied on, other than what follows from the above.
Results may differ from a plain program's by a relative error of at most 0.018.
Values may be sent and summed in bfloat16 or wider, within the bound.
A program may use at most 128 MiB of HBM per device.

v0:
```python
import math

import jax
import jax.numpy as jnp
from jax import lax
from jax.sharding import PartitionSpec as P

HEAD_DIM = 128
TROWS = 4
TCOLS = 8
WIN = 45
TILE = 64


def padded_2(block, sides, width):
    for axis, dim in sides:
        count = lax.axis_size(axis)
        forward = [(i, i + 1) for i in range(count - 1)]
        backward = [(target, source) for source, target in forward]
        low = lax.ppermute(
            lax.slice_in_dim(block, block.shape[dim] - width, None, axis=dim), axis, forward
        )
        high = lax.ppermute(lax.slice_in_dim(block, 0, width, axis=dim), axis, backward)
        block = jnp.concatenate([low, block, high], axis=dim)
    return block


def tile_allowed(mask_rows, frame, row, frames_total):
    frame_step = jnp.arange(3, dtype=jnp.int32)[None, :, None, None]
    row_step = jnp.arange(3, dtype=jnp.int32)[None, None, :, None]
    query_col = jnp.arange(TCOLS, dtype=jnp.int32)[:, None, None, None]
    key_col = jnp.arange(TCOLS, dtype=jnp.int32)[None, None, None, :]
    col_step = key_col - query_col
    offset = frame_step * 15 + row_step * 5 + col_step + 2
    picked = offset[..., None] == jnp.arange(WIN, dtype=jnp.int32)
    chosen = jnp.sum(jnp.where(picked, mask_rows[:, None, None, None, :], 0), axis=-1) > 0
    centre = (frame_step == 1) & (row_step == 1) & (col_step == 0)
    key_frame = frame + frame_step - 1
    key_row = row + row_step - 1
    inside = (key_frame >= 0) & (key_frame < frames_total) & (key_row >= 0) & (key_row < TROWS)
    nearby = jnp.abs(col_step) <= 2
    allowed = (chosen | centre) & nearby & inside
    expanded = jnp.broadcast_to(allowed[:, None, :, :, :, None], (TCOLS, TILE, 3, 3, TCOLS, TILE))
    return expanded.reshape(TCOLS * TILE, 9 * TCOLS * TILE)


def attend_block(query_block, key_block, value_block, allowed):
    scale = 1.0 / math.sqrt(HEAD_DIM)
    scores = jnp.dot(query_block, key_block.T, preferred_element_type=jnp.float32) * scale
    scores = jnp.where(allowed, scores, -jnp.inf)
    peak = jnp.max(scores, axis=1, keepdims=True)
    expos = jnp.exp(scores - peak)
    weights = (expos / jnp.sum(expos, axis=1, keepdims=True)).astype(jnp.bfloat16)
    return jnp.dot(weights, value_block, preferred_element_type=jnp.float32).astype(jnp.bfloat16)


def on_device(queries, keys, values, block_mask, out_weight):
    span = TCOLS * TILE
    tok_dev = queries.shape[0]
    width = queries.shape[1]
    heads_here = width // HEAD_DIM
    frames_here = tok_dev // (TROWS * span)
    frames_total = frames_here * lax.axis_size("frame")
    first_frame = lax.axis_index("frame") * frames_here
    pair = jnp.stack([keys, values]).reshape(2, frames_here, TROWS, span, width)
    padded = padded_2(pair, (("frame", 1),), 1)
    padded = jnp.pad(padded, ((0, 0), (0, 0), (1, 1), (0, 0), (0, 0)))
    query_grid = queries.reshape(frames_here, TROWS, span, width)
    mask_grid = block_mask.reshape(heads_here, frames_here, TROWS, TCOLS, WIN)

    def one_block(which):
        head = which // (frames_here * TROWS)
        frame = which // TROWS % frames_here
        row = which % TROWS
        zero = jnp.zeros((), jnp.int32)
        column = head * HEAD_DIM
        query_block = lax.dynamic_slice(
            query_grid, (frame, row, zero, column), (1, 1, span, HEAD_DIM)
        ).reshape(span, HEAD_DIM)
        pair_block = lax.dynamic_slice(
            padded, (zero, frame, row, zero, column), (2, 3, 3, span, HEAD_DIM)
        ).reshape(2, 9 * span, HEAD_DIM)
        mask_rows = lax.dynamic_slice(
            mask_grid, (head, frame, row, zero, zero), (1, 1, 1, TCOLS, WIN)
        ).reshape(TCOLS, WIN)
        allowed = tile_allowed(mask_rows, first_frame + frame, row, frames_total)
        return attend_block(query_block, pair_block[0], pair_block[1], allowed)

    blocks = lax.map(one_block, jnp.arange(heads_here * frames_here * TROWS, dtype=jnp.int32))
    attention = (
        blocks.reshape(heads_here, frames_here, TROWS, span, HEAD_DIM)
        .transpose(1, 2, 3, 0, 4)
        .reshape(tok_dev, width)
    )
    return lax.psum_scatter(
        jnp.dot(attention, out_weight, preferred_element_type=jnp.float32).astype(jnp.bfloat16),
        "head",
        scatter_dimension=0,
        tiled=True,
    )


def solution(mesh):
    return jax.shard_map(
        on_device,
        mesh=mesh,
        in_specs=(
            P("frame", "head"),
            P("frame", "head"),
            P("frame", "head"),
            P("head", "frame", None, None),
            P("head", None),
        ),
        out_specs=P(("frame", "head"), None),
        check_vma=False,
    )
```

profile of v0, /device:TPU:17, one launch (start us, length us, event | category | flops | bytes accessed | tf_op | source)
XLA Modules:
  0.0 312.0 jit_solution(3387030555236973554)
XLA Ops:
  6.5 2.4 pad_maximum_fusion
  8.9 3.7 %collective-permute-start = (bf16[2,1,4,512,128]{4,3,2,1,0:T(8,128)(2,1)}, bf16[2,1,4,512,128]{4,3,2,1,0:T(8,128)(2,1)S(1)}, u32[]{:S(2)}, u32[]{:S(2)}) collective-permute-start(bf16[2,1,4,512,128]{4,3,2,1,0:T(8,128)(2,1)} %pad_maximum_fusion), channel_id=1, source_target_pairs={{0,16},{16,32},{32,48},{48,64},{64,80},{80,96},{96,112},{112,128},... | collective-permute-start | bytes 3145736 | tf_op jit(solution)/shard_map/ppermute | solution.py:20
  12.6 1.9 collective-permute-start.1
  14.5 10.1 %collective-permute-done = bf16[2,1,4,512,128]{4,3,2,1,0:T(8,128)(2,1)S(1)} collective-permute-done((bf16[2,1,4,512,128]{4,3,2,1,0:T(8,128)(2,1)}, bf16[2,1,4,512,128]{4,3,2,1,0:T(8,128)(2,1)S(1)}, u32[]{:S(2)}, u32[]{:S(2)}) %collective-permute-start) | collective-permute-done | bytes 1048608 | tf_op jit(solution)/shard_map/ppermute | solution.py:20
  24.6 4.5 %collective-permute-done.1 = bf16[2,1,4,512,128]{4,3,2,1,0:T(8,128)(2,1)S(1)} collective-permute-done((bf16[2,1,4,512,128]{4,3,2,1,0:T(8,128)(2,1)}, bf16[2,1,4,512,128]{4,3,2,1,0:T(8,128)(2,1)S(1)}, u32[]{:S(2)}, u32[]{:S(2)}) %collective-permute-start.1) | collective-permute-done | bytes 1048608 | tf_op jit(solution)/shard_map/ppermute | solution.py:23
  29.1 4.8 %select_maximum_fusion = bf16[2,3,6,512,128]{4,3,2,1,0:T(8,128)(2,1)} fusion(bf16[2,1,4,512,128]{4,3,2,1,0:T(8,128)(2,1)S(1)} %collective-permute-done.1, bf16[2,1,4,512,128]{4,3,2,1,0:T(8,128)(2,1)S(1)} %collective-permute-done, bf16[1,1,4,512,128]{4,3,2,1,0:T(8,128)(2,1)} %bitcast.44, bf16[1,1,4,512,128]{4,3,2,1,0:T(8,128)(2,1)} %bitcast.46), kind=kLoop, calls=%fused_computation.35 | loop fusion | flops 35389440 | bytes 7864320 | tf_op jit(solution)/shard_map/concatenate | solution.py:24
  33.9 115.8 %while.13 = (s32[]{:T(128)}, bf16[4,512,128]{2,1,0:T(8,128)(2,1)}, s32[4]{0:T(128)S(1)}, s32[1,1,4,8,45]{4,3,2,1,0:T(8,128)}, s32[]{:T(128)}, /*index=5*/bf16[1,...) while((s32[]{:T(128)}, bf16[4,512,128]{2,1,0:T(8,128)(2,1)}, ...), condition=%wide.region_4.5_spmd, body=%wide.region_0.4_spmd.sunk | while | flops 1226980096 | bytes 45115500 | solution.py:89
  33.9 0.7 dynamic_slice.44
  36.5 0.7 dynamic-slice_bitcast_fusion.2
  37.2 0.1 broadcast_add_fusion.2
  37.2 0.1 add_add_fusion.3
  37.3 1.4 select_reduce_fusion.2
  38.8 0.1 and_and_fusion.4
  38.9 0.1 broadcast_and_fusion.2
  38.9 0.1 and_and_fusion.5
  39.0 3.4 %broadcast_in_dim.73 = pred[8,64,3,3,8,64]{5,4,3,2,1,0:T(8,128)(4,1)} broadcast(pred[8,3,3,8]{3,2,1,0:T(4,128)(4,1)S(1)} %and_and_fusion.5), dimensions={0,2,3,4} | broadcast | bytes 2359872 | tf_op jit(solution)/shard_map/while/body/eval_jaxpr/broadcast_in_dim | solution.py:43
  42.5 11.3 %reshape.262 = pred[512,4608]{1,0:T(32,128)(4,1)S(1)} reshape(pred[8,64,3,3,8,64]{5,4,3,2,1,0:T(8,128)(4,1)} %broadcast_in_dim.73) | data formatting | bytes 4718592 | tf_op jit(solution)/shard_map/while/body/eval_jaxpr/reshape | solution.py:44
  53.8 1.8 constant_dynamic-slice_fusion.3
  55.7 2.9 fusion.29
  58.6 1.4 fusion.30
  60.0 2.8 fusion.31
  62.8 0.6 dynamic_slice.44
  65.4 0.7 dynamic-slice_bitcast_fusion.2
  66.1 0.1 broadcast_add_fusion.2
  66.2 0.1 add_add_fusion.3
  66.3 1.4 select_reduce_fusion.2
  67.7 0.1 and_and_fusion.4
  67.8 0.1 broadcast_and_fusion.2
  67.9 0.1 and_and_fusion.5
  68.0 3.4 %broadcast_in_dim.73 = pred[8,64,3,3,8,64]{5,4,3,2,1,0:T(8,128)(4,1)} broadcast(pred[8,3,3,8]{3,2,1,0:T(4,128)(4,1)S(1)} %and_and_fusion.5), dimensions={0,2,3,4} | broadcast | bytes 2359872 | tf_op jit(solution)/shard_map/while/body/eval_jaxpr/broadcast_in_dim | solution.py:43
  71.4 11.3 %reshape.262 = pred[512,4608]{1,0:T(32,128)(4,1)S(1)} reshape(pred[8,64,3,3,8,64]{5,4,3,2,1,0:T(8,128)(4,1)} %broadcast_in_dim.73) | data formatting | bytes 4718592 | tf_op jit(solution)/shard_map/while/body/eval_jaxpr/reshape | solution.py:44
  82.8 1.8 constant_dynamic-slice_fusion.3
  84.6 2.9 fusion.29
  87.6 1.4 fusion.30
  89.0 2.8 fusion.31
  91.8 0.6 dynamic_slice.44
  94.4 0.7 dynamic-slice_bitcast_fusion.2
  95.1 0.1 broadcast_add_fusion.2
  95.2 0.1 add_add_fusion.3
  95.2 1.4 select_reduce_fusion.2
  96.7 0.1 and_and_fusion.4
  96.8 0.1 broadcast_and_fusion.2
  96.9 0.1 and_and_fusion.5
  97.0 3.4 %broadcast_in_dim.73 = pred[8,64,3,3,8,64]{5,4,3,2,1,0:T(8,128)(4,1)} broadcast(pred[8,3,3,8]{3,2,1,0:T(4,128)(4,1)S(1)} %and_and_fusion.5), dimensions={0,2,3,4} | broadcast | bytes 2359872 | tf_op jit(solution)/shard_map/while/body/eval_jaxpr/broadcast_in_dim | solution.py:43
  100.4 11.3 %reshape.262 = pred[512,4608]{1,0:T(32,128)(4,1)S(1)} reshape(pred[8,64,3,3,8,64]{5,4,3,2,1,0:T(8,128)(4,1)} %broadcast_in_dim.73) | data formatting | bytes 4718592 | tf_op jit(solution)/shard_map/while/body/eval_jaxpr/reshape | solution.py:44
  111.7 1.8 constant_dynamic-slice_fusion.3
  113.6 2.9 fusion.29
  116.5 1.4 fusion.30
  117.9 2.8 fusion.31
  120.8 0.6 dynamic_slice.44
  123.3 0.7 dynamic-slice_bitcast_fusion.2
  124.1 0.1 add_add_fusion.3
  124.2 1.4 select_reduce_fusion.2
  125.6 0.1 and_and_fusion.4
  125.7 0.1 broadcast_and_fusion.2
  125.8 0.1 and_and_fusion.5
  125.9 3.4 %broadcast_in_dim.73 = pred[8,64,3,3,8,64]{5,4,3,2,1,0:T(8,128)(4,1)} broadcast(pred[8,3,3,8]{3,2,1,0:T(4,128)(4,1)S(1)} %and_and_fusion.5), dimensions={0,2,3,4} | broadcast | bytes 2359872 | tf_op jit(solution)/shard_map/while/body/eval_jaxpr/broadcast_in_dim | solution.py:43
  129.4 11.3 %reshape.262 = pred[512,4608]{1,0:T(32,128)(4,1)S(1)} reshape(pred[8,64,3,3,8,64]{5,4,3,2,1,0:T(8,128)(4,1)} %broadcast_in_dim.73) | data formatting | bytes 4718592 | tf_op jit(solution)/shard_map/while/body/eval_jaxpr/reshape | solution.py:44
  140.7 1.8 constant_dynamic-slice_fusion.3
  142.5 2.9 fusion.29
  145.5 1.4 fusion.30
  146.9 2.8 fusion.31
  149.7 7.5 %convolution_convert_fusion = bf16[2048,3072]{1,0:T(8,128)(2,1)} fusion(bf16[2048,128]{1,0:T(8,128)(2,1)} %bitcast.48, bf16[128,3072]{1,0:T(8,128)(2,1)S(1)} %copy-done), kind=kOutput, calls=%fused_computation.33 | convolution fusion | flops 1616904192 | bytes 13893632 | tf_op jit(solution)/shard_map/dot_general | solution.py:96
  157.2 147.9 %reduce-scatter.2.cloned.1.call-done = bf16[128,3072]{1,0:T(8,128)(2,1)} async-done(((bf16[2048,3072]{1,0:T(8,128)(2,1)}), bf16[128,3072]{1,0:T(8,128)(2,1)}) %reduce-scatter.2.cloned.1.call-update) | async-done | bytes 786448 | tf_op jit(solution)/shard_map/reduce_scatter | solution.py:95
  (31 shorter events, 0.3 us)
Async XLA Ops:
  6.5 143.2 %copy-start = (bf16[128,3072]{1,0:T(8,128)(2,1)S(1)}, bf16[128,3072]{1,0:T(8,128)(2,1)}, u32[]{:S(2)}) copy-start(bf16[128,3072]{1,0:T(8,128)(2,1)} %param.11) | copy-start | bytes 2359300
  6.5 298.6 %reduce-scatter.2.cloned.1.call-start = ((), (), s32[]{:S(2)}) async-start(), calls=%async_computation.1 | async-start | bytes 13369344 | tf_op jit(solution)/shard_map/reduce_scatter | solution.py:95
  8.9 15.7 %collective-permute-start = (bf16[2,1,4,512,128]{4,3,2,1,0:T(8,128)(2,1)}, bf16[2,1,4,512,128]{4,3,2,1,0:T(8,128)(2,1)S(1)}, u32[]{:S(2)}, u32[]{:S(2)}) collective-permute-start(bf16[2,1,4,512,128]{4,3,2,1,0:T(8,128)(2,1)} %pad_maximum_fusion), channel_id=1, source_target_pairs={{0,16},{16,32},{32,48},{48,64},{64,80},{80,96},{96,112},{112,128},... | collective-permute-start | bytes 3145736 | tf_op jit(solution)/shard_map/ppermute | solution.py:20
  12.6 16.5 %collective-permute-start.1 = (bf16[2,1,4,512,128]{4,3,2,1,0:T(8,128)(2,1)}, bf16[2,1,4,512,128]{4,3,2,1,0:T(8,128)(2,1)S(1)}, u32[]{:S(2)}, u32[]{:S(2)}) collective-permute-start(bf16[2,1,4,512,128]{4,3,2,1,0:T(8,128)(2,1)} %pad_maximum_fusion), channel_id=1, source_target_pairs={{16,0},{32,16},{48,32},{64,48},{80,64},{96,80},{112,96},{128,112},... | collective-permute-start | bytes 3145736 | tf_op jit(solution)/shard_map/ppermute | solution.py:23
Sparse Core Ops, SparseCore 0:
  157.3 147.7 reduce-scatter.1
where the time goes:
time: 314 us; the launch traced here: 312 us
  waiting for transfers between devices  162 us (52%)
  local copies, waits for them, and re-layouts  71.7 us (23%)
  matrix products  30.6 us (10%)
  other arithmetic  20.2 us (6%)
  between operations  13.4 us (4%)
  loops' own time  7.91 us (3%)
  starting transfers between devices  5.59 us (2%)
    reduce_scatter x1, waiting for transfers between devices, on_device(): lax.psum_scatter(jnp.dot(attention, out_weight, preferred_element_type=jn...  148 us
    reshape x4, local copies, waits for them, and re-layouts, tile_allowed(): return expanded.reshape(TCOLS * TILE, 9 * TCOLS * TILE)  45.2 us
    broadcast_in_dim x4, local copies, waits for them, and re-layouts, tile_allowed(): jnp.broadcast_to(allowed[:, None, :, :, :, None], (TCOLS, TILE, 3, 3, TCO...  13.8 us
    dot_general x4, matrix products, attend_block(): jnp.dot(query_block, key_block.T, preferred_element_type=jnp.float32)  11.8 us
    dot_general x4, matrix products, attend_block(): jnp.dot(weights, value_block, preferred_element_type=jnp.float32)  11.4 us
    ppermute x1, waiting for transfers between devices, padded_2(): lax.ppermute(lax.slice_in_dim(block, block.shape[dim] - width, None, axis...  10.1 us
    another operation x1, loops' own time, on_device(): lax.map(one_block, jnp.arange(heads_here * frames_here * TROWS, dtype=jnp...  7.91 us
    dot_general x1, matrix products, on_device(): jnp.dot(attention, out_weight, preferred_element_type=jnp.float32)  7.48 us
  transfers between devices with their start and end apart: 3, of which 3 were waited for; matrix products, arithmetic and copies ran while one was open for 0% of the time, Pallas kernels for 0%

commit v1 on v0

--- a/solution.py
+++ b/solution.py
@@ -92,12 +92,9 @@
         .transpose(1, 2, 3, 0, 4)
         .reshape(tok_dev, width)
     )
-    return lax.psum_scatter(
-        jnp.dot(attention, out_weight, preferred_element_type=jnp.float32).astype(jnp.bfloat16),
-        "head",
-        scatter_dimension=0,
-        tiled=True,
-    )
+    full_weight = lax.all_gather(out_weight, "head", axis=0, tiled=True)
+    gathered = lax.all_to_all(attention, "head", 0, 1, tiled=True)
+    return jnp.dot(gathered, full_weight, preferred_element_type=jnp.float32).astype(jnp.bfloat16)
 
 
 def solution(mesh):

time: 314 us -> 195 us (0.62)
  the two profiles are of different devices: /device:TPU:17 before, /device:TPU:7 now
where the time goes in v1:
time: 195 us; the launch traced here: 194 us
  local copies, waits for them, and re-layouts  71.7 us (37%)
  matrix products  28.1 us (14%)
  blocking collectives  23.2 us (12%)
  waiting for transfers between devices  22.7 us (12%)
  other arithmetic  19.2 us (10%)
  between operations  13.4 us (7%)
  loops' own time  8.14 us (4%)
  starting transfers between devices  7.22 us (4%)
    reshape x4, local copies, waits for them, and re-layouts, tile_allowed(): return expanded.reshape(TCOLS * TILE, 9 * TCOLS * TILE)  45.2 us
    all_to_all x1, blocking collectives, on_device(): gathered = lax.all_to_all(attention, 'head', 0, 1, tiled=True)  23.2 us
    broadcast_in_dim x4, local copies, waits for them, and re-layouts, tile_allowed(): jnp.broadcast_to(allowed[:, None, :, :, :, None], (TCOLS, TILE, 3, 3, TCO...  13.7 us
    ppermute x1, waiting for transfers between devices, padded_2(): lax.ppermute(lax.slice_in_dim(block, 0, width, axis=dim), axis, backward)  12.2 us
    dot_general x4, matrix products, attend_block(): jnp.dot(query_block, key_block.T, preferred_element_type=jnp.float32)  11.8 us
    ppermute x1, waiting for transfers between devices, padded_2(): lax.ppermute(lax.slice_in_dim(block, block.shape[dim] - width, None, axis...  9.78 us
    dot_general x4, matrix products, attend_block(): jnp.dot(weights, value_block, preferred_element_type=jnp.float32)  9.07 us
    another operation x1, loops' own time, on_device(): lax.map(one_block, jnp.arange(heads_here * frames_here * TROWS, dtype=jnp...  8.14 us
  transfers between devices with their start and end apart: 3, of which 2 were waited for; matrix products, arithmetic and copies ran while one was open for 58% of the time, Pallas kernels for 0%

profile of v1, /device:TPU:7, one launch (start us, length us, event | category | flops | bytes accessed | tf_op | source)
XLA Modules:
  0.0 193.8 jit_solution(9423422050248519275)
XLA Ops:
  6.5 0.7 all-gather.2.cloned.1.call-update
  7.3 1.3 pad_maximum_fusion
  8.6 5.3 %collective-permute-start = (bf16[2,1,4,512,128]{4,3,2,1,0:T(8,128)(2,1)S(1)}, bf16[2,1,4,512,128]{4,3,2,1,0:T(8,128)(2,1)S(1)}, u32[]{:S(2)}, u32[]{:S(2)}) collective-permute-start(bf16[2,1,4,512,128]{4,3,2,1,0:T(8,128)(2,1)S(1)} %pad_maximum_fusion), channel_id=1, source_target_pairs={{0,16},{16,32},{32,48},{48,64},{64,80},{80,96},{96,112},{112,128},... | collective-permute-start | bytes 3145736 | tf_op jit(solution)/shard_map/ppermute | solution.py:20
  13.9 1.9 collective-permute-start.1
  15.8 9.8 %collective-permute-done = bf16[2,1,4,512,128]{4,3,2,1,0:T(8,128)(2,1)S(1)} collective-permute-done((bf16[2,1,4,512,128]{4,3,2,1,0:T(8,128)(2,1)S(1)}, bf16[2,1,4,512,128]{4,3,2,1,0:T(8,128)(2,1)S(1)}, u32[]{:S(2)}, u32[]{:S(2)}) %collective-permute-start) | collective-permute-done | bytes 1048608 | tf_op jit(solution)/shard_map/ppermute | solution.py:20
  25.6 12.2 %collective-permute-done.1 = bf16[2,1,4,512,128]{4,3,2,1,0:T(8,128)(2,1)S(1)} collective-permute-done((bf16[2,1,4,512,128]{4,3,2,1,0:T(8,128)(2,1)S(1)}, bf16[2,1,4,512,128]{4,3,2,1,0:T(8,128)(2,1)S(1)}, u32[]{:S(2)}, u32[]{:S(2)}) %collective-permute-start.1) | collective-permute-done | bytes 1048608 | tf_op jit(solution)/shard_map/ppermute | solution.py:23
  37.8 4.8 %select_maximum_fusion = bf16[2,3,6,512,128]{4,3,2,1,0:T(8,128)(2,1)} fusion(bf16[2,1,4,512,128]{4,3,2,1,0:T(8,128)(2,1)S(1)} %collective-permute-done.1, bf16[2,1,4,512,128]{4,3,2,1,0:T(8,128)(2,1)S(1)} %collective-permute-done, bf16[1,1,4,512,128]{4,3,2,1,0:T(8,128)(2,1)} %bitcast.48, bf16[1,1,4,512,128]{4,3,2,1,0:T(8,128)(2,1)} %bitcast.50), kind=kLoop, calls=%fused_computation.34 | loop fusion | flops 35389440 | bytes 7864320 | tf_op jit(solution)/shard_map/concatenate | solution.py:24
  42.6 113.6 %while.13 = (s32[]{:T(128)}, bf16[4,512,128]{2,1,0:T(8,128)(2,1)S(1)}, s32[4]{0:T(128)S(1)}, s32[1,1,4,8,45]{4,3,2,1,0:T(8,128)}, s32[]{:T(128)}, /*index=5*/bf1...) while((s32[]{:T(128)}, ...), condition=%wide.region_4.5_spmd, body=%wide.region_0.4_spmd.sunk | while | flops 1226980096 | bytes 45114992 | solution.py:89
  42.6 0.6 dynamic_slice.44
  45.2 0.7 dynamic-slice_bitcast_fusion.2
  45.9 0.1 broadcast_add_fusion.2
  45.9 0.1 add_add_fusion.3
  46.0 1.4 select_reduce_fusion.2
  47.5 0.1 and_and_fusion.4
  47.6 0.1 broadcast_and_fusion.2
  47.7 0.1 and_and_fusion.5
  47.8 3.4 %broadcast_in_dim.73 = pred[8,64,3,3,8,64]{5,4,3,2,1,0:T(8,128)(4,1)} broadcast(pred[8,3,3,8]{3,2,1,0:T(4,128)(4,1)S(1)} %and_and_fusion.5), dimensions={0,2,3,4} | broadcast | bytes 2359872 | tf_op jit(solution)/shard_map/while/body/eval_jaxpr/broadcast_in_dim | solution.py:43
  51.2 11.3 %reshape.266 = pred[512,4608]{1,0:T(32,128)(4,1)S(1)} reshape(pred[8,64,3,3,8,64]{5,4,3,2,1,0:T(8,128)(4,1)} %broadcast_in_dim.73) | data formatting | bytes 4718592 | tf_op jit(solution)/shard_map/while/body/eval_jaxpr/reshape | solution.py:44
  62.5 1.9 constant_dynamic-slice_fusion.3
  64.4 2.9 %fusion.29 = (f32[512]{0:T(512)S(1)}, f32[512,4608]{1,0:T(8,128)S(1)}) fusion(pred[512,4608]{1,0:T(32,128)(4,1)S(1)} %reshape.266, bf16[4608,128]{1,0:T(8,128)(2,1)S(1)} %bitcast.43, bf16[1,4,512,128]{3,2,1,0:T(8,128)(2,1)} %get-tuple-element.246, s32[]{:T(128)S(6)} %select_n.79), kind=kOutput, calls=%fused_computation.41.clone.1 | convolution fusion | flops 611057152 | bytes 13109252 | tf_op jit(solution)/shard_map/while/body/eval_jaxpr/dot_general | solution.py:49
  67.3 1.4 fusion.30
  68.7 2.3 %fusion.31 = bf16[4,512,128]{2,1,0:T(8,128)(2,1)S(1)} fusion(bf16[4,512,128]{2,1,0:T(8,128)(2,1)S(1)} %get-tuple-element.229, s32[]{:T(128)} %get-tuple-element.228, bf16[4608,128]{1,0:T(8,128)(2,1)S(1)} %bitcast.44, f32[512,4608]{1,0:T(8,128)S(1)} %get-tuple-element.213, f32[512]{0:T(512)S(1)} %fusion.30, f32[512]{0:T(512)S(1)} %get-tuple-element.214), kind=kOutput, calls=%fused_computation.7.clone.1 | convolution fusion | flops 611123200 | bytes 10752004 | tf_op jit(solution)/shard_map/while/body/eval_jaxpr/dot_general | solution.py:54
  71.0 0.6 dynamic_slice.44
  73.6 0.7 dynamic-slice_bitcast_fusion.2
  74.3 0.1 add_add_fusion.3
  74.4 1.4 select_reduce_fusion.2
  75.9 0.1 and_and_fusion.4
  76.0 0.1 broadcast_and_fusion.2
  76.1 0.1 and_and_fusion.5
  76.2 3.4 %broadcast_in_dim.73 = pred[8,64,3,3,8,64]{5,4,3,2,1,0:T(8,128)(4,1)} broadcast(pred[8,3,3,8]{3,2,1,0:T(4,128)(4,1)S(1)} %and_and_fusion.5), dimensions={0,2,3,4} | broadcast | bytes 2359872 | tf_op jit(solution)/shard_map/while/body/eval_jaxpr/broadcast_in_dim | solution.py:43
  79.6 11.3 %reshape.266 = pred[512,4608]{1,0:T(32,128)(4,1)S(1)} reshape(pred[8,64,3,3,8,64]{5,4,3,2,1,0:T(8,128)(4,1)} %broadcast_in_dim.73) | data formatting | bytes 4718592 | tf_op jit(solution)/shard_map/while/body/eval_jaxpr/reshape | solution.py:44
  90.9 1.8 constant_dynamic-slice_fusion.3
  92.8 2.9 %fusion.29 = (f32[512]{0:T(512)S(1)}, f32[512,4608]{1,0:T(8,128)S(1)}) fusion(pred[512,4608]{1,0:T(32,128)(4,1)S(1)} %reshape.266, bf16[4608,128]{1,0:T(8,128)(2,1)S(1)} %bitcast.43, bf16[1,4,512,128]{3,2,1,0:T(8,128)(2,1)} %get-tuple-element.246, s32[]{:T(128)S(6)} %select_n.79), kind=kOutput, calls=%fused_computation.41.clone.1 | convolution fusion | flops 611057152 | bytes 13109252 | tf_op jit(solution)/shard_map/while/body/eval_jaxpr/dot_general | solution.py:49
  95.7 1.4 fusion.30
  97.1 2.3 %fusion.31 = bf16[4,512,128]{2,1,0:T(8,128)(2,1)S(1)} fusion(bf16[4,512,128]{2,1,0:T(8,128)(2,1)S(1)} %get-tuple-element.229, s32[]{:T(128)} %get-tuple-element.228, bf16[4608,128]{1,0:T(8,128)(2,1)S(1)} %bitcast.44, f32[512,4608]{1,0:T(8,128)S(1)} %get-tuple-element.213, f32[512]{0:T(512)S(1)} %fusion.30, f32[512]{0:T(512)S(1)} %get-tuple-element.214), kind=kOutput, calls=%fused_computation.7.clone.1 | convolution fusion | flops 611123200 | bytes 10752004 | tf_op jit(solution)/shard_map/while/body/eval_jaxpr/dot_general | solution.py:54
  99.4 0.6 dynamic_slice.44
  102.0 0.7 dynamic-slice_bitcast_fusion.2
  102.7 0.1 add_add_fusion.3
  102.8 1.4 select_reduce_fusion.2
  104.3 0.1 and_and_fusion.4
  104.4 0.1 broadcast_and_fusion.2
  104.4 0.1 and_and_fusion.5
  104.5 3.4 %broadcast_in_dim.73 = pred[8,64,3,3,8,64]{5,4,3,2,1,0:T(8,128)(4,1)} broadcast(pred[8,3,3,8]{3,2,1,0:T(4,128)(4,1)S(1)} %and_and_fusion.5), dimensions={0,2,3,4} | broadcast | bytes 2359872 | tf_op jit(solution)/shard_map/while/body/eval_jaxpr/broadcast_in_dim | solution.py:43
  108.0 11.3 %reshape.266 = pred[512,4608]{1,0:T(32,128)(4,1)S(1)} reshape(pred[8,64,3,3,8,64]{5,4,3,2,1,0:T(8,128)(4,1)} %broadcast_in_dim.73) | data formatting | bytes 4718592 | tf_op jit(solution)/shard_map/while/body/eval_jaxpr/reshape | solution.py:44
  119.3 1.9 constant_dynamic-slice_fusion.3
  121.2 2.9 %fusion.29 = (f32[512]{0:T(512)S(1)}, f32[512,4608]{1,0:T(8,128)S(1)}) fusion(pred[512,4608]{1,0:T(32,128)(4,1)S(1)} %reshape.266, bf16[4608,128]{1,0:T(8,128)(2,1)S(1)} %bitcast.43, bf16[1,4,512,128]{3,2,1,0:T(8,128)(2,1)} %get-tuple-element.246, s32[]{:T(128)S(6)} %select_n.79), kind=kOutput, calls=%fused_computation.41.clone.1 | convolution fusion | flops 611057152 | bytes 13109252 | tf_op jit(solution)/shard_map/while/body/eval_jaxpr/dot_general | solution.py:49
  124.1 1.4 fusion.30
  125.5 2.3 %fusion.31 = bf16[4,512,128]{2,1,0:T(8,128)(2,1)S(1)} fusion(bf16[4,512,128]{2,1,0:T(8,128)(2,1)S(1)} %get-tuple-element.229, s32[]{:T(128)} %get-tuple-element.228, bf16[4608,128]{1,0:T(8,128)(2,1)S(1)} %bitcast.44, f32[512,4608]{1,0:T(8,128)S(1)} %get-tuple-element.213, f32[512]{0:T(512)S(1)} %fusion.30, f32[512]{0:T(512)S(1)} %get-tuple-element.214), kind=kOutput, calls=%fused_computation.7.clone.1 | convolution fusion | flops 611123200 | bytes 10752004 | tf_op jit(solution)/shard_map/while/body/eval_jaxpr/dot_general | solution.py:54
  127.8 0.6 dynamic_slice.44
  130.4 0.7 dynamic-slice_bitcast_fusion.2
  131.1 0.1 add_add_fusion.3
  131.2 1.4 select_reduce_fusion.2
  132.7 0.1 and_and_fusion.4
  132.8 0.1 broadcast_and_fusion.2
  132.9 0.1 and_and_fusion.5
  133.0 3.4 %broadcast_in_dim.73 = pred[8,64,3,3,8,64]{5,4,3,2,1,0:T(8,128)(4,1)} broadcast(pred[8,3,3,8]{3,2,1,0:T(4,128)(4,1)S(1)} %and_and_fusion.5), dimensions={0,2,3,4} | broadcast | bytes 2359872 | tf_op jit(solution)/shard_map/while/body/eval_jaxpr/broadcast_in_dim | solution.py:43
  136.4 11.3 %reshape.266 = pred[512,4608]{1,0:T(32,128)(4,1)S(1)} reshape(pred[8,64,3,3,8,64]{5,4,3,2,1,0:T(8,128)(4,1)} %broadcast_in_dim.73) | data formatting | bytes 4718592 | tf_op jit(solution)/shard_map/while/body/eval_jaxpr/reshape | solution.py:44
  147.7 1.8 constant_dynamic-slice_fusion.3
  149.6 3.0 %fusion.29 = (f32[512]{0:T(512)S(1)}, f32[512,4608]{1,0:T(8,128)S(1)}) fusion(pred[512,4608]{1,0:T(32,128)(4,1)S(1)} %reshape.266, bf16[4608,128]{1,0:T(8,128)(2,1)S(1)} %bitcast.43, bf16[1,4,512,128]{3,2,1,0:T(8,128)(2,1)} %get-tuple-element.246, s32[]{:T(128)S(6)} %select_n.79), kind=kOutput, calls=%fused_computation.41.clone.1 | convolution fusion | flops 611057152 | bytes 13109252 | tf_op jit(solution)/shard_map/while/body/eval_jaxpr/dot_general | solution.py:49
  152.5 1.4 fusion.30
  153.9 2.3 %fusion.31 = bf16[4,512,128]{2,1,0:T(8,128)(2,1)S(1)} fusion(bf16[4,512,128]{2,1,0:T(8,128)(2,1)S(1)} %get-tuple-element.229, s32[]{:T(128)} %get-tuple-element.228, bf16[4608,128]{1,0:T(8,128)(2,1)S(1)} %bitcast.44, f32[512,4608]{1,0:T(8,128)S(1)} %get-tuple-element.213, f32[512]{0:T(512)S(1)} %fusion.30, f32[512]{0:T(512)S(1)} %get-tuple-element.214), kind=kOutput, calls=%fused_computation.7.clone.1 | convolution fusion | flops 611123200 | bytes 10752004 | tf_op jit(solution)/shard_map/while/body/eval_jaxpr/dot_general | solution.py:54
  156.2 23.2 %all_to_all.19 = bf16[16,128,128]{2,1,0:T(8,128)(2,1)S(1)} all-to-all(bf16[16,128,128]{2,1,0:T(8,128)(2,1)S(1)} %bitcast.52), channel_id=1, replica_groups=mesh['frame'=16,'head'=16] {'head'}, dimensions={0} | all-to-all | bytes 1048576 | tf_op jit(solution)/shard_map/all_to_all | solution.py:96
  179.4 0.3 copy.7
  179.7 7.3 %convolution_convert_fusion = bf16[128,3072]{1,0:T(8,128)(2,1)} fusion(bf16[128,2048]{0,1:T(8,128)(2,1)S(1)} %bitcast.45, bf16[2048,3072]{1,0:T(8,128)(2,1)} %all-gather.2.cloned.1.call-done), kind=kOutput, calls=%fused_computation.39 | convolution fusion | flops 1611005952 | bytes 13893632 | tf_op jit(solution)/shard_map/dot_general | solution.py:97
  (33 shorter events, 0.4 us)
Async XLA Ops:
  6.5 173.1 %all-gather.2.cloned.1.call-start = ((), (), s32[]{:S(2)}) async-start(), calls=%async_computation.1 | async-start | bytes 13369344 | tf_op jit(solution)/shard_map/all_gather | solution.py:95
  8.6 17.0 %collective-permute-start = (bf16[2,1,4,512,128]{4,3,2,1,0:T(8,128)(2,1)S(1)}, bf16[2,1,4,512,128]{4,3,2,1,0:T(8,128)(2,1)S(1)}, u32[]{:S(2)}, u32[]{:S(2)}) collective-permute-start(bf16[2,1,4,512,128]{4,3,2,1,0:T(8,128)(2,1)S(1)} %pad_maximum_fusion), channel_id=1, source_target_pairs={{0,16},{16,32},{32,48},{48,64},{64,80},{80,96},{96,112},{112,128},... | collective-permute-start | bytes 3145736 | tf_op jit(solution)/shard_map/ppermute | solution.py:20
  13.9 23.9 %collective-permute-start.1 = (bf16[2,1,4,512,128]{4,3,2,1,0:T(8,128)(2,1)S(1)}, bf16[2,1,4,512,128]{4,3,2,1,0:T(8,128)(2,1)S(1)}, u32[]{:S(2)}, u32[]{:S(2)}) collective-permute-start(bf16[2,1,4,512,128]{4,3,2,1,0:T(8,128)(2,1)S(1)} %pad_maximum_fusion), channel_id=1, source_target_pairs={{16,0},{32,16},{48,32},{64,48},{80,64},{96,80},{112,96},{128,112},... | collective-permute-start | bytes 3145736 | tf_op jit(solution)/shard_map/ppermute | solution.py:23
  37.8 4.8 %copy-start = (bf16[4,512,128]{2,1,0:T(8,128)(2,1)S(1)}, bf16[4,512,128]{2,1,0:T(8,128)(2,1)}, u32[]{:S(2)}) copy-start(bf16[4,512,128]{2,1,0:T(8,128)(2,1)} %custom-call) | copy-start | bytes 1572868
Sparse Core Ops, SparseCore 0:
  9.1 146.0 all-gather.1

commit v2 on v1

v2 whole, which is shorter than its diff:
```python
import math

import numpy as np
import jax
import jax.numpy as jnp
from jax import lax
from jax.experimental import pallas as pl
from jax.experimental.pallas import tpu as pltpu
from jax.sharding import PartitionSpec as P

HEAD_DIM = 128
TROWS = 4
TCOLS = 8
WIN = 45
TILE = 64
QTILES = 2
KCOLS = 6
SEGS = 9
BLOCK_Q = QTILES * TILE
SEG_K = KCOLS * TILE
ROW_K = SEGS * SEG_K
GROUPS = TCOLS // QTILES


def window_tables():
    shape = (TROWS * GROUPS, QTILES, SEGS, KCOLS)
    qtile = np.zeros(shape, np.int32)
    offset = np.zeros(shape, np.int32)
    static_ok = np.zeros(shape, bool)
    centre = np.zeros(shape, bool)
    frame_step = np.zeros(shape, np.int32)
    for row in range(TROWS):
        for group in range(GROUPS):
            start = min(max(QTILES * group - 2, 0), TCOLS - KCOLS)
            for a in range(QTILES):
                col = QTILES * group + a
                for seg in range(SEGS):
                    df, dr = divmod(seg, 3)
                    for j in range(KCOLS):
                        dc = start + j - col
                        b = row * GROUPS + group
                        qtile[b, a, seg, j] = row * TCOLS + col
                        ok = abs(dc) <= 2 and 0 <= row + dr - 1 < TROWS
                        static_ok[b, a, seg, j] = ok
                        offset[b, a, seg, j] = 15 * df + 5 * dr + dc + 2 if ok else 0
                        centre[b, a, seg, j] = df == 1 and dr == 1 and dc == 0
                        frame_step[b, a, seg, j] = df - 1
    return qtile, offset, static_ok, centre, frame_step


def window_bias(mask_rows, frame, frames_total):
    qtile, offset, static_ok, centre, frame_step = window_tables()
    chosen = mask_rows[qtile, offset] > 0
    key_frame = frame + frame_step
    inside = (key_frame >= 0) & (key_frame < frames_total)
    allowed = (chosen | centre) & static_ok & inside
    bias = jnp.where(allowed, 0.0, -jnp.inf).astype(jnp.float32)
    bias = jnp.broadcast_to(bias[..., None], bias.shape + (TILE,))
    return bias.reshape(TROWS * GROUPS, QTILES, ROW_K)


def attention_kernel(q_ref, kp_ref, k_ref, kn_ref, vp_ref, v_ref, vn_ref, bias_ref, o_ref,
                     s_ref, p_ref):
    row = pl.program_id(0)
    group = pl.program_id(1)
    start = jnp.clip(QTILES * group - 2, 0, TCOLS - KCOLS) * TILE
    key_refs = (kp_ref, k_ref, kn_ref)
    value_refs = (vp_ref, v_ref, vn_ref)
    q = q_ref[...]
    bases = []
    for seg in range(SEGS):
        df, dr = divmod(seg, 3)
        key_row = jnp.clip(row + dr - 1, 0, TROWS - 1)
        base = pl.multiple_of(key_row * (TCOLS * TILE) + start, TILE)
        bases.append(base)
        k = key_refs[df][pl.ds(base, SEG_K), :]
        s_ref[:, seg * SEG_K:(seg + 1) * SEG_K] = lax.dot_general(
            q, k, (((1,), (1,)), ((), ())), preferred_element_type=jnp.float32
        )
    scale = 1.0 / math.sqrt(HEAD_DIM)
    for a in range(QTILES):
        rows = slice(a * TILE, (a + 1) * TILE)
        scores = s_ref[rows, :] * scale + bias_ref[0, a:a + 1, :]
        peak = jnp.max(scores, axis=1, keepdims=True)
        expos = jnp.exp(scores - peak)
        total = jnp.sum(expos, axis=1, keepdims=True)
        p_ref[rows, :] = (expos * (1.0 / total)).astype(jnp.bfloat16)
    acc = jnp.zeros((BLOCK_Q, HEAD_DIM), jnp.float32)
    for seg in range(SEGS):
        df, dr = divmod(seg, 3)
        v = value_refs[df][pl.ds(bases[seg], SEG_K), :]
        acc += jnp.dot(p_ref[:, seg * SEG_K:(seg + 1) * SEG_K], v,
                       preferred_element_type=jnp.float32)
    o_ref[...] = acc.astype(o_ref.dtype)


def attend(q, kp, k, kn, vp, v, vn, bias):
    tokens = q.shape[0]
    full = pl.BlockSpec((tokens, HEAD_DIM), lambda r, g: (0, 0))
    return pl.pallas_call(
        attention_kernel,
        grid=(TROWS, GROUPS),
        in_specs=[pl.BlockSpec((BLOCK_Q, HEAD_DIM), lambda r, g: (r * GROUPS + g, 0))]
        + [full] * 6
        + [pl.BlockSpec((1, QTILES, ROW_K), lambda r, g: (r * GROUPS + g, 0, 0))],
        out_specs=pl.BlockSpec((BLOCK_Q, HEAD_DIM), lambda r, g: (r * GROUPS + g, 0)),
        out_shape=jax.ShapeDtypeStruct((tokens, HEAD_DIM), jnp.bfloat16),
        scratch_shapes=[
            pltpu.VMEM((BLOCK_Q, ROW_K), jnp.float32),
            pltpu.VMEM((BLOCK_Q, ROW_K), jnp.bfloat16),
        ],
    )(q, kp, k, kn, vp, v, vn, bias)


def on_device(queries, keys, values, block_mask, out_weight):
    tok_dev = queries.shape[0]
    frames_here = tok_dev // (TROWS * TCOLS * TILE)
    assert frames_here == 1 and queries.shape[1] == HEAD_DIM
    count = lax.axis_size("frame")
    frames_total = frames_here * count
    frame = lax.axis_index("frame") * frames_here
    forward = [(i, i + 1) for i in range(count - 1)]
    backward = [(t, s) for s, t in forward]
    pair = jnp.stack([keys, values])
    prev = lax.ppermute(pair, "frame", forward)
    nxt = lax.ppermute(pair, "frame", backward)
    mask_rows = block_mask.reshape(TROWS * TCOLS, WIN)
    bias = window_bias(mask_rows, frame, frames_total)
    attention = attend(queries, prev[0], keys, nxt[0], prev[1], values, nxt[1], bias)
    full_weight = lax.all_gather(out_weight, "head", axis=0, tiled=True)
    gathered = lax.all_to_all(attention, "head", 0, 1, tiled=True)
    return jnp.dot(gathered, full_weight, preferred_element_type=jnp.float32).astype(jnp.bfloat16)


def solution(mesh):
    return jax.shard_map(
        on_device,
        mesh=mesh,
        in_specs=(
            P("frame", "head"),
            P("frame", "head"),
            P("frame", "head"),
            P("head", "frame", None, None),
            P("head", None),
        ),
        out_specs=P(("frame", "head"), None),
        check_vma=False,
    )
```

time: 195 us -> 187 us (0.959)
  the two profiles are of different devices: /device:TPU:7 before, /device:TPU:1 now
where the time goes in v2:
time: 187 us
  waiting for transfers between devices  85.1 us (46%)
  blocking collectives  30.1 us (16%)
  Pallas kernels  23.9 us (13%)
  local copies, waits for them, and re-layouts  18.6 us (10%)
  between operations  13.5 us (7%)
  matrix products  7.28 us (4%)
  starting transfers between devices  7.07 us (4%)
    all_gather x1, waiting for transfers between devices, on_device(): full_weight = lax.all_gather(out_weight, 'head', axis=0, tiled=True)  84.3 us
    all_to_all x1, blocking collectives, on_device(): gathered = lax.all_to_all(attention, 'head', 0, 1, tiled=True)  30.1 us
    pallas_call x1, Pallas kernels, attend(): pl.pallas_call(attention_kernel, grid=(TROWS, GROUPS), in_specs=[pl.Block...  23.9 us
    gather x1, local copies, waits for them, and re-layouts, window_bias(): chosen = mask_rows[qtile, offset] > 0  10.9 us
    dot_general x1, matrix products, on_device(): jnp.dot(gathered, full_weight, preferred_element_type=jnp.float32)  7.28 us
    ppermute x1, starting transfers between devices, on_device(): nxt = lax.ppermute(pair, 'frame', backward)  5.15 us
  transfers between devices with their start and end apart: 3, of which 1 were waited for; matrix products, arithmetic and copies ran while one was open for 11% of the time, Pallas kernels for 13%

profile of v2, /device:TPU:1, one launch (start us, length us, event | category | flops | bytes accessed | tf_op | source)
XLA Modules:
  0.0 186.9 jit_solution(3573340265462269642)
XLA Ops:
  6.5 0.0 copy-start
  6.5 0.0 all-gather.2.cloned.1.call-start
  6.5 0.7 all-gather.2.cloned.1.call-update
  7.3 0.0 copy-start.1
  7.3 1.3 pad_maximum_fusion
  8.6 5.2 %collective-permute-start.1 = (bf16[2,2048,128]{2,1,0:T(8,128)(2,1)S(1)}, bf16[2,2048,128]{2,1,0:T(8,128)(2,1)}, u32[]{:S(2)}, u32[]{:S(2)}) collective-permute-start(bf16[2,2048,128]{2,1,0:T(8,128)(2,1)S(1)} %pad_maximum_fusion), channel_id=1, source_target_pairs={{16,0},{32,16},{48,32},{64,48},{80,64},{96,80},{112,96},{128,112},... | collective-permute-start | bytes 3145736 | tf_op jit(solution)/shard_map/ppermute | solution.py:126
  13.7 1.9 %collective-permute-start = (bf16[2,2048,128]{2,1,0:T(8,128)(2,1)S(1)}, bf16[2,2048,128]{2,1,0:T(8,128)(2,1)}, u32[]{:S(2)}, u32[]{:S(2)}) collective-permute-start(bf16[2,2048,128]{2,1,0:T(8,128)(2,1)S(1)} %pad_maximum_fusion), channel_id=1, source_target_pairs={{0,16},{16,32},{32,48},{48,64},{64,80},{80,96},{96,112},{112,128},... | collective-permute-start | bytes 3145736 | tf_op jit(solution)/shard_map/ppermute | solution.py:125
  15.7 0.0 copy-done
  15.7 0.0 copy-done.1
  15.7 0.0 copy-start.3
  15.7 0.0 copy-start.4
  15.7 0.0 copy-start.2
  15.7 10.9 %gather_fusion = s32[1728]{0:T(1024)S(1)} fusion(s32[32,45]{1,0:T(8,128)S(1)} %bitcast.19, s32[1728]{0:T(1024)S(1)} %copy-done.1), kind=kCustom, calls=%fused_computation | custom fusion | bytes 27648 | tf_op jit(solution)/shard_map/gather | solution.py:53
  26.7 0.0 copy-done.3
  26.7 0.0 copy-done.4
  26.7 0.2 reshape.23
  26.9 0.0 copy-done.2
  26.9 0.1 fusion.2
  27.0 0.4 broadcast_in_dim.24
  27.4 0.3 reshape.11
  27.6 1.0 copy.14.bias_ref
  28.7 0.0 collective-permute-done.1
  28.7 2.2 %slice_bitcast_fusion = (bf16[2048,128]{1,0:T(8,128)(2,1)}, bf16[2048,128]{1,0:T(8,128)(2,1)}) fusion(bf16[2,2048,128]{2,1,0:T(8,128)(2,1)} %collective-permute-done.1), kind=kLoop, calls=%fused_computation.3 | loop fusion | bytes 2097152 | tf_op jit(solution)/shard_map/squeeze | solution.py:129
  30.9 0.0 collective-permute-done
  30.9 2.2 %slice_bitcast_fusion.1 = (bf16[2048,128]{1,0:T(8,128)(2,1)}, bf16[2048,128]{1,0:T(8,128)(2,1)}) fusion(bf16[2,2048,128]{2,1,0:T(8,128)(2,1)} %collective-permute-done), kind=kLoop, calls=%fused_computation.4 | loop fusion | bytes 2097152 | tf_op jit(solution)/shard_map/squeeze | solution.py:129
  33.2 23.9 %shard_map.118 = bf16[2048,128]{1,0:T(8,128)(2,1)} custom-call(bf16[2048,128]{1,0:T(8,128)(2,1)} %q_ref.1, bf16[2048,128]{1,0:T(8,128)(2,1)} %get-tuple-element.8.kp_ref, bf16[2048,128]{1,0:T(8,128)(2,1)} %k_ref.1, bf16[2048,128]{1,0:T(8,128)(2,1)} %get-tuple-element.6.kn_ref, bf16[2048,128]{1,0:T(8,128)(2,1)} %get-tuple-element.7.vp_ref, ...), custom_call_target="tpu_custom_call" | custom-call | tf_op jit(solution)/shard_map/pallas_call | solution.py:100
  57.1 1.3 copy.15
  58.4 30.1 %all_to_all.19 = bf16[16,128,128]{1,2,0:T(8,128)(2,1)S(1)} all-to-all(bf16[16,128,128]{1,2,0:T(8,128)(2,1)S(1)} %copy.15), channel_id=1, replica_groups=mesh['frame'=16,'head'=16] {'head'}, dimensions={0} | all-to-all | bytes 1048576 | tf_op jit(solution)/shard_map/all_to_all | solution.py:131
  88.5 84.3 %all-gather.2.cloned.1.call-done = bf16[2048,3072]{1,0:T(8,128)(2,1)} async-done(((bf16[128,3072]{1,0:T(8,128)(2,1)}), bf16[2048,3072]{1,0:T(8,128)(2,1)}) %all-gather.2.cloned.1.call-update) | async-done | bytes 12582928 | tf_op jit(solution)/shard_map/all_gather | solution.py:130
  172.8 7.3 %convolution_convert_fusion = bf16[128,3072]{1,0:T(8,128)(2,1)} fusion(bf16[128,2048]{0,1:T(8,128)(2,1)S(1)} %bitcast.20, bf16[2048,3072]{1,0:T(8,128)(2,1)} %all-gather.2.cloned.1.call-done), kind=kOutput, calls=%fused_computation.1 | convolution fusion | flops 1611005952 | bytes 13893632 | tf_op jit(solution)/shard_map/dot_general | solution.py:132
  (2 shorter events, 0.0 us)
Async XLA Ops:
  6.5 9.1 %copy-start = (s32[1,1,32,45]{3,2,1,0:T(8,128)S(1)}, s32[1,1,32,45]{3,2,1,0:T(8,128)}, u32[]{:S(2)}) copy-start(s32[1,1,32,45]{3,2,1,0:T(8,128)} %param.15) | copy-start | bytes 17284
  6.5 166.3 %all-gather.2.cloned.1.call-start = ((), (), s32[]{:S(2)}) async-start(), calls=%async_computation.1 | async-start | bytes 13369344 | tf_op jit(solution)/shard_map/all_gather | solution.py:130
  7.3 8.4 %copy-start.1 = (s32[1728]{0:T(1024)S(1)}, s32[1728]{0:T(1024)}, u32[]{:S(2)}) copy-start(s32[1728]{0:T(1024)} %constant.59) | copy-start | bytes 20740
  8.6 20.1 %collective-permute-start.1 = (bf16[2,2048,128]{2,1,0:T(8,128)(2,1)S(1)}, bf16[2,2048,128]{2,1,0:T(8,128)(2,1)}, u32[]{:S(2)}, u32[]{:S(2)}) collective-permute-start(bf16[2,2048,128]{2,1,0:T(8,128)(2,1)S(1)} %pad_maximum_fusion), channel_id=1, source_target_pairs={{16,0},{32,16},{48,32},{64,48},{80,64},{96,80},{112,96},{128,112},... | collective-permute-start | bytes 3145736 | tf_op jit(solution)/shard_map/ppermute | solution.py:126
  13.7 17.2 %collective-permute-start = (bf16[2,2048,128]{2,1,0:T(8,128)(2,1)S(1)}, bf16[2,2048,128]{2,1,0:T(8,128)(2,1)}, u32[]{:S(2)}, u32[]{:S(2)}) collective-permute-start(bf16[2,2048,128]{2,1,0:T(8,128)(2,1)S(1)} %pad_maximum_fusion), channel_id=1, source_target_pairs={{0,16},{16,32},{32,48},{48,64},{64,80},{80,96},{96,112},{112,128},... | collective-permute-start | bytes 3145736 | tf_op jit(solution)/shard_map/ppermute | solution.py:125
  15.7 11.0 %copy-start.3 = (pred[1728]{0:T(1024)(128)(4,1)S(1)}, pred[1728]{0:T(1024)(128)(4,1)}, u32[]{:S(2)}) copy-start(pred[1728]{0:T(1024)(128)(4,1)} %constant.60) | copy-start | bytes 5188
  15.7 11.0 %copy-start.4 = (pred[1728]{0:T(1024)(128)(4,1)S(1)}, pred[1728]{0:T(1024)(128)(4,1)}, u32[]{:S(2)}) copy-start(pred[1728]{0:T(1024)(128)(4,1)} %constant.61) | copy-start | bytes 5188
  15.7 11.2 %copy-start.2 = (s32[16,2,9,6]{3,2,1,0:T(8,128)S(1)}, s32[16,2,9,6]{3,2,1,0:T(8,128)}, u32[]{:S(2)}) copy-start(s32[16,2,9,6]{3,2,1,0:T(8,128)} %constant.32.clone) | copy-start | bytes 20740
Sparse Core Ops, SparseCore 0:
  9.1 163.6 all-gather.1

commit v3 on v2

--- a/solution.py
+++ b/solution.py
@@ -127,9 +127,21 @@
     mask_rows = block_mask.reshape(TROWS * TCOLS, WIN)
     bias = window_bias(mask_rows, frame, frames_total)
     attention = attend(queries, prev[0], keys, nxt[0], prev[1], values, nxt[1], bias)
-    full_weight = lax.all_gather(out_weight, "head", axis=0, tiled=True)
-    gathered = lax.all_to_all(attention, "head", 0, 1, tiled=True)
-    return jnp.dot(gathered, full_weight, preferred_element_type=jnp.float32).astype(jnp.bfloat16)
+    core = lax.axis_index("frame") % 2
+    half = out_weight.shape[1] // 2
+    partners = [(i, i ^ 1) for i in range(count)]
+    weight_half = lax.dynamic_slice_in_dim(out_weight, core * half, half, axis=1)
+    weight_half = lax.all_gather(weight_half, "head", axis=0, tiled=True)
+    mine = lax.all_to_all(attention, "head", 0, 1, tiled=True)
+    theirs = lax.ppermute(mine, "frame", partners)
+    project = lambda x: jnp.dot(x, weight_half, preferred_element_type=jnp.float32).astype(jnp.bfloat16)
+    own_half = project(mine)
+    other_half = lax.ppermute(project(theirs), "frame", partners)
+    return jnp.where(
+        core == 0,
+        jnp.concatenate([own_half, other_half], axis=1),
+        jnp.concatenate([other_half, own_half], axis=1),
+    )
 
 
 def solution(mesh):

time: 187 us -> 129 us (0.69)
  the two profiles are of different devices: /device:TPU:1 before, /device:TPU:31 now
where the time goes in v3:
time: 129 us; the launch traced here: 128 us
  blocking collectives  29.2 us (23%)
  Pallas kernels  23.9 us (19%)
  waiting for transfers between devices  21.8 us (17%)
  local copies, waits for them, and re-layouts  19.4 us (15%)
  between operations  13.6 us (11%)
  starting transfers between devices  13.2 us (10%)
  matrix products  4.97 us (4%)
  other arithmetic  2.24 us (2%)
    all_to_all x1, blocking collectives, on_device(): mine = lax.all_to_all(attention, 'head', 0, 1, tiled=True)  29.2 us
    pallas_call x1, Pallas kernels, attend(): pl.pallas_call(attention_kernel, grid=(TROWS, GROUPS), in_specs=[pl.Block...  23.9 us
    all_gather x1, waiting for transfers between devices, on_device(): weight_half = lax.all_gather(weight_half, 'head', axis=0, tiled=True)  19.9 us
    gather x1, local copies, waits for them, and re-layouts, window_bias(): chosen = mask_rows[qtile, offset] > 0  10.9 us
    ppermute x1, starting transfers between devices, on_device(): other_half = lax.ppermute(project(theirs), 'frame', partners)  5.74 us
    dot_general x2, matrix products, on_device(): jnp.dot(x, weight_half, preferred_element_type=jnp.float32)  4.97 us
    ppermute x1, starting transfers between devices, on_device(): nxt = lax.ppermute(pair, 'frame', backward)  3.27 us
    ppermute x1, starting transfers between devices, on_device(): theirs = lax.ppermute(mine, 'frame', partners)  2.94 us
  transfers between devices with their start and end apart: 5, of which 3 were waited for; matrix products, arithmetic and copies ran while one was open for 15% of the time, Pallas kernels for 19%

profile of v3, /device:TPU:31, one launch (start us, length us, event | category | flops | bytes accessed | tf_op | source)
XLA Modules:
  0.0 128.3 jit_solution(4680630841513379428)
XLA Ops:
  6.5 0.0 copy-start
  6.5 0.0 copy-start.4
  6.5 0.0 copy-start.5
  6.5 0.0 all-gather.2.cloned.1.call-start
  6.6 1.1 copy-done
  7.7 0.0 copy-start.1
  7.7 0.0 copy-start.2
  7.7 0.8 constant_dynamic-slice_fusion
  8.4 0.0 all-gather.2.cloned.1.call-update
  8.5 0.0 copy-done.4
  8.5 0.0 copy-done.5
  8.5 1.1 pad_maximum_fusion
  9.6 1.3 collective-permute-start
  10.9 3.3 %collective-permute-start.1 = (bf16[2,2048,128]{2,1,0:T(8,128)(2,1)}, bf16[2,2048,128]{2,1,0:T(8,128)(2,1)S(1)}, u32[]{:S(2)}, u32[]{:S(2)}) collective-permute-start(bf16[2,2048,128]{2,1,0:T(8,128)(2,1)} %pad_maximum_fusion), channel_id=1, source_target_pairs={{16,0},{32,16},{48,32},{64,48},{80,64},{96,80},{112,96},{128,112},... | collective-permute-start | bytes 3145736 | tf_op jit(solution)/shard_map/ppermute | solution.py:126
  14.1 0.0 copy-done.1
  14.2 0.0 copy-done.2
  14.2 0.0 copy-start.7
  14.2 0.0 copy-start.8
  14.2 0.0 copy-start.6
  14.2 10.9 %gather_fusion = s32[1728]{0:T(1024)S(1)} fusion(s32[32,45]{1,0:T(8,128)S(1)} %bitcast.21, s32[1728]{0:T(1024)S(1)} %copy-done.2), kind=kCustom, calls=%fused_computation | custom fusion | bytes 27648 | tf_op jit(solution)/shard_map/gather | solution.py:53
  25.2 0.0 copy-done.7
  25.2 0.0 copy-done.8
  25.2 0.2 reshape.23
  25.4 0.0 copy-done.6
  25.4 0.1 fusion.2
  25.5 0.4 broadcast_in_dim.24
  25.9 0.3 reshape.11
  26.1 1.0 copy.14.bias_ref
  27.2 0.0 collective-permute-done
  27.2 2.3 %slice_bitcast_fusion.1 = (bf16[2048,128]{1,0:T(8,128)(2,1)}, bf16[2048,128]{1,0:T(8,128)(2,1)}) fusion(bf16[2,2048,128]{2,1,0:T(8,128)(2,1)} %collective-permute-done), kind=kLoop, calls=%fused_computation.6 | loop fusion | bytes 2097152 | tf_op jit(solution)/shard_map/squeeze | solution.py:129
  29.5 0.0 collective-permute-done.1
  29.5 1.1 slice_bitcast_fusion
  30.5 23.9 %shard_map.118 = bf16[2048,128]{1,0:T(8,128)(2,1)} custom-call(bf16[2048,128]{1,0:T(8,128)(2,1)} %q_ref.1, bf16[2048,128]{1,0:T(8,128)(2,1)} %get-tuple-element.8.kp_ref, bf16[2048,128]{1,0:T(8,128)(2,1)} %k_ref.1, bf16[2048,128]{1,0:T(8,128)(2,1)} %get-tuple-element.6.kn_ref, bf16[2048,128]{1,0:T(8,128)(2,1)} %get-tuple-element.7.vp_ref, ...), custom_call_target="tpu_custom_call" | custom-call | tf_op jit(solution)/shard_map/pallas_call | solution.py:100
  54.4 1.3 %copy.15 = bf16[16,128,128]{1,2,0:T(8,128)(2,1)S(1)} copy(bf16[16,128,128]{2,1,0:T(8,128)(2,1)} %bitcast.24) | data formatting | bytes 1048576 | tf_op jit(solution)/shard_map/all_to_all | solution.py:135
  55.7 29.2 %all_to_all.19 = bf16[16,128,128]{1,2,0:T(8,128)(2,1)S(1)} all-to-all(bf16[16,128,128]{1,2,0:T(8,128)(2,1)S(1)} %copy.15), channel_id=1, replica_groups=mesh['frame'=16,'head'=16] {'head'}, dimensions={0} | all-to-all | bytes 1048576 | tf_op jit(solution)/shard_map/all_to_all | solution.py:135
  84.9 2.9 %collective-permute-start.2 = (bf16[128,2048]{0,1:T(8,128)(2,1)S(1)}, bf16[128,2048]{0,1:T(8,128)(2,1)S(1)}, u32[]{:S(2)}, u32[]{:S(2)}) collective-permute-start(bf16[128,2048]{0,1:T(8,128)(2,1)S(1)} %bitcast.22), channel_id=1, source_target_pairs={{0,16},{16,0},{32,48},{48,32},{64,80},{80,64},{96,112},{112,96},{1... | collective-permute-start | bytes 1572872 | tf_op jit(solution)/shard_map/ppermute | solution.py:136
  87.8 1.5 %collective-permute-done.2 = bf16[128,2048]{0,1:T(8,128)(2,1)S(1)} collective-permute-done((bf16[128,2048]{0,1:T(8,128)(2,1)S(1)}, bf16[128,2048]{0,1:T(8,128)(2,1)S(1)}, u32[]{:S(2)}, u32[]{:S(2)}) %collective-permute-start.2) | collective-permute-done | bytes 524320 | tf_op jit(solution)/shard_map/ppermute | solution.py:136
  89.4 19.9 %all-gather.2.cloned.1.call-done = bf16[2048,1536]{1,0:T(8,128)(2,1)} async-done(((bf16[128,1536]{1,0:T(8,128)(2,1)}), bf16[2048,1536]{1,0:T(8,128)(2,1)}) %all-gather.2.cloned.1.call-update) | async-done | bytes 6291472 | tf_op jit(solution)/shard_map/all_gather | solution.py:134
  109.3 0.0 copy-start.3
  109.3 4.0 %convolution_convert_fusion = bf16[128,1536]{1,0:T(8,128)(2,1)S(1)} fusion(bf16[128,2048]{0,1:T(8,128)(2,1)S(1)} %collective-permute-done.2, bf16[2048,1536]{1,0:T(8,128)(2,1)} %all-gather.2.cloned.1.call-done), kind=kOutput, calls=%fused_computation.1 | convolution fusion | flops 805502976 | bytes 7208960 | tf_op jit(solution)/shard_map/dot_general | solution.py:137
  113.3 5.7 %collective-permute-start.3 = (bf16[128,1536]{1,0:T(8,128)(2,1)S(1)}, bf16[128,1536]{1,0:T(8,128)(2,1)S(1)}, u32[]{:S(2)}, u32[]{:S(2)}) collective-permute-start(bf16[128,1536]{1,0:T(8,128)(2,1)S(1)} %convolution_convert_fusion), channel_id=1, source_target_pairs={{0,16},{16,0},{32,48},{48,32},{64,80},{80,64},{96,112},{112,96},{1... | collective-permute-start | bytes 1179656 | tf_op jit(solution)/shard_map/ppermute | solution.py:139
  119.0 0.0 copy-done.3
  119.0 1.0 convolution_convert_fusion.1
  120.0 0.3 collective-permute-done.3
  120.3 1.1 maximum_select_fusion
  (2 shorter events, 0.0 us)
Async XLA Ops:
  6.5 1.1 copy-start
  6.5 1.9 %copy-start.4 = (bf16[2048,128]{1,0:T(8,128)(2,1)S(1)}, bf16[2048,128]{1,0:T(8,128)(2,1)}, u32[]{:S(2)}) copy-start(bf16[2048,128]{1,0:T(8,128)(2,1)} %v_ref.1) | copy-start | bytes 1572868
  6.5 1.9 %copy-start.5 = (bf16[2048,128]{1,0:T(8,128)(2,1)S(1)}, bf16[2048,128]{1,0:T(8,128)(2,1)}, u32[]{:S(2)}) copy-start(bf16[2048,128]{1,0:T(8,128)(2,1)} %k_ref.1) | copy-start | bytes 1572868
  6.5 102.8 %all-gather.2.cloned.1.call-start = ((), (), s32[]{:S(2)}) async-start(), calls=%async_computation.1 | async-start | bytes 6684672 | tf_op jit(solution)/shard_map/all_gather | solution.py:134
  7.7 6.5 %copy-start.1 = (s32[1,1,32,45]{3,2,1,0:T(8,128)S(1)}, s32[1,1,32,45]{3,2,1,0:T(8,128)}, u32[]{:S(2)}) copy-start(s32[1,1,32,45]{3,2,1,0:T(8,128)} %param.15) | copy-start | bytes 17284
  7.7 6.5 %copy-start.2 = (s32[1728]{0:T(1024)S(1)}, s32[1728]{0:T(1024)}, u32[]{:S(2)}) copy-start(s32[1728]{0:T(1024)} %constant.76) | copy-start | bytes 20740
  9.6 17.6 %collective-permute-start = (bf16[2,2048,128]{2,1,0:T(8,128)(2,1)}, bf16[2,2048,128]{2,1,0:T(8,128)(2,1)}, u32[]{:S(2)}, u32[]{:S(2)}) collective-permute-start(bf16[2,2048,128]{2,1,0:T(8,128)(2,1)} %pad_maximum_fusion), channel_id=1, source_target_pairs={{0,16},{16,32},{32,48},{48,64},{64,80},{80,96},{96,112},{112,128},... | collective-permute-start | bytes 3145736 | tf_op jit(solution)/shard_map/ppermute | solution.py:125
  10.9 18.6 %collective-permute-start.1 = (bf16[2,2048,128]{2,1,0:T(8,128)(2,1)}, bf16[2,2048,128]{2,1,0:T(8,128)(2,1)S(1)}, u32[]{:S(2)}, u32[]{:S(2)}) collective-permute-start(bf16[2,2048,128]{2,1,0:T(8,128)(2,1)} %pad_maximum_fusion), channel_id=1, source_target_pairs={{16,0},{32,16},{48,32},{64,48},{80,64},{96,80},{112,96},{128,112},... | collective-permute-start | bytes 3145736 | tf_op jit(solution)/shard_map/ppermute | solution.py:126
  14.2 11.0 %copy-start.7 = (pred[1728]{0:T(1024)(128)(4,1)S(1)}, pred[1728]{0:T(1024)(128)(4,1)}, u32[]{:S(2)}) copy-start(pred[1728]{0:T(1024)(128)(4,1)} %constant.78) | copy-start | bytes 5188
  14.2 11.0 %copy-start.8 = (pred[1728]{0:T(1024)(128)(4,1)S(1)}, pred[1728]{0:T(1024)(128)(4,1)}, u32[]{:S(2)}) copy-start(pred[1728]{0:T(1024)(128)(4,1)} %constant.77) | copy-start | bytes 5188
  14.2 11.2 %copy-start.6 = (s32[16,2,9,6]{3,2,1,0:T(8,128)S(1)}, s32[16,2,9,6]{3,2,1,0:T(8,128)}, u32[]{:S(2)}) copy-start(s32[16,2,9,6]{3,2,1,0:T(8,128)} %constant.49.clone) | copy-start | bytes 20740
  84.9 4.5 %collective-permute-start.2 = (bf16[128,2048]{0,1:T(8,128)(2,1)S(1)}, bf16[128,2048]{0,1:T(8,128)(2,1)S(1)}, u32[]{:S(2)}, u32[]{:S(2)}) collective-permute-start(bf16[128,2048]{0,1:T(8,128)(2,1)S(1)} %bitcast.22), channel_id=1, source_target_pairs={{0,16},{16,0},{32,48},{48,32},{64,80},{80,64},{96,112},{112,96},{1... | collective-permute-start | bytes 1572872 | tf_op jit(solution)/shard_map/ppermute | solution.py:136
  109.3 9.7 %copy-start.3 = (bf16[2048,1536]{1,0:T(8,128)(2,1)S(1)}, bf16[2048,1536]{1,0:T(8,128)(2,1)}, u32[]{:S(2)}) copy-start(bf16[2048,1536]{1,0:T(8,128)(2,1)} %all-gather.2.cloned.1.call-done) | copy-start | bytes 18874372
  113.3 7.1 %collective-permute-start.3 = (bf16[128,1536]{1,0:T(8,128)(2,1)S(1)}, bf16[128,1536]{1,0:T(8,128)(2,1)S(1)}, u32[]{:S(2)}, u32[]{:S(2)}) collective-permute-start(bf16[128,1536]{1,0:T(8,128)(2,1)S(1)} %convolution_convert_fusion), channel_id=1, source_target_pairs={{0,16},{16,0},{32,48},{48,32},{64,80},{80,64},{96,112},{112,96},{1... | collective-permute-start | bytes 1179656 | tf_op jit(solution)/shard_map/ppermute | solution.py:139
Sparse Core Ops, SparseCore 0:
  9.2 100.1 all-gather.1

commit v4 on v3

--- a/solution.py
+++ b/solution.py
@@ -128,15 +128,26 @@
     bias = window_bias(mask_rows, frame, frames_total)
     attention = attend(queries, prev[0], keys, nxt[0], prev[1], values, nxt[1], bias)
     core = lax.axis_index("frame") % 2
+    side = lax.axis_index("hy")
+    sides = lax.axis_size("hy")
     half = out_weight.shape[1] // 2
     partners = [(i, i ^ 1) for i in range(count)]
     weight_half = lax.dynamic_slice_in_dim(out_weight, core * half, half, axis=1)
-    weight_half = lax.all_gather(weight_half, "head", axis=0, tiled=True)
-    mine = lax.all_to_all(attention, "head", 0, 1, tiled=True)
+    weight_half = lax.all_gather(weight_half, "hz", axis=0, tiled=True)
+    chunks = attention.reshape(sides, -1, tok_dev // (sides * lax.axis_size("hz")), HEAD_DIM)
+    chunks = chunks.transpose(1, 0, 2, 3).reshape(tok_dev, HEAD_DIM)
+    mine = lax.all_to_all(chunks, "hz", 0, 1, tiled=True)
     theirs = lax.ppermute(mine, "frame", partners)
-    project = lambda x: jnp.dot(x, weight_half, preferred_element_type=jnp.float32).astype(jnp.bfloat16)
-    own_half = project(mine)
-    other_half = lax.ppermute(project(theirs), "frame", partners)
+    block = mine.shape[0] // sides
+
+    def project(x, which):
+        rows = lax.dynamic_slice_in_dim(x, which * block, block, axis=0)
+        return jnp.dot(rows, weight_half, preferred_element_type=jnp.float32)
+
+    flip = [(0, 1), (1, 0)]
+    sent = lax.ppermute(jnp.stack([project(mine, 1 - side), project(theirs, 1 - side)]), "hy", flip)
+    own_half = (project(mine, side) + sent[0]).astype(jnp.bfloat16)
+    other_half = lax.ppermute((project(theirs, side) + sent[1]).astype(jnp.bfloat16), "frame", partners)
     return jnp.where(
         core == 0,
         jnp.concatenate([own_half, other_half], axis=1),
@@ -145,16 +156,20 @@
 
 
 def solution(mesh):
+    frames, heads = mesh.devices.shape
+    grid = mesh.devices.reshape(frames, 2, heads // 2)
+    split = jax.sharding.Mesh(grid, ("frame", "hy", "hz"))
+    head = ("hy", "hz")
     return jax.shard_map(
         on_device,
-        mesh=mesh,
+        mesh=split,
         in_specs=(
-            P("frame", "head"),
-            P("frame", "head"),
-            P("frame", "head"),
-            P("head", "frame", None, None),
-            P("head", None),
+            P("frame", head),
+            P("frame", head),
+            P("frame", head),
+            P(head, "frame", None, None),
+            P(head, None),
         ),
-        out_specs=P(("frame", "head"), None),
+        out_specs=P(("frame",) + head, None),
         check_vma=False,
     )

time: 129 us -> 140 us (1.085)
  the two profiles are of different devices: /device:TPU:31 before, /device:TPU:17 now
where the time goes in v4:
time: 140 us; the launch traced here: 139 us
  waiting for transfers between devices  35.2 us (25%)
  Pallas kernels  23.9 us (17%)
  blocking collectives  21 us (15%)
  local copies, waits for them, and re-layouts  19.5 us (14%)
  between operations  13.6 us (10%)
  starting transfers between devices  13 us (9%)
  matrix products  9 us (6%)
  other arithmetic  3.52 us (3%)
    ppermute x1, waiting for transfers between devices, on_device(): lax.ppermute(jnp.stack([project(mine, 1 - side), project(theirs, 1 - side...  35.2 us
    pallas_call x1, Pallas kernels, attend(): pl.pallas_call(attention_kernel, grid=(TROWS, GROUPS), in_specs=[pl.Block...  23.9 us
    all_to_all x1, blocking collectives, on_device(): mine = lax.all_to_all(chunks, 'hz', 0, 1, tiled=True)  21 us
    gather x1, local copies, waits for them, and re-layouts, window_bias(): chosen = mask_rows[qtile, offset] > 0  10.9 us
    dot_general x4, matrix products, project(): return jnp.dot(rows, weight_half, preferred_element_type=jnp.float32)  9 us
    ppermute x1, starting transfers between devices, on_device(): theirs = lax.ppermute(mine, 'frame', partners)  5.56 us
    ppermute x1, starting transfers between devices, on_device(): prev = lax.ppermute(pair, 'frame', forward)  3.02 us
  transfers between devices with their start and end apart: 6, of which 1 were waited for; matrix products, arithmetic and copies ran while one was open for 17% of the time, Pallas kernels for 17%

profile of v4, /device:TPU:17, one launch (start us, length us, event | category | flops | bytes accessed | tf_op | source)
XLA Modules:
  0.0 138.7 jit_solution(8039087778668126037)
XLA Ops:
  6.5 0.0 copy-start
  6.5 0.0 copy-start.5
  6.5 0.0 copy-start.4
  6.5 0.0 all-gather.2.cloned.1.call-start
  6.6 1.1 copy-done
  7.7 0.0 copy-start.1
  7.7 0.0 copy-start.2
  7.7 0.8 constant_dynamic-slice_fusion
  8.5 0.0 all-gather.2.cloned.1.call-update
  8.5 0.0 copy-done.5
  8.5 0.0 copy-done.4
  8.5 1.1 pad_maximum_fusion.1
  9.6 2.6 %collective-permute-start.1 = (bf16[2,2048,128]{2,1,0:T(8,128)(2,1)}, bf16[2,2048,128]{2,1,0:T(8,128)(2,1)}, u32[]{:S(2)}, u32[]{:S(2)}) collective-permute-start(bf16[2,2048,128]{2,1,0:T(8,128)(2,1)} %pad_maximum_fusion.1), channel_id=1, source_target_pairs={{16,0},{32,16},{48,32},{64,48},{80,64},{96,80},{112,96},{128,112},... | collective-permute-start | bytes 3145736 | tf_op jit(solution)/shard_map/ppermute | solution.py:126
  12.2 3.0 %collective-permute-start = (bf16[2,2048,128]{2,1,0:T(8,128)(2,1)}, bf16[2,2048,128]{2,1,0:T(8,128)(2,1)S(1)}, u32[]{:S(2)}, u32[]{:S(2)}) collective-permute-start(bf16[2,2048,128]{2,1,0:T(8,128)(2,1)} %pad_maximum_fusion.1), channel_id=1, source_target_pairs={{0,16},{16,32},{32,48},{48,64},{64,80},{80,96},{96,112},{112,128},... | collective-permute-start | bytes 3145736 | tf_op jit(solution)/shard_map/ppermute | solution.py:125
  15.2 0.0 copy-done.1
  15.2 0.0 copy-done.2
  15.2 0.0 copy-start.7
  15.2 0.0 copy-start.8
  15.2 0.0 copy-start.6
  15.3 10.9 %gather_fusion = s32[1728]{0:T(1024)S(1)} fusion(s32[32,45]{1,0:T(8,128)S(1)} %bitcast.37, s32[1728]{0:T(1024)S(1)} %copy-done.2), kind=kCustom, calls=%fused_computation | custom fusion | bytes 27648 | tf_op jit(solution)/shard_map/gather | solution.py:53
  26.2 0.0 copy-done.7
  26.2 0.0 copy-done.8
  26.2 0.2 reshape.29
  26.4 0.0 copy-done.6
  26.4 0.1 fusion.12
  26.5 0.4 broadcast_in_dim.24
  26.9 0.3 reshape.16
  27.2 1.0 copy.14.bias_ref
  28.2 0.0 collective-permute-done.1
  28.2 2.3 %slice_bitcast_fusion.2 = (bf16[2048,128]{1,0:T(8,128)(2,1)}, bf16[2048,128]{1,0:T(8,128)(2,1)}) fusion(bf16[2,2048,128]{2,1,0:T(8,128)(2,1)} %collective-permute-done.1), kind=kLoop, calls=%fused_computation.12 | loop fusion | bytes 2097152 | tf_op jit(solution)/shard_map/squeeze | solution.py:129
  30.5 0.0 collective-permute-done
  30.5 1.0 slice_bitcast_fusion.3
  31.5 23.9 %shard_map.118 = bf16[2048,128]{1,0:T(8,128)(2,1)} custom-call(bf16[2048,128]{1,0:T(8,128)(2,1)} %q_ref.1, bf16[2048,128]{1,0:T(8,128)(2,1)} %get-tuple-element.8.kp_ref, bf16[2048,128]{1,0:T(8,128)(2,1)} %k_ref.1, bf16[2048,128]{1,0:T(8,128)(2,1)} %get-tuple-element.6.kn_ref, bf16[2048,128]{1,0:T(8,128)(2,1)} %get-tuple-element.7.vp_ref, ...), custom_call_target="tpu_custom_call" | custom-call | tf_op jit(solution)/shard_map/pallas_call | solution.py:100
  55.4 1.1 copy.15
  56.5 21.0 %all_to_all.19 = bf16[8,256,128]{2,1,0:T(8,128)(2,1)S(1)} all-to-all(bf16[8,256,128]{2,1,0:T(8,128)(2,1)S(1)} %bitcast.44), channel_id=1, replica_groups=mesh['frame'=16,'hy'=2,'hz'=8] {'hz'}, dimensions={0} | all-to-all | bytes 1048576 | tf_op jit(solution)/shard_map/all_to_all | solution.py:139
  77.5 0.2 copy.16
  77.7 5.6 %collective-permute-start.2 = (bf16[256,1024]{0,1:T(8,128)(2,1)S(1)}, bf16[256,1024]{0,1:T(8,128)(2,1)S(1)}, u32[]{:S(2)}, u32[]{:S(2)}) collective-permute-start(bf16[256,1024]{0,1:T(8,128)(2,1)S(1)} %bitcast.38), channel_id=1, source_target_pairs={{0,16},{16,0},{32,48},{48,32},{64,80},{80,64},{96,112},{112,96},{1... | collective-permute-start | bytes 1572872 | tf_op jit(solution)/shard_map/ppermute | solution.py:140
  83.2 0.0 all-gather.2.cloned.1.call-done
  83.2 0.0 copy-start.3
  83.2 2.6 %convolution_bitcast_fusion.1 = f32[1,128,1536]{2,1,0:T(8,128)S(1)} fusion(bf16[1024,1536]{1,0:T(8,128)(2,1)} %all-gather.2.cloned.1.call-done, bf16[256,1024]{0,1:T(8,128)(2,1)S(1)} %bitcast.39, s32[]{:T(128)S(6)} %select_n.43), kind=kOutput, calls=%fused_computation.3 | convolution fusion | flops 402653184 | bytes 4194308 | tf_op jit(solution)/shard_map/dot_general | solution.py:145
  85.9 0.0 collective-permute-done.2
  85.9 0.2 copy-done.3
  86.1 0.6 convolution_bitcast_fusion
  86.7 1.3 pad_maximum_fusion
  88.0 1.0 collective-permute-start.3
  89.0 35.2 %collective-permute-done.3 = f32[2,128,1536]{2,1,0:T(8,128)S(1)} collective-permute-done((f32[2,128,1536]{2,1,0:T(8,128)}, f32[2,128,1536]{2,1,0:T(8,128)S(1)}, u32[]{:S(2)}, u32[]{:S(2)}) %collective-permute-start.3) | collective-permute-done | bytes 1572896 | tf_op jit(solution)/shard_map/ppermute | solution.py:148
  124.2 3.2 %fusion = bf16[128,1536]{1,0:T(8,128)(2,1)} fusion(bf16[1024,1536]{1,0:T(8,128)(2,1)} %all-gather.2.cloned.1.call-done, f32[2,128,1536]{2,1,0:T(8,128)S(1)} %collective-permute-done.3, bf16[256,1024]{0,1:T(8,128)(2,1)S(1)} %collective-permute-done.2, s32[]{:T(128)S(6)} %select_n.41), kind=kOutput, calls=%fused_computation.4 | convolution fusion | flops 403046400 | bytes 4587524 | tf_op jit(solution)/shard_map/dot_general | solution.py:145
  127.4 0.8 collective-permute-start.4
  128.2 2.5 %fusion.2 = bf16[128,1536]{1,0:T(8,128)(2,1)S(1)} fusion(f32[2,128,1536]{2,1,0:T(8,128)S(1)} %collective-permute-done.3, bf16[1024,1536]{1,0:T(8,128)(2,1)} %all-gather.2.cloned.1.call-done, bf16[256,1024]{0,1:T(8,128)(2,1)S(1)} %bitcast.40, s32[]{:T(128)S(6)} %select_n.41), kind=kOutput, calls=%fused_computation.10 | convolution fusion | flops 403046400 | bytes 4587524 | tf_op jit(solution)/shard_map/dot_general | solution.py:145
  130.7 0.0 collective-permute-done.4
  130.7 1.1 maximum_select_fusion
  (2 shorter events, 0.0 us)
Async XLA Ops:
  6.5 1.1 copy-start
  6.5 1.9 %copy-start.5 = (bf16[2048,128]{1,0:T(8,128)(2,1)S(1)}, bf16[2048,128]{1,0:T(8,128)(2,1)}, u32[]{:S(2)}) copy-start(bf16[2048,128]{1,0:T(8,128)(2,1)} %k_ref.1) | copy-start | bytes 1572868
  6.5 2.0 %copy-start.4 = (bf16[2048,128]{1,0:T(8,128)(2,1)S(1)}, bf16[2048,128]{1,0:T(8,128)(2,1)}, u32[]{:S(2)}) copy-start(bf16[2048,128]{1,0:T(8,128)(2,1)} %v_ref.1) | copy-start | bytes 1572868
  6.5 76.7 %all-gather.2.cloned.1.call-start = ((), (), s32[]{:S(2)}) async-start(), calls=%async_computation.1 | async-start | bytes 3538944 | tf_op jit(solution)/shard_map/all_gather | solution.py:136
  7.7 7.5 %copy-start.1 = (s32[1,1,32,45]{3,2,1,0:T(8,128)S(1)}, s32[1,1,32,45]{3,2,1,0:T(8,128)}, u32[]{:S(2)}) copy-start(s32[1,1,32,45]{3,2,1,0:T(8,128)} %param.15) | copy-start | bytes 17284
  7.7 7.5 %copy-start.2 = (s32[1728]{0:T(1024)S(1)}, s32[1728]{0:T(1024)}, u32[]{:S(2)}) copy-start(s32[1728]{0:T(1024)} %constant.87) | copy-start | bytes 20740
  9.6 18.6 %collective-permute-start.1 = (bf16[2,2048,128]{2,1,0:T(8,128)(2,1)}, bf16[2,2048,128]{2,1,0:T(8,128)(2,1)}, u32[]{:S(2)}, u32[]{:S(2)}) collective-permute-start(bf16[2,2048,128]{2,1,0:T(8,128)(2,1)} %pad_maximum_fusion.1), channel_id=1, source_target_pairs={{16,0},{32,16},{48,32},{64,48},{80,64},{96,80},{112,96},{128,112},... | collective-permute-start | bytes 3145736 | tf_op jit(solution)/shard_map/ppermute | solution.py:126
  12.2 18.3 %collective-permute-start = (bf16[2,2048,128]{2,1,0:T(8,128)(2,1)}, bf16[2,2048,128]{2,1,0:T(8,128)(2,1)S(1)}, u32[]{:S(2)}, u32[]{:S(2)}) collective-permute-start(bf16[2,2048,128]{2,1,0:T(8,128)(2,1)} %pad_maximum_fusion.1), channel_id=1, source_target_pairs={{0,16},{16,32},{32,48},{48,64},{64,80},{80,96},{96,112},{112,128},... | collective-permute-start | bytes 3145736 | tf_op jit(solution)/shard_map/ppermute | solution.py:125
  15.2 11.0 %copy-start.7 = (pred[1728]{0:T(1024)(128)(4,1)S(1)}, pred[1728]{0:T(1024)(128)(4,1)}, u32[]{:S(2)}) copy-start(pred[1728]{0:T(1024)(128)(4,1)} %constant.89) | copy-start | bytes 5188
  15.2 11.0 %copy-start.8 = (pred[1728]{0:T(1024)(128)(4,1)S(1)}, pred[1728]{0:T(1024)(128)(4,1)}, u32[]{:S(2)}) copy-start(pred[1728]{0:T(1024)(128)(4,1)} %constant.88) | copy-start | bytes 5188
  15.2 11.2 %copy-start.6 = (s32[16,2,9,6]{3,2,1,0:T(8,128)S(1)}, s32[16,2,9,6]{3,2,1,0:T(8,128)}, u32[]{:S(2)}) copy-start(s32[16,2,9,6]{3,2,1,0:T(8,128)} %constant.60.clone) | copy-start | bytes 20740
  77.7 8.2 %collective-permute-start.2 = (bf16[256,1024]{0,1:T(8,128)(2,1)S(1)}, bf16[256,1024]{0,1:T(8,128)(2,1)S(1)}, u32[]{:S(2)}, u32[]{:S(2)}) collective-permute-start(bf16[256,1024]{0,1:T(8,128)(2,1)S(1)} %bitcast.38), channel_id=1, source_target_pairs={{0,16},{16,0},{32,48},{48,32},{64,80},{80,64},{96,112},{112,96},{1... | collective-permute-start | bytes 1572872 | tf_op jit(solution)/shard_map/ppermute | solution.py:140
  83.2 2.8 %copy-start.3 = (bf16[1024,1536]{1,0:T(8,128)(2,1)S(1)}, bf16[1024,1536]{1,0:T(8,128)(2,1)}, u32[]{:S(2)}) copy-start(bf16[1024,1536]{1,0:T(8,128)(2,1)} %all-gather.2.cloned.1.call-done) | copy-start | bytes 9437188
  88.0 36.2 %collective-permute-start.3 = (f32[2,128,1536]{2,1,0:T(8,128)}, f32[2,128,1536]{2,1,0:T(8,128)S(1)}, u32[]{:S(2)}, u32[]{:S(2)}) collective-permute-start(f32[2,128,1536]{2,1,0:T(8,128)} %pad_maximum_fusion), channel_id=1, source_target_pairs={{0,8},{8,0},{1,9},{9,1},{2,10},{10,2},{3,11},{11,3},{4,12},{12,4},... | collective-permute-start | bytes 4718600 | tf_op jit(solution)/shard_map/ppermute | solution.py:148
  127.4 3.3 %collective-permute-start.4 = (bf16[128,1536]{1,0:T(8,128)(2,1)}, bf16[128,1536]{1,0:T(8,128)(2,1)S(1)}, u32[]{:S(2)}, u32[]{:S(2)}) collective-permute-start(bf16[128,1536]{1,0:T(8,128)(2,1)} %fusion), channel_id=1, source_target_pairs={{0,16},{16,0},{32,48},{48,32},{64,80},{80,64},{96,112},{112,96},{1... | collective-permute-start | bytes 1179656 | tf_op jit(solution)/shard_map/ppermute | solution.py:150
Sparse Core Ops, SparseCore 0:
  9.2 47.5 all-gather.1

commit v5 on v4

--- a/solution.py
+++ b/solution.py
@@ -48,9 +48,24 @@
     return qtile, offset, static_ok, centre, frame_step
 
 
+def window_picks():
+    picks = np.zeros((TCOLS, WIN, SEGS, KCOLS), np.float32)
+    for col in range(TCOLS):
+        start = min(max(QTILES * (col // QTILES) - 2, 0), TCOLS - KCOLS)
+        for seg in range(SEGS):
+            df, dr = divmod(seg, 3)
+            for j in range(KCOLS):
+                dc = start + j - col
+                if abs(dc) <= 2:
+                    picks[col, 15 * df + 5 * dr + dc + 2, seg, j] = 1.0
+    return picks
+
+
 def window_bias(mask_rows, frame, frames_total):
     qtile, offset, static_ok, centre, frame_step = window_tables()
-    chosen = mask_rows[qtile, offset] > 0
+    grid = mask_rows.astype(jnp.float32).reshape(TROWS, TCOLS, WIN)
+    chosen = jnp.einsum("rcw,cwk->rck", grid, window_picks().reshape(TCOLS, WIN, SEGS * KCOLS))
+    chosen = chosen.reshape(static_ok.shape) > 0.5
     key_frame = frame + frame_step
     inside = (key_frame >= 0) & (key_frame < frames_total)
     allowed = (chosen | centre) & static_ok & inside
@@ -145,9 +160,11 @@
         return jnp.dot(rows, weight_half, preferred_element_type=jnp.float32)
 
     flip = [(0, 1), (1, 0)]
-    sent = lax.ppermute(jnp.stack([project(mine, 1 - side), project(theirs, 1 - side)]), "hy", flip)
-    own_half = (project(mine, side) + sent[0]).astype(jnp.bfloat16)
-    other_half = lax.ppermute((project(theirs, side) + sent[1]).astype(jnp.bfloat16), "frame", partners)
+    sent_mine = lax.ppermute(project(mine, 1 - side).astype(jnp.bfloat16), "hy", flip)
+    sent_theirs = lax.ppermute(project(theirs, 1 - side).astype(jnp.bfloat16), "hy", flip)
+    other = (project(theirs, side) + sent_theirs.astype(jnp.float32)).astype(jnp.bfloat16)
+    other_half = lax.ppermute(other, "frame", partners)
+    own_half = (project(mine, side) + sent_mine.astype(jnp.float32)).astype(jnp.bfloat16)
     return jnp.where(
         core == 0,
         jnp.concatenate([own_half, other_half], axis=1),

time: 140 us -> 118 us (0.84)
  waiting for transfers between devices: 35.2 us -> 23.1 us
  local copies, waits for them, and re-layouts: 19.5 us -> 9.5 us
  starting transfers between devices: 13 us -> 16.2 us
    ppermute x2 -> x3, waiting for transfers between devices: 35.2 us -> 12.8 us  [the longest x1 6.41 us: on_device(): lax.ppermute(project(theirs, 1 - side).astype(jnp.bfloat16), 'hy', flip)]
    gather x1 -> x0, local copies, waits for them, and re-layouts: 10.9 us -> none  [window_bias(): chosen = mask_rows[qtile, offset] > 0]
    ppermute x1, waiting for transfers between devices: 0.01 us -> 8.8 us  [on_device(): nxt = lax.ppermute(pair, 'frame', backward)]
    ppermute x2 -> x3, starting transfers between devices: 1.8 us -> 3.56 us  [the longest x1 1.98 us: on_device(): lax.ppermute(project(theirs, 1 - side).astype(jnp.bfloat16), 'hy', flip)]
    ppermute x1, waiting for transfers between devices: 0.01 us -> 1.54 us  [on_device(): theirs = lax.ppermute(mine, 'frame', partners)]
    ppermute x1, starting transfers between devices: 5.56 us -> 7 us  [on_device(): theirs = lax.ppermute(mine, 'frame', partners)]
  transfers between devices with their start and end apart: 6 -> 7, of which waited for: 1 -> 4; matrix products, arithmetic and copies ran while one was open for 17% -> 13% of each run, Pallas kernels for 17% -> 20%
where the time goes in v5:
time: 118 us; the launch traced here: 117 us
  Pallas kernels  23.9 us (20%)
  waiting for transfers between devices  23.1 us (20%)
  blocking collectives  20.2 us (17%)
  starting transfers between devices  16.2 us (14%)
  between operations  13.6 us (12%)
  local copies, waits for them, and re-layouts  9.5 us (8%)
  matrix products  8.4 us (7%)
  other arithmetic  2.45 us (2%)
    pallas_call x1, Pallas kernels, attend(): pl.pallas_call(attention_kernel, grid=(TROWS, GROUPS), in_specs=[pl.Block...  23.9 us
    all_to_all x1, blocking collectives, on_device(): mine = lax.all_to_all(chunks, 'hz', 0, 1, tiled=True)  20.2 us
    ppermute x1, waiting for transfers between devices, on_device(): nxt = lax.ppermute(pair, 'frame', backward)  8.8 us
    dot_general x4, matrix products, project(): return jnp.dot(rows, weight_half, preferred_element_type=jnp.float32)  8.25 us
    ppermute x1, starting transfers between devices, on_device(): theirs = lax.ppermute(mine, 'frame', partners)  7 us
    ppermute x1, waiting for transfers between devices, on_device(): lax.ppermute(project(theirs, 1 - side).astype(jnp.bfloat16), 'hy', flip)  6.41 us
    ppermute x1, waiting for transfers between devices, on_device(): lax.ppermute(project(mine, 1 - side).astype(jnp.bfloat16), 'hy', flip)  6.34 us
    ppermute x1, starting transfers between devices, on_device(): prev = lax.ppermute(pair, 'frame', forward)  3.02 us
  transfers between devices with their start and end apart: 7, of which 4 were waited for; matrix products, arithmetic and copies ran while one was open for 13% of the time, Pallas kernels for 20%

profile of v5, /device:TPU:17, one launch (start us, length us, event | category | flops | bytes accessed | tf_op | source)
XLA Modules:
  0.0 117.3 jit_solution(15538986429995233131)
XLA Ops:
  6.5 0.0 copy-start
  6.5 0.0 copy-start.5
  6.5 0.0 copy-start.6
  6.5 0.0 copy-start.4
  6.5 0.0 copy-start.2
  6.6 0.0 copy-start.3
  6.6 0.0 all-gather.2.cloned.1.call-start
  6.6 1.1 copy-done
  7.7 0.8 constant_dynamic-slice_fusion
  8.5 0.0 all-gather.2.cloned.1.call-update
  8.5 1.3 %pad_maximum_fusion = bf16[2,2048,128]{2,1,0:T(8,128)(2,1)S(1)} fusion(bf16[1,2048,128]{2,1,0:T(8,128)(2,1)} %bitcast.31, bf16[1,2048,128]{2,1,0:T(8,128)(2,1)} %bitcast.32), kind=kLoop, calls=%fused_computation.8 | loop fusion | flops 524288 | bytes 2097152 | tf_op jit(solution)/shard_map/stack | solution.py:139
  9.8 2.6 %collective-permute-start.1 = (bf16[2,2048,128]{2,1,0:T(8,128)(2,1)S(1)}, bf16[2,2048,128]{2,1,0:T(8,128)(2,1)}, u32[]{:S(2)}, u32[]{:S(2)}) collective-permute-start(bf16[2,2048,128]{2,1,0:T(8,128)(2,1)S(1)} %pad_maximum_fusion), channel_id=1, source_target_pairs={{16,0},{32,16},{48,32},{64,48},{80,64},{96,80},{112,96},{128,112},... | collective-permute-start | bytes 3145736 | tf_op jit(solution)/shard_map/ppermute | solution.py:141
  12.4 3.0 %collective-permute-start = (bf16[2,2048,128]{2,1,0:T(8,128)(2,1)S(1)}, bf16[2,2048,128]{2,1,0:T(8,128)(2,1)}, u32[]{:S(2)}, u32[]{:S(2)}) collective-permute-start(bf16[2,2048,128]{2,1,0:T(8,128)(2,1)S(1)} %pad_maximum_fusion), channel_id=1, source_target_pairs={{0,16},{16,32},{32,48},{48,64},{64,80},{80,96},{96,112},{112,128},... | collective-permute-start | bytes 3145736 | tf_op jit(solution)/shard_map/ppermute | solution.py:140
  15.4 0.0 copy-done.3
  15.4 0.0 copy-done.5
  15.5 0.0 copy-done.6
  15.5 0.0 copy-done.4
  15.5 0.1 fusion.3
  15.6 0.1 reshape.24
  15.8 0.0 copy-done.2
  15.8 0.1 fusion.13
  15.9 0.4 broadcast_in_dim.16
  16.3 0.3 reshape.19
  16.5 1.0 copy.14.bias_ref
  17.6 8.8 %collective-permute-done.1 = bf16[2,2048,128]{2,1,0:T(8,128)(2,1)} collective-permute-done((bf16[2,2048,128]{2,1,0:T(8,128)(2,1)S(1)}, bf16[2,2048,128]{2,1,0:T(8,128)(2,1)}, u32[]{:S(2)}, u32[]{:S(2)}) %collective-permute-start.1) | collective-permute-done | bytes 1048608 | tf_op jit(solution)/shard_map/ppermute | solution.py:141
  26.4 2.3 %slice_bitcast_fusion = (bf16[2048,128]{1,0:T(8,128)(2,1)}, bf16[2048,128]{1,0:T(8,128)(2,1)}) fusion(bf16[2,2048,128]{2,1,0:T(8,128)(2,1)} %collective-permute-done.1), kind=kLoop, calls=%fused_computation.11 | loop fusion | bytes 2097152 | tf_op jit(solution)/shard_map/squeeze | solution.py:144
  28.6 0.0 collective-permute-done
  28.6 2.3 %slice_bitcast_fusion.1 = (bf16[2048,128]{1,0:T(8,128)(2,1)}, bf16[2048,128]{1,0:T(8,128)(2,1)}) fusion(bf16[2,2048,128]{2,1,0:T(8,128)(2,1)} %collective-permute-done), kind=kLoop, calls=%fused_computation.12 | loop fusion | bytes 2097152 | tf_op jit(solution)/shard_map/squeeze | solution.py:144
  30.9 23.9 %shard_map.91 = bf16[2048,128]{1,0:T(8,128)(2,1)} custom-call(bf16[2048,128]{1,0:T(8,128)(2,1)} %q_ref.1, bf16[2048,128]{1,0:T(8,128)(2,1)} %get-tuple-element.8.kp_ref, bf16[2048,128]{1,0:T(8,128)(2,1)} %k_ref.1, bf16[2048,128]{1,0:T(8,128)(2,1)} %get-tuple-element.6.kn_ref, bf16[2048,128]{1,0:T(8,128)(2,1)} %get-tuple-element.7.vp_ref, ...), custom_call_target="tpu_custom_call" | custom-call | tf_op jit(solution)/shard_map/pallas_call | solution.py:115
  54.8 1.1 copy.15
  55.9 20.2 %all_to_all.19 = bf16[8,256,128]{2,1,0:T(8,128)(2,1)S(1)} all-to-all(bf16[8,256,128]{2,1,0:T(8,128)(2,1)S(1)} %bitcast.33), channel_id=1, replica_groups=mesh['frame'=16,'hy'=2,'hz'=8] {'hz'}, dimensions={0} | all-to-all | bytes 1048576 | tf_op jit(solution)/shard_map/all_to_all | solution.py:154
  76.1 0.2 copy.16
  76.3 7.0 %collective-permute-start.3 = (bf16[256,1024]{0,1:T(8,128)(2,1)S(1)}, bf16[256,1024]{0,1:T(8,128)(2,1)S(1)}, u32[]{:S(2)}, u32[]{:S(2)}) collective-permute-start(bf16[256,1024]{0,1:T(8,128)(2,1)S(1)} %bitcast.27), channel_id=1, source_target_pairs={{0,16},{16,0},{32,48},{48,32},{64,80},{80,64},{96,112},{112,96},{1... | collective-permute-start | bytes 1572872 | tf_op jit(solution)/shard_map/ppermute | solution.py:155
  83.3 1.5 %collective-permute-done.3 = bf16[256,1024]{0,1:T(8,128)(2,1)S(1)} collective-permute-done((bf16[256,1024]{0,1:T(8,128)(2,1)S(1)}, bf16[256,1024]{0,1:T(8,128)(2,1)S(1)}, u32[]{:S(2)}, u32[]{:S(2)}) %collective-permute-start.3) | collective-permute-done | bytes 524320 | tf_op jit(solution)/shard_map/ppermute | solution.py:155
  84.8 0.0 all-gather.2.cloned.1.call-done
  84.8 2.5 %convolution_convert_fusion = bf16[128,1536]{1,0:T(8,128)(2,1)S(1)} fusion(bf16[1024,1536]{1,0:T(8,128)(2,1)} %all-gather.2.cloned.1.call-done, bf16[256,1024]{0,1:T(8,128)(2,1)S(1)} %collective-permute-done.3, s32[]{:T(128)S(6)} %select_n.35), kind=kOutput, calls=%fused_computation.2 | convolution fusion | flops 402849792 | bytes 3801092 | tf_op jit(solution)/shard_map/dot_general | solution.py:160
  87.3 2.0 %collective-permute-start.4 = (bf16[128,1536]{1,0:T(8,128)(2,1)S(1)}, bf16[128,1536]{1,0:T(8,128)(2,1)S(1)}, u32[]{:S(2)}, u32[]{:S(2)}) collective-permute-start(bf16[128,1536]{1,0:T(8,128)(2,1)S(1)} %convolution_convert_fusion), channel_id=1, source_target_pairs={{0,8},{8,0},{1,9},{9,1},{2,10},{10,2},{3,11},{11,3},{4,12},{12,4},... | collective-permute-start | bytes 1179656 | tf_op jit(solution)/shard_map/ppermute | solution.py:164
  89.3 0.0 copy-start.1
  89.3 2.6 %convolution_convert_fusion.1 = bf16[128,1536]{1,0:T(8,128)(2,1)S(1)} fusion(bf16[1024,1536]{1,0:T(8,128)(2,1)} %all-gather.2.cloned.1.call-done, bf16[256,1024]{0,1:T(8,128)(2,1)S(1)} %bitcast.28, s32[]{:T(128)S(6)} %select_n.35), kind=kOutput, calls=%fused_computation.3 | convolution fusion | flops 402849792 | bytes 3801092 | tf_op jit(solution)/shard_map/dot_general | solution.py:160
  92.0 0.1 collective-permute-start.2
  92.1 6.4 %collective-permute-done.4 = bf16[128,1536]{1,0:T(8,128)(2,1)S(1)} collective-permute-done((bf16[128,1536]{1,0:T(8,128)(2,1)S(1)}, bf16[128,1536]{1,0:T(8,128)(2,1)S(1)}, u32[]{:S(2)}, u32[]{:S(2)}) %collective-permute-start.4) | collective-permute-done | bytes 393248 | tf_op jit(solution)/shard_map/ppermute | solution.py:164
  98.5 0.0 copy-done.1
  98.5 0.6 fusion
  99.1 1.5 %collective-permute-start.5 = (bf16[128,1536]{1,0:T(8,128)(2,1)S(1)}, bf16[128,1536]{1,0:T(8,128)(2,1)S(1)}, u32[]{:S(2)}, u32[]{:S(2)}) collective-permute-start(bf16[128,1536]{1,0:T(8,128)(2,1)S(1)} %fusion), channel_id=1, source_target_pairs={{0,16},{16,0},{32,48},{48,32},{64,80},{80,64},{96,112},{112,96},{1... | collective-permute-start | bytes 1179656 | tf_op jit(solution)/shard_map/ppermute | solution.py:166
  100.6 6.3 %collective-permute-done.2 = bf16[128,1536]{1,0:T(8,128)(2,1)S(1)} collective-permute-done((bf16[128,1536]{1,0:T(8,128)(2,1)S(1)}, bf16[128,1536]{1,0:T(8,128)(2,1)S(1)}, u32[]{:S(2)}, u32[]{:S(2)}) %collective-permute-start.2) | collective-permute-done | bytes 393248 | tf_op jit(solution)/shard_map/ppermute | solution.py:163
  106.9 2.5 %add_convert_fusion = bf16[128,1536]{1,0:T(8,128)(2,1)S(1)} fusion(bf16[128,1536]{1,0:T(8,128)(2,1)S(1)} %collective-permute-done.2, bf16[1024,1536]{1,0:T(8,128)(2,1)} %all-gather.2.cloned.1.call-done, bf16[256,1024]{0,1:T(8,128)(2,1)S(1)} %bitcast.29, s32[]{:T(128)S(6)} %select_n.33), kind=kOutput, calls=%fused_computation.10 | convolution fusion | flops 403243008 | bytes 4194308 | tf_op jit(solution)/shard_map/dot_general | solution.py:160
  109.4 0.0 collective-permute-done.5
  109.4 1.1 maximum_select_fusion
  (3 shorter events, 0.0 us)
Async XLA Ops:
  6.5 1.1 copy-start
  6.5 8.9 %copy-start.5 = (pred[8,54,4]{1,2,0:T(4,128)(4,1)S(1)}, pred[8,54,4]{1,2,0:T(4,128)(4,1)}, u32[]{:S(2)}) copy-start(pred[8,54,4]{1,2,0:T(4,128)(4,1)} %constant.57) | copy-start | bytes 5188
  6.5 8.9 %copy-start.6 = (pred[8,54,4]{1,2,0:T(4,128)(4,1)S(1)}, pred[8,54,4]{1,2,0:T(4,128)(4,1)}, u32[]{:S(2)}) copy-start(pred[8,54,4]{1,2,0:T(4,128)(4,1)} %constant.59) | copy-start | bytes 5188
  6.5 8.9 %copy-start.4 = (bf16[8,45,54]{2,1,0:T(8,128)(2,1)S(1)}, bf16[8,45,54]{2,1,0:T(8,128)(2,1)}, u32[]{:S(2)}) copy-start(bf16[8,45,54]{2,1,0:T(8,128)(2,1)} %constant.78) | copy-start | bytes 116644
  6.5 9.2 %copy-start.2 = (s32[16,2,9,6]{3,2,1,0:T(8,128)S(1)}, s32[16,2,9,6]{3,2,1,0:T(8,128)}, u32[]{:S(2)}) copy-start(s32[16,2,9,6]{3,2,1,0:T(8,128)} %constant.52.clone) | copy-start | bytes 20740
  6.6 8.9 %copy-start.3 = (s32[1,1,32,45]{3,2,1,0:T(8,128)S(1)}, s32[1,1,32,45]{3,2,1,0:T(8,128)}, u32[]{:S(2)}) copy-start(s32[1,1,32,45]{3,2,1,0:T(8,128)} %param.12) | copy-start | bytes 17284
  6.6 78.3 %all-gather.2.cloned.1.call-start = ((), (), s32[]{:S(2)}) async-start(), calls=%async_computation.1 | async-start | bytes 3538944 | tf_op jit(solution)/shard_map/all_gather | solution.py:151
  9.8 16.6 %collective-permute-start.1 = (bf16[2,2048,128]{2,1,0:T(8,128)(2,1)S(1)}, bf16[2,2048,128]{2,1,0:T(8,128)(2,1)}, u32[]{:S(2)}, u32[]{:S(2)}) collective-permute-start(bf16[2,2048,128]{2,1,0:T(8,128)(2,1)S(1)} %pad_maximum_fusion), channel_id=1, source_target_pairs={{16,0},{32,16},{48,32},{64,48},{80,64},{96,80},{112,96},{128,112},... | collective-permute-start | bytes 3145736 | tf_op jit(solution)/shard_map/ppermute | solution.py:141
  12.4 16.2 %collective-permute-start = (bf16[2,2048,128]{2,1,0:T(8,128)(2,1)S(1)}, bf16[2,2048,128]{2,1,0:T(8,128)(2,1)}, u32[]{:S(2)}, u32[]{:S(2)}) collective-permute-start(bf16[2,2048,128]{2,1,0:T(8,128)(2,1)S(1)} %pad_maximum_fusion), channel_id=1, source_target_pairs={{0,16},{16,32},{32,48},{48,64},{64,80},{80,96},{96,112},{112,128},... | collective-permute-start | bytes 3145736 | tf_op jit(solution)/shard_map/ppermute | solution.py:140
  76.3 8.5 %collective-permute-start.3 = (bf16[256,1024]{0,1:T(8,128)(2,1)S(1)}, bf16[256,1024]{0,1:T(8,128)(2,1)S(1)}, u32[]{:S(2)}, u32[]{:S(2)}) collective-permute-start(bf16[256,1024]{0,1:T(8,128)(2,1)S(1)} %bitcast.27), channel_id=1, source_target_pairs={{0,16},{16,0},{32,48},{48,32},{64,80},{80,64},{96,112},{112,96},{1... | collective-permute-start | bytes 1572872 | tf_op jit(solution)/shard_map/ppermute | solution.py:155
  87.3 11.2 %collective-permute-start.4 = (bf16[128,1536]{1,0:T(8,128)(2,1)S(1)}, bf16[128,1536]{1,0:T(8,128)(2,1)S(1)}, u32[]{:S(2)}, u32[]{:S(2)}) collective-permute-start(bf16[128,1536]{1,0:T(8,128)(2,1)S(1)} %convolution_convert_fusion), channel_id=1, source_target_pairs={{0,8},{8,0},{1,9},{9,1},{2,10},{10,2},{3,11},{11,3},{4,12},{12,4},... | collective-permute-start | bytes 1179656 | tf_op jit(solution)/shard_map/ppermute | solution.py:164
  89.3 9.2 %copy-start.1 = (bf16[1024,1536]{1,0:T(8,128)(2,1)S(1)}, bf16[1024,1536]{1,0:T(8,128)(2,1)}, u32[]{:S(2)}) copy-start(bf16[1024,1536]{1,0:T(8,128)(2,1)} %all-gather.2.cloned.1.call-done) | copy-start | bytes 9437188
  92.0 14.9 %collective-permute-start.2 = (bf16[128,1536]{1,0:T(8,128)(2,1)S(1)}, bf16[128,1536]{1,0:T(8,128)(2,1)S(1)}, u32[]{:S(2)}, u32[]{:S(2)}) collective-permute-start(bf16[128,1536]{1,0:T(8,128)(2,1)S(1)} %convolution_convert_fusion.1), channel_id=1, source_target_pairs={{0,8},{8,0},{1,9},{9,1},{2,10},{10,2},{3,11},{11,3},{4,12},{12,4},... | collective-permute-start | bytes 1179656 | tf_op jit(solution)/shard_map/ppermute | solution.py:163
  99.1 10.3 %collective-permute-start.5 = (bf16[128,1536]{1,0:T(8,128)(2,1)S(1)}, bf16[128,1536]{1,0:T(8,128)(2,1)S(1)}, u32[]{:S(2)}, u32[]{:S(2)}) collective-permute-start(bf16[128,1536]{1,0:T(8,128)(2,1)S(1)} %fusion), channel_id=1, source_target_pairs={{0,16},{16,0},{32,48},{48,32},{64,80},{80,64},{96,112},{112,96},{1... | collective-permute-start | bytes 1179656 | tf_op jit(solution)/shard_map/ppermute | solution.py:166
Sparse Core Ops, SparseCore 0:
  9.2 47.5 all-gather.1

commit v6 on v5

--- a/solution.py
+++ b/solution.py
@@ -127,6 +127,47 @@
     )(q, kp, k, kn, vp, v, vn, bias)
 
 
+def exchange_kernel(x_ref, o_ref, send_sem, recv_sem):
+    me = lax.axis_index("hz")
+    peers = lax.axis_size("hz")
+    frame = lax.axis_index("frame")
+    side = lax.axis_index("hy")
+    mesh = pl.DeviceIdType.MESH
+    barrier = pltpu.get_barrier_semaphore()
+    for i in range(1, peers):
+        peer = lax.rem(me + i, peers)
+        pl.semaphore_signal(barrier, inc=1, device_id=(frame, side, peer), device_id_type=mesh)
+    pl.semaphore_wait(barrier, peers - 1)
+    copies = []
+    for i in range(1, peers):
+        peer = lax.rem(me + i, peers)
+        copy = pltpu.make_async_remote_copy(
+            src_ref=x_ref.at[peer],
+            dst_ref=o_ref.at[me],
+            send_sem=send_sem.at[i],
+            recv_sem=recv_sem.at[i],
+            device_id=(frame, side, peer),
+            device_id_type=mesh,
+        )
+        copy.start()
+        copies.append(copy)
+    o_ref[me] = x_ref[me]
+    for copy in copies:
+        copy.wait()
+
+
+def exchange(x):
+    peers = x.shape[0]
+    return pl.pallas_call(
+        exchange_kernel,
+        out_shape=jax.ShapeDtypeStruct(x.shape, x.dtype),
+        in_specs=[pl.BlockSpec(memory_space=pltpu.VMEM)],
+        out_specs=pl.BlockSpec(memory_space=pltpu.VMEM),
+        scratch_shapes=[pltpu.SemaphoreType.DMA((peers,)), pltpu.SemaphoreType.DMA((peers,))],
+        compiler_params=pltpu.CompilerParams(collective_id=0, has_side_effects=True),
+    )(x)
+
+
 def on_device(queries, keys, values, block_mask, out_weight):
     tok_dev = queries.shape[0]
     frames_here = tok_dev // (TROWS * TCOLS * TILE)
@@ -150,8 +191,9 @@
     weight_half = lax.dynamic_slice_in_dim(out_weight, core * half, half, axis=1)
     weight_half = lax.all_gather(weight_half, "hz", axis=0, tiled=True)
     chunks = attention.reshape(sides, -1, tok_dev // (sides * lax.axis_size("hz")), HEAD_DIM)
-    chunks = chunks.transpose(1, 0, 2, 3).reshape(tok_dev, HEAD_DIM)
-    mine = lax.all_to_all(chunks, "hz", 0, 1, tiled=True)
+    peers = lax.axis_size("hz")
+    chunks = chunks.transpose(1, 0, 2, 3).reshape(peers, tok_dev // peers, HEAD_DIM)
+    mine = exchange(chunks).transpose(1, 0, 2).reshape(tok_dev // peers, peers * HEAD_DIM)
     theirs = lax.ppermute(mine, "frame", partners)
     block = mine.shape[0] // sides
 

time: 118 us -> 116 us (0.983)
  blocking collectives: 20.2 us -> 0 us
  Pallas kernels: 23.9 us -> 40.4 us
  local copies, waits for them, and re-layouts: 9.5 us -> 11.3 us
    all_to_all x1 -> x0, blocking collectives: 20.2 us -> none  [on_device(): mine = lax.all_to_all(chunks, 'hz', 0, 1, tiled=True)]
    pallas_call x0 -> x1, Pallas kernels: none -> 16.5 us  [exchange(): pl.pallas_call(exchange_kernel, out_shape=jax.ShapeDtypeStruct(x.shape, x...]
    transpose x0 -> x1, local copies, waits for them, and re-layouts: none -> 1.25 us  [on_device(): exchange(chunks).transpose(1, 0, 2)]
  transfers between devices with their start and end apart: 7 -> 7, of which waited for: 4 -> 4; matrix products, arithmetic and copies ran while one was open for 13% -> 15% of each run, Pallas kernels for 20% -> 35%
where the time goes in v6:
time: 116 us; the launch traced here: 115 us
  Pallas kernels  40.4 us (35%)
  waiting for transfers between devices  22.2 us (19%)
  starting transfers between devices  16.7 us (14%)
  between operations  13.6 us (12%)
  local copies, waits for them, and re-layouts  11.3 us (10%)
  matrix products  8.39 us (7%)
  other arithmetic  2.45 us (2%)
    pallas_call x1, Pallas kernels, attend(): pl.pallas_call(attention_kernel, grid=(TROWS, GROUPS), in_specs=[pl.Block...  23.9 us
    pallas_call x1, Pallas kernels, exchange(): pl.pallas_call(exchange_kernel, out_shape=jax.ShapeDtypeStruct(x.shape, x...  16.5 us
    ppermute x1, waiting for transfers between devices, on_device(): nxt = lax.ppermute(pair, 'frame', backward)  8.8 us
    dot_general x4, matrix products, project(): return jnp.dot(rows, weight_half, preferred_element_type=jnp.float32)  8.24 us
    ppermute x1, starting transfers between devices, on_device(): theirs = lax.ppermute(mine, 'frame', partners)  7.3 us
    ppermute x1, waiting for transfers between devices, on_device(): lax.ppermute(project(theirs, 1 - side).astype(jnp.bfloat16), 'hy', flip)  6.13 us
    ppermute x1, waiting for transfers between devices, on_device(): lax.ppermute(project(mine, 1 - side).astype(jnp.bfloat16), 'hy', flip)  5.73 us
    ppermute x1, starting transfers between devices, on_device(): prev = lax.ppermute(pair, 'frame', forward)  3.02 us
  transfers between devices with their start and end apart: 7, of which 4 were waited for; matrix products, arithmetic and copies ran while one was open for 15% of the time, Pallas kernels for 35%

profile of v6, /device:TPU:17, one launch (start us, length us, event | category | flops | bytes accessed | tf_op | source)
XLA Modules:
  0.0 115.1 jit_solution(8159913569083315889)
XLA Ops:
  6.5 0.0 copy-start
  6.5 0.0 copy-start.5
  6.5 0.0 copy-start.6
  6.5 0.0 copy-start.4
  6.5 0.0 copy-start.2
  6.6 0.0 copy-start.3
  6.6 0.0 all-gather.2.cloned.1.call-start
  6.6 1.1 copy-done
  7.7 0.8 constant_dynamic-slice_fusion
  8.5 0.0 all-gather.2.cloned.1.call-update
  8.5 1.3 %pad_maximum_fusion = bf16[2,2048,128]{2,1,0:T(8,128)(2,1)S(1)} fusion(bf16[1,2048,128]{2,1,0:T(8,128)(2,1)} %bitcast.31, bf16[1,2048,128]{2,1,0:T(8,128)(2,1)} %bitcast.32), kind=kLoop, calls=%fused_computation.8 | loop fusion | flops 524288 | bytes 2097152 | tf_op jit(solution)/shard_map/stack | solution.py:180
  9.8 2.6 %collective-permute-start.1 = (bf16[2,2048,128]{2,1,0:T(8,128)(2,1)S(1)}, bf16[2,2048,128]{2,1,0:T(8,128)(2,1)}, u32[]{:S(2)}, u32[]{:S(2)}) collective-permute-start(bf16[2,2048,128]{2,1,0:T(8,128)(2,1)S(1)} %pad_maximum_fusion), channel_id=1, source_target_pairs={{16,0},{32,16},{48,32},{64,48},{80,64},{96,80},{112,96},{128,112},... | collective-permute-start | bytes 3145736 | tf_op jit(solution)/shard_map/ppermute | solution.py:182
  12.4 3.0 %collective-permute-start = (bf16[2,2048,128]{2,1,0:T(8,128)(2,1)S(1)}, bf16[2,2048,128]{2,1,0:T(8,128)(2,1)}, u32[]{:S(2)}, u32[]{:S(2)}) collective-permute-start(bf16[2,2048,128]{2,1,0:T(8,128)(2,1)S(1)} %pad_maximum_fusion), channel_id=1, source_target_pairs={{0,16},{16,32},{32,48},{48,64},{64,80},{80,96},{96,112},{112,128},... | collective-permute-start | bytes 3145736 | tf_op jit(solution)/shard_map/ppermute | solution.py:181
  15.4 0.0 copy-done.3
  15.4 0.0 copy-done.5
  15.5 0.0 copy-done.6
  15.5 0.0 copy-done.4
  15.5 0.1 fusion.3
  15.6 0.1 reshape.27
  15.8 0.0 copy-done.2
  15.8 0.1 fusion.13
  15.9 0.4 broadcast_in_dim.16
  16.3 0.3 reshape.20
  16.5 1.0 copy.15.bias_ref
  17.6 8.8 %collective-permute-done.1 = bf16[2,2048,128]{2,1,0:T(8,128)(2,1)} collective-permute-done((bf16[2,2048,128]{2,1,0:T(8,128)(2,1)S(1)}, bf16[2,2048,128]{2,1,0:T(8,128)(2,1)}, u32[]{:S(2)}, u32[]{:S(2)}) %collective-permute-start.1) | collective-permute-done | bytes 1048608 | tf_op jit(solution)/shard_map/ppermute | solution.py:182
  26.4 2.3 %slice_bitcast_fusion = (bf16[2048,128]{1,0:T(8,128)(2,1)}, bf16[2048,128]{1,0:T(8,128)(2,1)}) fusion(bf16[2,2048,128]{2,1,0:T(8,128)(2,1)} %collective-permute-done.1), kind=kLoop, calls=%fused_computation.11 | loop fusion | bytes 2097152 | tf_op jit(solution)/shard_map/squeeze | solution.py:185
  28.6 0.0 collective-permute-done
  28.6 2.3 %slice_bitcast_fusion.1 = (bf16[2048,128]{1,0:T(8,128)(2,1)}, bf16[2048,128]{1,0:T(8,128)(2,1)}) fusion(bf16[2,2048,128]{2,1,0:T(8,128)(2,1)} %collective-permute-done), kind=kLoop, calls=%fused_computation.12 | loop fusion | bytes 2097152 | tf_op jit(solution)/shard_map/squeeze | solution.py:185
  30.9 23.9 %shard_map.91 = bf16[2048,128]{1,0:T(8,128)(2,1)} custom-call(bf16[2048,128]{1,0:T(8,128)(2,1)} %q_ref.1, bf16[2048,128]{1,0:T(8,128)(2,1)} %get-tuple-element.8.kp_ref, bf16[2048,128]{1,0:T(8,128)(2,1)} %k_ref.1, bf16[2048,128]{1,0:T(8,128)(2,1)} %get-tuple-element.6.kn_ref, bf16[2048,128]{1,0:T(8,128)(2,1)} %get-tuple-element.7.vp_ref, ...), custom_call_target="tpu_custom_call" | custom-call | tf_op jit(solution)/shard_map/pallas_call | solution.py:115
  54.8 1.9 %copy.16 = bf16[2,8,128,128]{3,2,0,1:T(8,128)(2,1)} copy(bf16[2,8,128,128]{3,2,1,0:T(8,128)(2,1)} %bitcast.30) | data formatting | bytes 1048576 | tf_op jit(solution)/shard_map/reshape | solution.py:193
  56.7 16.5 %shard_map.92 = bf16[8,256,128]{2,1,0:T(8,128)(2,1)} custom-call(bf16[8,256,128]{2,1,0:T(8,128)(2,1)} %bitcast.33), custom_call_target="tpu_custom_call" | custom-call | tf_op jit(solution)/shard_map/pallas_call | solution.py:161
  73.2 1.2 %copy.17 = bf16[256,8,128]{0,2,1:T(8,128)(2,1)S(1)} copy(bf16[256,8,128]{2,0,1:T(8,128)(2,1)} %bitcast.34) | data formatting | bytes 1048576 | tf_op jit(solution)/shard_map/transpose | solution.py:196
  74.5 7.3 %collective-permute-start.3 = (bf16[256,1024]{0,1:T(8,128)(2,1)S(1)}, bf16[256,1024]{0,1:T(8,128)(2,1)S(1)}, u32[]{:S(2)}, u32[]{:S(2)}) collective-permute-start(bf16[256,1024]{0,1:T(8,128)(2,1)S(1)} %bitcast.27), channel_id=1, source_target_pairs={{0,16},{16,0},{32,48},{48,32},{64,80},{80,64},{96,112},{112,96},{1... | collective-permute-start | bytes 1572872 | tf_op jit(solution)/shard_map/ppermute | solution.py:197
  81.8 1.5 %collective-permute-done.3 = bf16[256,1024]{0,1:T(8,128)(2,1)S(1)} collective-permute-done((bf16[256,1024]{0,1:T(8,128)(2,1)S(1)}, bf16[256,1024]{0,1:T(8,128)(2,1)S(1)}, u32[]{:S(2)}, u32[]{:S(2)}) %collective-permute-start.3) | collective-permute-done | bytes 524320 | tf_op jit(solution)/shard_map/ppermute | solution.py:197
  83.3 0.0 all-gather.2.cloned.1.call-done
  83.3 2.5 %convolution_convert_fusion = bf16[128,1536]{1,0:T(8,128)(2,1)S(1)} fusion(bf16[1024,1536]{1,0:T(8,128)(2,1)} %all-gather.2.cloned.1.call-done, bf16[256,1024]{0,1:T(8,128)(2,1)S(1)} %collective-permute-done.3, s32[]{:T(128)S(6)} %select_n.35), kind=kOutput, calls=%fused_computation.2 | convolution fusion | flops 402849792 | bytes 3801092 | tf_op jit(solution)/shard_map/dot_general | solution.py:202
  85.8 1.2 %collective-permute-start.4 = (bf16[128,1536]{1,0:T(8,128)(2,1)S(1)}, bf16[128,1536]{1,0:T(8,128)(2,1)S(1)}, u32[]{:S(2)}, u32[]{:S(2)}) collective-permute-start(bf16[128,1536]{1,0:T(8,128)(2,1)S(1)} %convolution_convert_fusion), channel_id=1, source_target_pairs={{0,8},{8,0},{1,9},{9,1},{2,10},{10,2},{3,11},{11,3},{4,12},{12,4},... | collective-permute-start | bytes 1179656 | tf_op jit(solution)/shard_map/ppermute | solution.py:206
  87.0 0.0 copy-start.1
  87.0 2.6 %convolution_convert_fusion.1 = bf16[128,1536]{1,0:T(8,128)(2,1)S(1)} fusion(bf16[1024,1536]{1,0:T(8,128)(2,1)} %all-gather.2.cloned.1.call-done, bf16[256,1024]{0,1:T(8,128)(2,1)S(1)} %bitcast.28, s32[]{:T(128)S(6)} %select_n.35), kind=kOutput, calls=%fused_computation.3 | convolution fusion | flops 402849792 | bytes 3801092 | tf_op jit(solution)/shard_map/dot_general | solution.py:202
  89.6 0.5 collective-permute-start.2
  90.1 6.1 %collective-permute-done.4 = bf16[128,1536]{1,0:T(8,128)(2,1)S(1)} collective-permute-done((bf16[128,1536]{1,0:T(8,128)(2,1)S(1)}, bf16[128,1536]{1,0:T(8,128)(2,1)S(1)}, u32[]{:S(2)}, u32[]{:S(2)}) %collective-permute-start.4) | collective-permute-done | bytes 393248 | tf_op jit(solution)/shard_map/ppermute | solution.py:206
  96.2 0.0 copy-done.1
  96.2 0.6 fusion
  96.9 2.1 %collective-permute-start.5 = (bf16[128,1536]{1,0:T(8,128)(2,1)S(1)}, bf16[128,1536]{1,0:T(8,128)(2,1)S(1)}, u32[]{:S(2)}, u32[]{:S(2)}) collective-permute-start(bf16[128,1536]{1,0:T(8,128)(2,1)S(1)} %fusion), channel_id=1, source_target_pairs={{0,16},{16,0},{32,48},{48,32},{64,80},{80,64},{96,112},{112,96},{1... | collective-permute-start | bytes 1179656 | tf_op jit(solution)/shard_map/ppermute | solution.py:208
  98.9 5.7 %collective-permute-done.2 = bf16[128,1536]{1,0:T(8,128)(2,1)S(1)} collective-permute-done((bf16[128,1536]{1,0:T(8,128)(2,1)S(1)}, bf16[128,1536]{1,0:T(8,128)(2,1)S(1)}, u32[]{:S(2)}, u32[]{:S(2)}) %collective-permute-start.2) | collective-permute-done | bytes 393248 | tf_op jit(solution)/shard_map/ppermute | solution.py:205
  104.7 2.5 %add_convert_fusion = bf16[128,1536]{1,0:T(8,128)(2,1)S(1)} fusion(bf16[128,1536]{1,0:T(8,128)(2,1)S(1)} %collective-permute-done.2, bf16[1024,1536]{1,0:T(8,128)(2,1)} %all-gather.2.cloned.1.call-done, bf16[256,1024]{0,1:T(8,128)(2,1)S(1)} %bitcast.29, s32[]{:T(128)S(6)} %select_n.33), kind=kOutput, calls=%fused_computation.10 | convolution fusion | flops 403243008 | bytes 4194308 | tf_op jit(solution)/shard_map/dot_general | solution.py:202
  107.2 0.0 collective-permute-done.5
  107.2 1.1 maximum_select_fusion
  (3 shorter events, 0.0 us)
Async XLA Ops:
  6.5 1.1 copy-start
  6.5 8.9 %copy-start.5 = (pred[8,54,4]{1,2,0:T(4,128)(4,1)S(1)}, pred[8,54,4]{1,2,0:T(4,128)(4,1)}, u32[]{:S(2)}) copy-start(pred[8,54,4]{1,2,0:T(4,128)(4,1)} %constant.57) | copy-start | bytes 5188
  6.5 8.9 %copy-start.6 = (pred[8,54,4]{1,2,0:T(4,128)(4,1)S(1)}, pred[8,54,4]{1,2,0:T(4,128)(4,1)}, u32[]{:S(2)}) copy-start(pred[8,54,4]{1,2,0:T(4,128)(4,1)} %constant.59) | copy-start | bytes 5188
  6.5 8.9 %copy-start.4 = (bf16[8,45,54]{2,1,0:T(8,128)(2,1)S(1)}, bf16[8,45,54]{2,1,0:T(8,128)(2,1)}, u32[]{:S(2)}) copy-start(bf16[8,45,54]{2,1,0:T(8,128)(2,1)} %constant.78) | copy-start | bytes 116644
  6.5 9.2 %copy-start.2 = (s32[16,2,9,6]{3,2,1,0:T(8,128)S(1)}, s32[16,2,9,6]{3,2,1,0:T(8,128)}, u32[]{:S(2)}) copy-start(s32[16,2,9,6]{3,2,1,0:T(8,128)} %constant.52.clone) | copy-start | bytes 20740
  6.6 8.9 %copy-start.3 = (s32[1,1,32,45]{3,2,1,0:T(8,128)S(1)}, s32[1,1,32,45]{3,2,1,0:T(8,128)}, u32[]{:S(2)}) copy-start(s32[1,1,32,45]{3,2,1,0:T(8,128)} %param.12) | copy-start | bytes 17284
  6.6 76.7 %all-gather.2.cloned.1.call-start = ((), (), s32[]{:S(2)}) async-start(), calls=%async_computation | async-start | bytes 3538944 | tf_op jit(solution)/shard_map/all_gather | solution.py:192
  9.8 16.6 %collective-permute-start.1 = (bf16[2,2048,128]{2,1,0:T(8,128)(2,1)S(1)}, bf16[2,2048,128]{2,1,0:T(8,128)(2,1)}, u32[]{:S(2)}, u32[]{:S(2)}) collective-permute-start(bf16[2,2048,128]{2,1,0:T(8,128)(2,1)S(1)} %pad_maximum_fusion), channel_id=1, source_target_pairs={{16,0},{32,16},{48,32},{64,48},{80,64},{96,80},{112,96},{128,112},... | collective-permute-start | bytes 3145736 | tf_op jit(solution)/shard_map/ppermute | solution.py:182
  12.4 16.2 %collective-permute-start = (bf16[2,2048,128]{2,1,0:T(8,128)(2,1)S(1)}, bf16[2,2048,128]{2,1,0:T(8,128)(2,1)}, u32[]{:S(2)}, u32[]{:S(2)}) collective-permute-start(bf16[2,2048,128]{2,1,0:T(8,128)(2,1)S(1)} %pad_maximum_fusion), channel_id=1, source_target_pairs={{0,16},{16,32},{32,48},{48,64},{64,80},{80,96},{96,112},{112,128},... | collective-permute-start | bytes 3145736 | tf_op jit(solution)/shard_map/ppermute | solution.py:181
  74.5 8.8 %collective-permute-start.3 = (bf16[256,1024]{0,1:T(8,128)(2,1)S(1)}, bf16[256,1024]{0,1:T(8,128)(2,1)S(1)}, u32[]{:S(2)}, u32[]{:S(2)}) collective-permute-start(bf16[256,1024]{0,1:T(8,128)(2,1)S(1)} %bitcast.27), channel_id=1, source_target_pairs={{0,16},{16,0},{32,48},{48,32},{64,80},{80,64},{96,112},{112,96},{1... | collective-permute-start | bytes 1572872 | tf_op jit(solution)/shard_map/ppermute | solution.py:197
  85.8 10.4 %collective-permute-start.4 = (bf16[128,1536]{1,0:T(8,128)(2,1)S(1)}, bf16[128,1536]{1,0:T(8,128)(2,1)S(1)}, u32[]{:S(2)}, u32[]{:S(2)}) collective-permute-start(bf16[128,1536]{1,0:T(8,128)(2,1)S(1)} %convolution_convert_fusion), channel_id=1, source_target_pairs={{0,8},{8,0},{1,9},{9,1},{2,10},{10,2},{3,11},{11,3},{4,12},{12,4},... | collective-permute-start | bytes 1179656 | tf_op jit(solution)/shard_map/ppermute | solution.py:206
  87.0 9.2 %copy-start.1 = (bf16[1024,1536]{1,0:T(8,128)(2,1)S(1)}, bf16[1024,1536]{1,0:T(8,128)(2,1)}, u32[]{:S(2)}) copy-start(bf16[1024,1536]{1,0:T(8,128)(2,1)} %all-gather.2.cloned.1.call-done) | copy-start | bytes 9437188
  89.6 15.0 %collective-permute-start.2 = (bf16[128,1536]{1,0:T(8,128)(2,1)S(1)}, bf16[128,1536]{1,0:T(8,128)(2,1)S(1)}, u32[]{:S(2)}, u32[]{:S(2)}) collective-permute-start(bf16[128,1536]{1,0:T(8,128)(2,1)S(1)} %convolution_convert_fusion.1), channel_id=1, source_target_pairs={{0,8},{8,0},{1,9},{9,1},{2,10},{10,2},{3,11},{11,3},{4,12},{12,4},... | collective-permute-start | bytes 1179656 | tf_op jit(solution)/shard_map/ppermute | solution.py:205
  96.9 10.3 %collective-permute-start.5 = (bf16[128,1536]{1,0:T(8,128)(2,1)S(1)}, bf16[128,1536]{1,0:T(8,128)(2,1)S(1)}, u32[]{:S(2)}, u32[]{:S(2)}) collective-permute-start(bf16[128,1536]{1,0:T(8,128)(2,1)S(1)} %fusion), channel_id=1, source_target_pairs={{0,16},{16,0},{32,48},{48,32},{64,80},{80,64},{96,112},{112,96},{1... | collective-permute-start | bytes 1179656 | tf_op jit(solution)/shard_map/ppermute | solution.py:208
Sparse Core Ops, SparseCore 0:
  9.2 47.5 all-gather.1

commit v7 on v6

--- a/solution.py
+++ b/solution.py
@@ -177,9 +177,8 @@
     frame = lax.axis_index("frame") * frames_here
     forward = [(i, i + 1) for i in range(count - 1)]
     backward = [(t, s) for s, t in forward]
-    pair = jnp.stack([keys, values])
-    prev = lax.ppermute(pair, "frame", forward)
-    nxt = lax.ppermute(pair, "frame", backward)
+    prev = [lax.ppermute(x, "frame", forward) for x in (keys, values)]
+    nxt = [lax.ppermute(x, "frame", backward) for x in (keys, values)]
     mask_rows = block_mask.reshape(TROWS * TCOLS, WIN)
     bias = window_bias(mask_rows, frame, frames_total)
     attention = attend(queries, prev[0], keys, nxt[0], prev[1], values, nxt[1], bias)

time: 116 us -> 116 us (level)
  the two profiles are of different devices: /device:TPU:17 before, /device:TPU:6 now
where the time goes in v7:
time: 116 us; the launch traced here: 115 us
  Pallas kernels  41.3 us (36%)
  starting transfers between devices  23 us (20%)
  waiting for transfers between devices  18.2 us (16%)
  between operations  13.5 us (12%)
  matrix products  9.29 us (8%)
  local copies, waits for them, and re-layouts  6.88 us (6%)
  other arithmetic  2.82 us (2%)
    pallas_call x1, Pallas kernels, attend(): pl.pallas_call(attention_kernel, grid=(TROWS, GROUPS), in_specs=[pl.Block...  23.9 us
    pallas_call x1, Pallas kernels, exchange(): pl.pallas_call(exchange_kernel, out_shape=jax.ShapeDtypeStruct(x.shape, x...  17.4 us
    ppermute x1, starting transfers between devices, on_device(): theirs = lax.ppermute(mine, 'frame', partners)  9.51 us
    dot_general x4, matrix products, project(): return jnp.dot(rows, weight_half, preferred_element_type=jnp.float32)  8.24 us
    ppermute x1, waiting for transfers between devices, on_device(): lax.ppermute(project(theirs, 1 - side).astype(jnp.bfloat16), 'hy', flip)  7.17 us
    ppermute x1, waiting for transfers between devices, on_device(): lax.ppermute(project(mine, 1 - side).astype(jnp.bfloat16), 'hy', flip)  7.15 us
    ppermute x2, starting transfers between devices, on_device(): nxt = [lax.ppermute(x, 'frame', backward) for x in (keys, values)]  5.81 us
    ppermute x2, starting transfers between devices, on_device(): prev = [lax.ppermute(x, 'frame', forward) for x in (keys, values)]  5.32 us
  transfers between devices with their start and end apart: 9, of which 5 were waited for; matrix products, arithmetic and copies ran while one was open for 12% of the time, Pallas kernels for 36%

profile of v7, /device:TPU:6, one launch (start us, length us, event | category | flops | bytes accessed | tf_op | source)
XLA Modules:
  0.0 115.0 jit_solution(13657536443535718262)
XLA Ops:
  6.5 0.0 copy-start
  6.5 0.0 all-gather.2.cloned.1.call-start
  6.5 1.1 copy-done
  7.7 0.8 constant_dynamic-slice_fusion
  8.5 0.0 all-gather.2.cloned.1.call-update
  8.5 1.9 %collective-permute-start = (bf16[2048,128]{1,0:T(8,128)(2,1)}, bf16[2048,128]{1,0:T(8,128)(2,1)S(1)}, u32[]{:S(2)}, u32[]{:S(2)}) collective-permute-start(bf16[2048,128]{1,0:T(8,128)(2,1)} %k_ref.1), channel_id=1, source_target_pairs={{0,16},{16,32},{32,48},{48,64},{64,80},{80,96},{96,112},{112,128},... | collective-permute-start | bytes 1572872 | tf_op jit(solution)/shard_map/ppermute | solution.py:180
  10.4 3.6 %collective-permute-start.1 = (bf16[2048,128]{1,0:T(8,128)(2,1)}, bf16[2048,128]{1,0:T(8,128)(2,1)S(1)}, u32[]{:S(2)}, u32[]{:S(2)}) collective-permute-start(bf16[2048,128]{1,0:T(8,128)(2,1)} %k_ref.1), channel_id=1, source_target_pairs={{16,0},{32,16},{48,32},{64,48},{80,64},{96,80},{112,96},{128,112},... | collective-permute-start | bytes 1572872 | tf_op jit(solution)/shard_map/ppermute | solution.py:181
  14.1 3.4 %collective-permute-start.2 = (bf16[2048,128]{1,0:T(8,128)(2,1)}, bf16[2048,128]{1,0:T(8,128)(2,1)}, u32[]{:S(2)}, u32[]{:S(2)}) collective-permute-start(bf16[2048,128]{1,0:T(8,128)(2,1)} %v_ref.1), channel_id=1, source_target_pairs={{0,16},{16,32},{32,48},{48,64},{64,80},{80,96},{96,112},{112,128},... | collective-permute-start | bytes 1572872 | tf_op jit(solution)/shard_map/ppermute | solution.py:180
  17.5 2.2 %collective-permute-start.3 = (bf16[2048,128]{1,0:T(8,128)(2,1)}, bf16[2048,128]{1,0:T(8,128)(2,1)}, u32[]{:S(2)}, u32[]{:S(2)}) collective-permute-start(bf16[2048,128]{1,0:T(8,128)(2,1)} %v_ref.1), channel_id=1, source_target_pairs={{16,0},{32,16},{48,32},{64,48},{80,64},{96,80},{112,96},{128,112},... | collective-permute-start | bytes 1572872 | tf_op jit(solution)/shard_map/ppermute | solution.py:181
  19.6 0.7 convert_bitcast_fusion
  20.4 1.0 fusion.3
  21.4 0.1 reshape.27
  21.6 1.0 fusion.13
  22.6 0.4 broadcast_in_dim.16
  23.0 0.3 reshape.20
  23.3 1.0 copy.15.bias_ref
  24.3 0.0 collective-permute-done.kp_ref
  24.3 0.0 copy-start.2
  24.3 0.0 collective-permute-done.1.kn_ref
  24.3 0.0 copy-start.3
  24.3 0.6 collective-permute-done.2.vp_ref
  24.9 1.8 %collective-permute-done.3.vn_ref = bf16[2048,128]{1,0:T(8,128)(2,1)} collective-permute-done((bf16[2048,128]{1,0:T(8,128)(2,1)}, bf16[2048,128]{1,0:T(8,128)(2,1)}, u32[]{:S(2)}, u32[]{:S(2)}) %collective-permute-start.3) | collective-permute-done | bytes 524320 | tf_op jit(solution)/shard_map/ppermute | solution.py:181
  26.7 0.0 copy-done.2
  26.7 0.0 copy-done.3
  26.7 23.9 %shard_map.91 = bf16[2048,128]{1,0:T(8,128)(2,1)} custom-call(bf16[2048,128]{1,0:T(8,128)(2,1)} %q_ref.1, bf16[2048,128]{1,0:T(8,128)(2,1)} %copy-done.2, bf16[2048,128]{1,0:T(8,128)(2,1)} %k_ref.1, bf16[2048,128]{1,0:T(8,128)(2,1)} %copy-done.3, bf16[2048,128]{1,0:T(8,128)(2,1)} %collective-permute-done.2.vp_ref, bf16[2048,128]{1,0:T(8,128)(2,1)} %v_ref.1, ...), custom_call_target="tpu_custom_call" | custom-call | tf_op jit(solution)/shard_map/pallas_call | solution.py:115
  50.6 1.9 %copy.16 = bf16[2,8,128,128]{3,2,0,1:T(8,128)(2,1)} copy(bf16[2,8,128,128]{3,2,1,0:T(8,128)(2,1)} %bitcast.20) | data formatting | bytes 1048576 | tf_op jit(solution)/shard_map/reshape | solution.py:192
  52.4 17.4 %shard_map.92 = bf16[8,256,128]{2,1,0:T(8,128)(2,1)} custom-call(bf16[8,256,128]{2,1,0:T(8,128)(2,1)} %bitcast.21), custom_call_target="tpu_custom_call" | custom-call | tf_op jit(solution)/shard_map/pallas_call | solution.py:161
  69.9 1.2 %copy.17 = bf16[256,8,128]{0,2,1:T(8,128)(2,1)S(1)} copy(bf16[256,8,128]{2,0,1:T(8,128)(2,1)} %bitcast.22) | data formatting | bytes 1048576 | tf_op jit(solution)/shard_map/transpose | solution.py:195
  71.1 9.5 %collective-permute-start.5 = (bf16[256,1024]{0,1:T(8,128)(2,1)S(1)}, bf16[256,1024]{0,1:T(8,128)(2,1)S(1)}, u32[]{:S(2)}, u32[]{:S(2)}) collective-permute-start(bf16[256,1024]{0,1:T(8,128)(2,1)S(1)} %bitcast.17), channel_id=1, source_target_pairs={{0,16},{16,0},{32,48},{48,32},{64,80},{80,64},{96,112},{112,96},{1... | collective-permute-start | bytes 1572872 | tf_op jit(solution)/shard_map/ppermute | solution.py:196
  80.6 1.5 %collective-permute-done.5 = bf16[256,1024]{0,1:T(8,128)(2,1)S(1)} collective-permute-done((bf16[256,1024]{0,1:T(8,128)(2,1)S(1)}, bf16[256,1024]{0,1:T(8,128)(2,1)S(1)}, u32[]{:S(2)}, u32[]{:S(2)}) %collective-permute-start.5) | collective-permute-done | bytes 524320 | tf_op jit(solution)/shard_map/ppermute | solution.py:196
  82.2 0.0 all-gather.2.cloned.1.call-done
  82.2 2.5 %convolution_convert_fusion = bf16[128,1536]{1,0:T(8,128)(2,1)S(1)} fusion(bf16[1024,1536]{1,0:T(8,128)(2,1)} %all-gather.2.cloned.1.call-done, bf16[256,1024]{0,1:T(8,128)(2,1)S(1)} %collective-permute-done.5, s32[]{:T(128)S(6)} %select_n.35), kind=kOutput, calls=%fused_computation.2 | convolution fusion | flops 402849792 | bytes 3801092 | tf_op jit(solution)/shard_map/dot_general | solution.py:201
  84.7 0.8 collective-permute-start.6
  85.5 0.0 copy-start.1
  85.5 2.6 %convolution_convert_fusion.1 = bf16[128,1536]{1,0:T(8,128)(2,1)S(1)} fusion(bf16[1024,1536]{1,0:T(8,128)(2,1)} %all-gather.2.cloned.1.call-done, bf16[256,1024]{0,1:T(8,128)(2,1)S(1)} %bitcast.18, s32[]{:T(128)S(6)} %select_n.35), kind=kOutput, calls=%fused_computation.3 | convolution fusion | flops 402849792 | bytes 3801092 | tf_op jit(solution)/shard_map/dot_general | solution.py:201
  88.1 1.4 %collective-permute-start.4 = (bf16[128,1536]{1,0:T(8,128)(2,1)S(1)}, bf16[128,1536]{1,0:T(8,128)(2,1)S(1)}, u32[]{:S(2)}, u32[]{:S(2)}) collective-permute-start(bf16[128,1536]{1,0:T(8,128)(2,1)S(1)} %convolution_convert_fusion.1), channel_id=1, source_target_pairs={{0,8},{8,0},{1,9},{9,1},{2,10},{10,2},{3,11},{11,3},{4,12},{12,4},... | collective-permute-start | bytes 1179656 | tf_op jit(solution)/shard_map/ppermute | solution.py:204
  89.5 7.2 %collective-permute-done.6 = bf16[128,1536]{1,0:T(8,128)(2,1)S(1)} collective-permute-done((bf16[128,1536]{1,0:T(8,128)(2,1)S(1)}, bf16[128,1536]{1,0:T(8,128)(2,1)S(1)}, u32[]{:S(2)}, u32[]{:S(2)}) %collective-permute-start.6) | collective-permute-done | bytes 393248 | tf_op jit(solution)/shard_map/ppermute | solution.py:205
  96.7 0.0 copy-done.1
  96.7 0.6 fusion
  97.3 0.1 collective-permute-start.7
  97.4 7.1 %collective-permute-done.4 = bf16[128,1536]{1,0:T(8,128)(2,1)S(1)} collective-permute-done((bf16[128,1536]{1,0:T(8,128)(2,1)S(1)}, bf16[128,1536]{1,0:T(8,128)(2,1)S(1)}, u32[]{:S(2)}, u32[]{:S(2)}) %collective-permute-start.4) | collective-permute-done | bytes 393248 | tf_op jit(solution)/shard_map/ppermute | solution.py:204
  104.6 2.5 %add_convert_fusion = bf16[128,1536]{1,0:T(8,128)(2,1)S(1)} fusion(bf16[128,1536]{1,0:T(8,128)(2,1)S(1)} %collective-permute-done.4, bf16[1024,1536]{1,0:T(8,128)(2,1)} %all-gather.2.cloned.1.call-done, bf16[256,1024]{0,1:T(8,128)(2,1)S(1)} %bitcast.19, s32[]{:T(128)S(6)} %select_n.33), kind=kOutput, calls=%fused_computation.9 | convolution fusion | flops 403243008 | bytes 4194308 | tf_op jit(solution)/shard_map/dot_general | solution.py:201
  107.1 0.0 collective-permute-done.7
  107.1 1.1 maximum_select_fusion
  (2 shorter events, 0.0 us)
Async XLA Ops:
  6.5 1.1 copy-start
  6.5 75.6 %all-gather.2.cloned.1.call-start = ((), (), s32[]{:S(2)}) async-start(), calls=%async_computation | async-start | bytes 3538944 | tf_op jit(solution)/shard_map/all_gather | solution.py:191
  8.5 15.8 %collective-permute-start = (bf16[2048,128]{1,0:T(8,128)(2,1)}, bf16[2048,128]{1,0:T(8,128)(2,1)S(1)}, u32[]{:S(2)}, u32[]{:S(2)}) collective-permute-start(bf16[2048,128]{1,0:T(8,128)(2,1)} %k_ref.1), channel_id=1, source_target_pairs={{0,16},{16,32},{32,48},{48,64},{64,80},{80,96},{96,112},{112,128},... | collective-permute-start | bytes 1572872 | tf_op jit(solution)/shard_map/ppermute | solution.py:180
  10.4 13.9 %collective-permute-start.1 = (bf16[2048,128]{1,0:T(8,128)(2,1)}, bf16[2048,128]{1,0:T(8,128)(2,1)S(1)}, u32[]{:S(2)}, u32[]{:S(2)}) collective-permute-start(bf16[2048,128]{1,0:T(8,128)(2,1)} %k_ref.1), channel_id=1, source_target_pairs={{16,0},{32,16},{48,32},{64,48},{80,64},{96,80},{112,96},{128,112},... | collective-permute-start | bytes 1572872 | tf_op jit(solution)/shard_map/ppermute | solution.py:181
  14.1 10.9 %collective-permute-start.2 = (bf16[2048,128]{1,0:T(8,128)(2,1)}, bf16[2048,128]{1,0:T(8,128)(2,1)}, u32[]{:S(2)}, u32[]{:S(2)}) collective-permute-start(bf16[2048,128]{1,0:T(8,128)(2,1)} %v_ref.1), channel_id=1, source_target_pairs={{0,16},{16,32},{32,48},{48,64},{64,80},{80,96},{96,112},{112,128},... | collective-permute-start | bytes 1572872 | tf_op jit(solution)/shard_map/ppermute | solution.py:180
  17.5 9.2 %collective-permute-start.3 = (bf16[2048,128]{1,0:T(8,128)(2,1)}, bf16[2048,128]{1,0:T(8,128)(2,1)}, u32[]{:S(2)}, u32[]{:S(2)}) collective-permute-start(bf16[2048,128]{1,0:T(8,128)(2,1)} %v_ref.1), channel_id=1, source_target_pairs={{16,0},{32,16},{48,32},{64,48},{80,64},{96,80},{112,96},{128,112},... | collective-permute-start | bytes 1572872 | tf_op jit(solution)/shard_map/ppermute | solution.py:181
  24.3 2.4 %copy-start.2 = (bf16[2048,128]{1,0:T(8,128)(2,1)}, bf16[2048,128]{1,0:T(8,128)(2,1)S(1)}, u32[]{:S(2)}) copy-start(bf16[2048,128]{1,0:T(8,128)(2,1)S(1)} %collective-permute-done.kp_ref) | copy-start | bytes 1572868
  24.3 2.4 %copy-start.3 = (bf16[2048,128]{1,0:T(8,128)(2,1)}, bf16[2048,128]{1,0:T(8,128)(2,1)S(1)}, u32[]{:S(2)}) copy-start(bf16[2048,128]{1,0:T(8,128)(2,1)S(1)} %collective-permute-done.1.kn_ref) | copy-start | bytes 1572868
  71.1 11.1 %collective-permute-start.5 = (bf16[256,1024]{0,1:T(8,128)(2,1)S(1)}, bf16[256,1024]{0,1:T(8,128)(2,1)S(1)}, u32[]{:S(2)}, u32[]{:S(2)}) collective-permute-start(bf16[256,1024]{0,1:T(8,128)(2,1)S(1)} %bitcast.17), channel_id=1, source_target_pairs={{0,16},{16,0},{32,48},{48,32},{64,80},{80,64},{96,112},{112,96},{1... | collective-permute-start | bytes 1572872 | tf_op jit(solution)/shard_map/ppermute | solution.py:196
  84.7 12.0 %collective-permute-start.6 = (bf16[128,1536]{1,0:T(8,128)(2,1)S(1)}, bf16[128,1536]{1,0:T(8,128)(2,1)S(1)}, u32[]{:S(2)}, u32[]{:S(2)}) collective-permute-start(bf16[128,1536]{1,0:T(8,128)(2,1)S(1)} %convolution_convert_fusion), channel_id=1, source_target_pairs={{0,8},{8,0},{1,9},{9,1},{2,10},{10,2},{3,11},{11,3},{4,12},{12,4},... | collective-permute-start | bytes 1179656 | tf_op jit(solution)/shard_map/ppermute | solution.py:205
  85.5 11.3 %copy-start.1 = (bf16[1024,1536]{1,0:T(8,128)(2,1)S(1)}, bf16[1024,1536]{1,0:T(8,128)(2,1)}, u32[]{:S(2)}) copy-start(bf16[1024,1536]{1,0:T(8,128)(2,1)} %all-gather.2.cloned.1.call-done) | copy-start | bytes 9437188
  88.1 16.5 %collective-permute-start.4 = (bf16[128,1536]{1,0:T(8,128)(2,1)S(1)}, bf16[128,1536]{1,0:T(8,128)(2,1)S(1)}, u32[]{:S(2)}, u32[]{:S(2)}) collective-permute-start(bf16[128,1536]{1,0:T(8,128)(2,1)S(1)} %convolution_convert_fusion.1), channel_id=1, source_target_pairs={{0,8},{8,0},{1,9},{9,1},{2,10},{10,2},{3,11},{11,3},{4,12},{12,4},... | collective-permute-start | bytes 1179656 | tf_op jit(solution)/shard_map/ppermute | solution.py:204
  97.3 9.8 %collective-permute-start.7 = (bf16[128,1536]{1,0:T(8,128)(2,1)S(1)}, bf16[128,1536]{1,0:T(8,128)(2,1)S(1)}, u32[]{:S(2)}, u32[]{:S(2)}) collective-permute-start(bf16[128,1536]{1,0:T(8,128)(2,1)S(1)} %fusion), channel_id=1, source_target_pairs={{0,16},{16,0},{32,48},{48,32},{64,80},{80,64},{96,112},{112,96},{1... | collective-permute-start | bytes 1179656 | tf_op jit(solution)/shard_map/ppermute | solution.py:207
Sparse Core Ops, SparseCore 0:
  9.1 47.8 all-gather.1

commit v8 on v7

--- a/solution.py
+++ b/solution.py
@@ -1,3 +1,4 @@
+import functools
 import math
 
 import numpy as np
@@ -74,9 +75,9 @@
     return bias.reshape(TROWS * GROUPS, QTILES, ROW_K)
 
 
-def attention_kernel(q_ref, kp_ref, k_ref, kn_ref, vp_ref, v_ref, vn_ref, bias_ref, o_ref,
+def attention_kernel(first, q_ref, kp_ref, k_ref, kn_ref, vp_ref, v_ref, vn_ref, bias_ref, o_ref,
                      s_ref, p_ref):
-    row = pl.program_id(0)
+    row = half_base(first) + pl.program_id(0)
     group = pl.program_id(1)
     start = jnp.clip(QTILES * group - 2, 0, TCOLS - KCOLS) * TILE
     key_refs = (kp_ref, k_ref, kn_ref)
@@ -109,17 +110,23 @@
     o_ref[...] = acc.astype(o_ref.dtype)
 
 
-def attend(q, kp, k, kn, vp, v, vn, bias):
-    tokens = q.shape[0]
+def half_base(first):
+    side = lax.axis_index("hy")
+    owner = 1 - side if first else side
+    return owner * (TROWS // 2)
+
+
+def attend(first, q, kp, k, kn, vp, v, vn, bias):
+    tokens = k.shape[0]
     full = pl.BlockSpec((tokens, HEAD_DIM), lambda r, g: (0, 0))
     return pl.pallas_call(
-        attention_kernel,
-        grid=(TROWS, GROUPS),
+        functools.partial(attention_kernel, first),
+        grid=(TROWS // 2, GROUPS),
         in_specs=[pl.BlockSpec((BLOCK_Q, HEAD_DIM), lambda r, g: (r * GROUPS + g, 0))]
         + [full] * 6
         + [pl.BlockSpec((1, QTILES, ROW_K), lambda r, g: (r * GROUPS + g, 0, 0))],
         out_specs=pl.BlockSpec((BLOCK_Q, HEAD_DIM), lambda r, g: (r * GROUPS + g, 0)),
-        out_shape=jax.ShapeDtypeStruct((tokens, HEAD_DIM), jnp.bfloat16),
+        out_shape=jax.ShapeDtypeStruct((tokens // 2, HEAD_DIM), jnp.bfloat16),
         scratch_shapes=[
             pltpu.VMEM((BLOCK_Q, ROW_K), jnp.float32),
             pltpu.VMEM((BLOCK_Q, ROW_K), jnp.bfloat16),
@@ -156,7 +163,7 @@
         copy.wait()
 
 
-def exchange(x):
+def exchange(x, channel):
     peers = x.shape[0]
     return pl.pallas_call(
         exchange_kernel,
@@ -164,7 +171,7 @@
         in_specs=[pl.BlockSpec(memory_space=pltpu.VMEM)],
         out_specs=pl.BlockSpec(memory_space=pltpu.VMEM),
         scratch_shapes=[pltpu.SemaphoreType.DMA((peers,)), pltpu.SemaphoreType.DMA((peers,))],
-        compiler_params=pltpu.CompilerParams(collective_id=0, has_side_effects=True),
+        compiler_params=pltpu.CompilerParams(collective_id=channel, has_side_effects=True),
     )(x)
 
 
@@ -181,31 +188,36 @@
     nxt = [lax.ppermute(x, "frame", backward) for x in (keys, values)]
     mask_rows = block_mask.reshape(TROWS * TCOLS, WIN)
     bias = window_bias(mask_rows, frame, frames_total)
-    attention = attend(queries, prev[0], keys, nxt[0], prev[1], values, nxt[1], bias)
     core = lax.axis_index("frame") % 2
     side = lax.axis_index("hy")
-    sides = lax.axis_size("hy")
     half = out_weight.shape[1] // 2
     partners = [(i, i ^ 1) for i in range(count)]
+    flip = [(0, 1), (1, 0)]
     weight_half = lax.dynamic_slice_in_dim(out_weight, core * half, half, axis=1)
     weight_half = lax.all_gather(weight_half, "hz", axis=0, tiled=True)
-    chunks = attention.reshape(sides, -1, tok_dev // (sides * lax.axis_size("hz")), HEAD_DIM)
     peers = lax.axis_size("hz")
-    chunks = chunks.transpose(1, 0, 2, 3).reshape(peers, tok_dev // peers, HEAD_DIM)
-    mine = exchange(chunks).transpose(1, 0, 2).reshape(tok_dev // peers, peers * HEAD_DIM)
-    theirs = lax.ppermute(mine, "frame", partners)
-    block = mine.shape[0] // sides
-
-    def project(x, which):
-        rows = lax.dynamic_slice_in_dim(x, which * block, block, axis=0)
-        return jnp.dot(rows, weight_half, preferred_element_type=jnp.float32)
-
-    flip = [(0, 1), (1, 0)]
-    sent_mine = lax.ppermute(project(mine, 1 - side).astype(jnp.bfloat16), "hy", flip)
-    sent_theirs = lax.ppermute(project(theirs, 1 - side).astype(jnp.bfloat16), "hy", flip)
-    other = (project(theirs, side) + sent_theirs.astype(jnp.float32)).astype(jnp.bfloat16)
+    rows = tok_dev // 2
+    bias_rows = bias.shape[0] // 2
+
+    def half_attention(first):
+        base = half_base(first)
+        q = lax.dynamic_slice_in_dim(queries, base * (rows // 2), rows, axis=0)
+        b = lax.dynamic_slice_in_dim(bias, base * (bias_rows // 2), bias_rows, axis=0)
+        out = attend(first, q, prev[0], keys, nxt[0], prev[1], values, nxt[1], b)
+        got = exchange(out.reshape(peers, rows // peers, HEAD_DIM), 1 if first else 2)
+        mine = got.transpose(1, 0, 2).reshape(rows // peers, peers * HEAD_DIM)
+        theirs = lax.ppermute(mine, "frame", partners)
+        return mine, theirs
+
+    project = lambda x: jnp.dot(x, weight_half, preferred_element_type=jnp.float32)
+    mine, theirs = half_attention(True)
+    partials = jnp.stack([project(mine), project(theirs)]).astype(jnp.bfloat16)
+    partials, queries = lax.optimization_barrier((partials, queries))
+    sent_mine, sent_theirs = lax.ppermute(partials, "hy", flip)
+    mine, theirs = half_attention(False)
+    other = (project(theirs) + sent_theirs.astype(jnp.float32)).astype(jnp.bfloat16)
     other_half = lax.ppermute(other, "frame", partners)
-    own_half = (project(mine, side) + sent_mine.astype(jnp.float32)).astype(jnp.bfloat16)
+    own_half = (project(mine) + sent_mine.astype(jnp.float32)).astype(jnp.bfloat16)
     return jnp.where(
         core == 0,
         jnp.concatenate([own_half, other_half], axis=1),

time: 116 us -> 115 us (level)
  the two profiles are of different devices: /device:TPU:6 before, /device:TPU:17 now
where the time goes in v8:
time: 115 us
  Pallas kernels  55.6 us (48%)
  starting transfers between devices  19.9 us (17%)
  between operations  13.6 us (12%)
  local copies, waits for them, and re-layouts  12.1 us (11%)
  matrix products  9.29 us (8%)
  other arithmetic  2.89 us (3%)
  waiting for transfers between devices  1.2 us (1%)
    pallas_call x2, Pallas kernels, exchange(): pl.pallas_call(exchange_kernel, out_shape=jax.ShapeDtypeStruct(x.shape, x...  29.2 us
    pallas_call x2, Pallas kernels, attend(): pl.pallas_call(functools.partial(attention_kernel, first), grid=(TROWS //...  26.4 us
    dot_general x4, matrix products, on_device(): jnp.dot(x, weight_half, preferred_element_type=jnp.float32)  8.23 us
    ppermute x2, starting transfers between devices, on_device(): prev = [lax.ppermute(x, 'frame', forward) for x in (keys, values)]  7.33 us
    ppermute x2, starting transfers between devices, on_device(): nxt = [lax.ppermute(x, 'frame', backward) for x in (keys, values)]  6.36 us
    ppermute x2, starting transfers between devices, half_attention(): theirs = lax.ppermute(mine, 'frame', partners)  4.78 us
    unnamed x14, local copies, waits for them, and re-layouts  4.01 us
    dynamic_slice x2, local copies, waits for them, and re-layouts, half_attention(): q = lax.dynamic_slice_in_dim(queries, base * (rows // 2), rows, axis=0)  2.42 us
  transfers between devices with their start and end apart: 9, of which 1 were waited for; matrix products, arithmetic and copies ran while one was open for 15% of the time, Pallas kernels for 49%

profile of v8, /device:TPU:17, one launch (start us, length us, event | category | flops | bytes accessed | tf_op | source)
XLA Modules:
  0.0 114.6 jit_solution(791004986937284775)
XLA Ops:
  6.5 0.0 copy-start
  6.5 0.0 all-gather.2.cloned.1.call-start
  6.5 1.1 copy-done
  7.7 0.8 constant_dynamic-slice_fusion.2
  8.4 0.0 all-gather.2.cloned.1.call-update
  8.5 3.7 %collective-permute-start = (bf16[2048,128]{1,0:T(8,128)(2,1)}, bf16[2048,128]{1,0:T(8,128)(2,1)S(1)}, u32[]{:S(2)}, u32[]{:S(2)}) collective-permute-start(bf16[2048,128]{1,0:T(8,128)(2,1)} %k_ref.3), channel_id=1, source_target_pairs={{0,16},{16,32},{32,48},{48,64},{64,80},{80,96},{96,112},{112,128},... | collective-permute-start | bytes 1572872 | tf_op jit(solution)/shard_map/ppermute | solution.py:187
  12.1 1.9 %collective-permute-start.1 = (bf16[2048,128]{1,0:T(8,128)(2,1)}, bf16[2048,128]{1,0:T(8,128)(2,1)S(1)}, u32[]{:S(2)}, u32[]{:S(2)}) collective-permute-start(bf16[2048,128]{1,0:T(8,128)(2,1)} %k_ref.3), channel_id=1, source_target_pairs={{16,0},{32,16},{48,32},{64,48},{80,64},{96,80},{112,96},{128,112},... | collective-permute-start | bytes 1572872 | tf_op jit(solution)/shard_map/ppermute | solution.py:188
  14.1 3.6 %collective-permute-start.2 = (bf16[2048,128]{1,0:T(8,128)(2,1)}, bf16[2048,128]{1,0:T(8,128)(2,1)S(1)}, u32[]{:S(2)}, u32[]{:S(2)}) collective-permute-start(bf16[2048,128]{1,0:T(8,128)(2,1)} %v_ref.3), channel_id=1, source_target_pairs={{0,16},{16,32},{32,48},{48,64},{64,80},{80,96},{96,112},{112,128},... | collective-permute-start | bytes 1572872 | tf_op jit(solution)/shard_map/ppermute | solution.py:187
  17.7 4.4 %collective-permute-start.3 = (bf16[2048,128]{1,0:T(8,128)(2,1)}, bf16[2048,128]{1,0:T(8,128)(2,1)}, u32[]{:S(2)}, u32[]{:S(2)}) collective-permute-start(bf16[2048,128]{1,0:T(8,128)(2,1)} %v_ref.3), channel_id=1, source_target_pairs={{16,0},{32,16},{48,32},{64,48},{80,64},{96,80},{112,96},{128,112},... | collective-permute-start | bytes 1572872 | tf_op jit(solution)/shard_map/ppermute | solution.py:188
  22.2 0.7 convert_bitcast_fusion
  22.9 1.1 fusion.5
  24.0 0.1 reshape.37
  24.1 1.0 fusion.9
  25.2 0.4 broadcast_in_dim.16
  25.6 1.1 reshape.27
  26.6 1.1 constant_dynamic-slice_fusion
  27.7 0.8 copy.18.bias_ref
  28.5 1.7 %constant_dynamic-slice_fusion.4.q_ref = bf16[1024,128]{1,0:T(8,128)(2,1)} fusion(bf16[2048,128]{1,0:T(8,128)(2,1)} %param.9, s32[]{:T(128)S(6)} %select_n.36), kind=kLoop, calls=%fused_computation.27 | loop fusion | bytes 524292 | tf_op jit(solution)/shard_map/dynamic_slice | solution.py:204
  30.2 0.0 collective-permute-done.kp_ref
  30.2 0.0 copy-start.2
  30.2 0.0 collective-permute-done.1.kn_ref
  30.2 0.0 copy-start.3
  30.2 0.0 collective-permute-done.2.vp_ref
  30.2 0.0 copy-start.4
  30.2 0.0 collective-permute-done.3.vn_ref
  30.2 0.7 copy-done.2
  31.0 0.2 copy-done.3
  31.2 0.2 copy-done.4
  31.3 13.2 %shard_map.91 = bf16[1024,128]{1,0:T(8,128)(2,1)} custom-call(bf16[1024,128]{1,0:T(8,128)(2,1)} %constant_dynamic-slice_fusion.4.q_ref, bf16[2048,128]{1,0:T(8,128)(2,1)} %copy-done.2, bf16[2048,128]{1,0:T(8,128)(2,1)} %k_ref.3, bf16[2048,128]{1,0:T(8,128)(2,1)} %copy-done.3, bf16[2048,128]{1,0:T(8,128)(2,1)} %copy-done.4, bf16[2048,128]{1,0:T(8,128)(2,1)} %v_ref.3, ...), custom_call_target="tpu_custom_call" | custom-call | tf_op jit(solution)/shard_map/pallas_call | solution.py:122
  44.6 16.1 %shard_map.92 = bf16[8,128,128]{2,1,0:T(8,128)(2,1)} custom-call(bf16[8,128,128]{2,1,0:T(8,128)(2,1)} %bitcast.42), custom_call_target="tpu_custom_call" | custom-call | tf_op jit(solution)/shard_map/pallas_call | solution.py:168
  60.6 1.1 copy.15
  61.8 4.0 %collective-permute-start.4 = (bf16[128,1024]{0,1:T(8,128)(2,1)S(1)}, bf16[128,1024]{0,1:T(8,128)(2,1)S(1)}, u32[]{:S(2)}, u32[]{:S(2)}) collective-permute-start(bf16[128,1024]{0,1:T(8,128)(2,1)S(1)} %bitcast.39), channel_id=1, source_target_pairs={{0,16},{16,0},{32,48},{48,32},{64,80},{80,64},{96,112},{112,96},{1... | collective-permute-start | bytes 786440 | tf_op jit(solution)/shard_map/ppermute | solution.py:209
  65.7 0.0 all-gather.2.cloned.1.call-done
  65.7 0.0 copy-start.1
  65.7 2.6 %fusion.1 = bf16[1,128,1536]{2,1,0:T(8,128)(2,1)S(1)} fusion(bf16[128,1024]{0,1:T(8,128)(2,1)S(1)} %bitcast.40, bf16[1024,1536]{1,0:T(8,128)(2,1)} %all-gather.2.cloned.1.call-done), kind=kOutput, calls=%fused_computation.4 | convolution fusion | flops 402849792 | bytes 3801088 | tf_op jit(solution)/shard_map/dot_general | solution.py:212
  68.4 0.0 copy-start.5
  68.4 0.0 collective-permute-done.4
  68.4 0.2 copy-done.1
  68.6 0.6 fusion.2
  69.2 0.1 pad_maximum_fusion
  69.3 1.0 collective-permute-start.5
  70.3 0.8 copy.19.bias_ref
  71.1 0.0 copy-done.5
  71.1 0.7 constant_dynamic-slice_fusion.1.q_ref
  71.8 13.2 %shard_map.93 = bf16[1024,128]{1,0:T(8,128)(2,1)} custom-call(bf16[1024,128]{1,0:T(8,128)(2,1)} %constant_dynamic-slice_fusion.1.q_ref, bf16[2048,128]{1,0:T(8,128)(2,1)} %copy-done.2, bf16[2048,128]{1,0:T(8,128)(2,1)} %k_ref.3, bf16[2048,128]{1,0:T(8,128)(2,1)} %copy-done.3, bf16[2048,128]{1,0:T(8,128)(2,1)} %copy-done.4, bf16[2048,128]{1,0:T(8,128)(2,1)} %v_ref.3, ...), custom_call_target="tpu_custom_call" | custom-call | tf_op jit(solution)/shard_map/pallas_call | solution.py:122
  85.0 13.1 %shard_map.94 = bf16[8,128,128]{2,1,0:T(8,128)(2,1)} custom-call(bf16[8,128,128]{2,1,0:T(8,128)(2,1)} %bitcast.41), custom_call_target="tpu_custom_call" | custom-call | tf_op jit(solution)/shard_map/pallas_call | solution.py:168
  98.1 1.1 copy.17
  99.3 0.8 collective-permute-start.6
  100.1 1.2 %collective-permute-done.6 = bf16[128,1024]{0,1:T(8,128)(2,1)S(1)} collective-permute-done((bf16[128,1024]{0,1:T(8,128)(2,1)S(1)}, bf16[128,1024]{0,1:T(8,128)(2,1)S(1)}, u32[]{:S(2)}, u32[]{:S(2)}) %collective-permute-start.6) | collective-permute-done | bytes 262176 | tf_op jit(solution)/shard_map/ppermute | solution.py:209
  101.2 0.0 collective-permute-done.5
  101.2 2.5 %fusion = bf16[128,1536]{1,0:T(8,128)(2,1)S(1)} fusion(bf16[128,1024]{0,1:T(8,128)(2,1)S(1)} %collective-permute-done.6, bf16[1024,1536]{1,0:T(8,128)(2,1)} %all-gather.2.cloned.1.call-done, bf16[2,128,1536]{2,1,0:T(8,128)(2,1)S(1)} %collective-permute-done.5), kind=kOutput, calls=%fused_computation.1 | convolution fusion | flops 403243008 | bytes 4194304 | tf_op jit(solution)/shard_map/dot_general | solution.py:212
  103.7 0.5 collective-permute-start.7
  104.2 2.5 %fusion.6 = bf16[128,1536]{1,0:T(8,128)(2,1)S(1)} fusion(bf16[2,128,1536]{2,1,0:T(8,128)(2,1)S(1)} %collective-permute-done.5, bf16[128,1024]{0,1:T(8,128)(2,1)S(1)} %bitcast.36, bf16[1024,1536]{1,0:T(8,128)(2,1)} %all-gather.2.cloned.1.call-done), kind=kOutput, calls=%fused_computation.13 | convolution fusion | flops 403243008 | bytes 4194304 | tf_op jit(solution)/shard_map/dot_general | solution.py:212
  106.7 0.0 collective-permute-done.7
  106.7 1.1 maximum_select_fusion
  (2 shorter events, 0.0 us)
Async XLA Ops:
  6.5 1.1 copy-start
  6.5 59.2 %all-gather.2.cloned.1.call-start = ((), (), s32[]{:S(2)}) async-start(), calls=%async_computation | async-start | bytes 3538944 | tf_op jit(solution)/shard_map/all_gather | solution.py:197
  8.5 21.7 %collective-permute-start = (bf16[2048,128]{1,0:T(8,128)(2,1)}, bf16[2048,128]{1,0:T(8,128)(2,1)S(1)}, u32[]{:S(2)}, u32[]{:S(2)}) collective-permute-start(bf16[2048,128]{1,0:T(8,128)(2,1)} %k_ref.3), channel_id=1, source_target_pairs={{0,16},{16,32},{32,48},{48,64},{64,80},{80,96},{96,112},{112,128},... | collective-permute-start | bytes 1572872 | tf_op jit(solution)/shard_map/ppermute | solution.py:187
  12.1 18.1 %collective-permute-start.1 = (bf16[2048,128]{1,0:T(8,128)(2,1)}, bf16[2048,128]{1,0:T(8,128)(2,1)S(1)}, u32[]{:S(2)}, u32[]{:S(2)}) collective-permute-start(bf16[2048,128]{1,0:T(8,128)(2,1)} %k_ref.3), channel_id=1, source_target_pairs={{16,0},{32,16},{48,32},{64,48},{80,64},{96,80},{112,96},{128,112},... | collective-permute-start | bytes 1572872 | tf_op jit(solution)/shard_map/ppermute | solution.py:188
  14.1 16.1 %collective-permute-start.2 = (bf16[2048,128]{1,0:T(8,128)(2,1)}, bf16[2048,128]{1,0:T(8,128)(2,1)S(1)}, u32[]{:S(2)}, u32[]{:S(2)}) collective-permute-start(bf16[2048,128]{1,0:T(8,128)(2,1)} %v_ref.3), channel_id=1, source_target_pairs={{0,16},{16,32},{32,48},{48,64},{64,80},{80,96},{96,112},{112,128},... | collective-permute-start | bytes 1572872 | tf_op jit(solution)/shard_map/ppermute | solution.py:187
  17.7 12.5 %collective-permute-start.3 = (bf16[2048,128]{1,0:T(8,128)(2,1)}, bf16[2048,128]{1,0:T(8,128)(2,1)}, u32[]{:S(2)}, u32[]{:S(2)}) collective-permute-start(bf16[2048,128]{1,0:T(8,128)(2,1)} %v_ref.3), channel_id=1, source_target_pairs={{16,0},{32,16},{48,32},{64,48},{80,64},{96,80},{112,96},{128,112},... | collective-permute-start | bytes 1572872 | tf_op jit(solution)/shard_map/ppermute | solution.py:188
  30.2 0.8 copy-start.2
  30.2 1.0 copy-start.3
  30.2 1.1 copy-start.4
  61.8 6.6 %collective-permute-start.4 = (bf16[128,1024]{0,1:T(8,128)(2,1)S(1)}, bf16[128,1024]{0,1:T(8,128)(2,1)S(1)}, u32[]{:S(2)}, u32[]{:S(2)}) collective-permute-start(bf16[128,1024]{0,1:T(8,128)(2,1)S(1)} %bitcast.39), channel_id=1, source_target_pairs={{0,16},{16,0},{32,48},{48,32},{64,80},{80,64},{96,112},{112,96},{1... | collective-permute-start | bytes 786440 | tf_op jit(solution)/shard_map/ppermute | solution.py:209
  65.7 2.8 %copy-start.1 = (bf16[1024,1536]{1,0:T(8,128)(2,1)S(1)}, bf16[1024,1536]{1,0:T(8,128)(2,1)}, u32[]{:S(2)}) copy-start(bf16[1024,1536]{1,0:T(8,128)(2,1)} %all-gather.2.cloned.1.call-done) | copy-start | bytes 9437188
  68.4 2.7 %copy-start.5 = (bf16[2048,128]{1,0:T(8,128)(2,1)S(1)}, bf16[2048,128]{1,0:T(8,128)(2,1)}, u32[]{:S(2)}) copy-start(bf16[2048,128]{1,0:T(8,128)(2,1)} %param.9) | copy-start | bytes 1572868
  69.3 32.0 %collective-permute-start.5 = (bf16[2,128,1536]{2,1,0:T(8,128)(2,1)S(1)}, bf16[2,128,1536]{2,1,0:T(8,128)(2,1)S(1)}, u32[]{:S(2)}, u32[]{:S(2)}) collective-permute-start(bf16[2,128,1536]{2,1,0:T(8,128)(2,1)S(1)} %pad_maximum_fusion), channel_id=1, source_target_pairs={{0,8},{8,0},{1,9},{9,1},{2,10},{10,2},{3,11},{11,3},{4,12},{12,4},... | collective-permute-start | bytes 2359304 | tf_op jit(solution)/shard_map/ppermute | solution.py:216
  99.3 2.0 %collective-permute-start.6 = (bf16[128,1024]{0,1:T(8,128)(2,1)S(1)}, bf16[128,1024]{0,1:T(8,128)(2,1)S(1)}, u32[]{:S(2)}, u32[]{:S(2)}) collective-permute-start(bf16[128,1024]{0,1:T(8,128)(2,1)S(1)} %bitcast.35), channel_id=1, source_target_pairs={{0,16},{16,0},{32,48},{48,32},{64,80},{80,64},{96,112},{112,96},{1... | collective-permute-start | bytes 786440 | tf_op jit(solution)/shard_map/ppermute | solution.py:209
  103.7 3.0 %collective-permute-start.7 = (bf16[128,1536]{1,0:T(8,128)(2,1)S(1)}, bf16[128,1536]{1,0:T(8,128)(2,1)S(1)}, u32[]{:S(2)}, u32[]{:S(2)}) collective-permute-start(bf16[128,1536]{1,0:T(8,128)(2,1)S(1)} %fusion), channel_id=1, source_target_pairs={{0,16},{16,0},{32,48},{48,32},{64,80},{80,64},{96,112},{112,96},{1... | collective-permute-start | bytes 1179656 | tf_op jit(solution)/shard_map/ppermute | solution.py:219
Sparse Core Ops, SparseCore 0:
  9.1 49.8 all-gather.1

commit v9 on v7

--- a/solution.py
+++ b/solution.py
@@ -74,10 +74,83 @@
     return bias.reshape(TROWS * GROUPS, QTILES, ROW_K)
 
 
-def attention_kernel(q_ref, kp_ref, k_ref, kn_ref, vp_ref, v_ref, vn_ref, bias_ref, o_ref,
-                     s_ref, p_ref):
+def attention_kernel(q_ref, k_ref, v_ref, bias_ref, o_ref,
+                     kp_ref, kn_ref, vp_ref, vn_ref, s_ref, p_ref, send_sem, recv_sem):
     row = pl.program_id(0)
     group = pl.program_id(1)
+
+    @pl.when((row == 0) & (group == 0))
+    def _():
+        frame = lax.axis_index("frame")
+        count = lax.axis_size("frame")
+        side = lax.axis_index("hy")
+        peer = lax.axis_index("hz")
+        mesh = pl.DeviceIdType.MESH
+        has_prev = frame > 0
+        has_next = frame < count - 1
+        prev_dev = (frame - 1, side, peer)
+        next_dev = (frame + 1, side, peer)
+        barrier = pltpu.get_barrier_semaphore()
+
+        @pl.when(has_prev)
+        def _():
+            pl.semaphore_signal(barrier, inc=1, device_id=prev_dev, device_id_type=mesh)
+
+        @pl.when(has_next)
+        def _():
+            pl.semaphore_signal(barrier, inc=1, device_id=next_dev, device_id_type=mesh)
+
+        @pl.when(has_prev & has_next)
+        def _():
+            pl.semaphore_wait(barrier, 2)
+
+        @pl.when(has_prev != has_next)
+        def _():
+            pl.semaphore_wait(barrier, 1)
+
+        def push(src, dst, slot, device):
+            return pltpu.make_async_remote_copy(
+                src_ref=src, dst_ref=dst, send_sem=send_sem.at[slot], recv_sem=recv_sem.at[slot],
+                device_id=device, device_id_type=mesh,
+            )
+
+        to_next = [push(k_ref, kp_ref, 0, next_dev), push(v_ref, vp_ref, 1, next_dev)]
+        to_prev = [push(k_ref, kn_ref, 2, prev_dev), push(v_ref, vn_ref, 3, prev_dev)]
+
+        @pl.when(has_next)
+        def _():
+            for copy in to_next:
+                copy.start()
+
+        @pl.when(has_prev)
+        def _():
+            for copy in to_prev:
+                copy.start()
+
+        @pl.when(has_prev)
+        def _():
+            for copy in to_prev:
+                copy.wait_send()
+            for copy in to_next:
+                copy.wait_recv()
+
+        @pl.when(has_next)
+        def _():
+            for copy in to_next:
+                copy.wait_send()
+            for copy in to_prev:
+                copy.wait_recv()
+
+        @pl.when(jnp.logical_not(has_prev))
+        def _():
+            kp_ref[...] = jnp.zeros_like(kp_ref)
+            vp_ref[...] = jnp.zeros_like(vp_ref)
+
+        @pl.when(jnp.logical_not(has_next))
+        def _():
+            kn_ref[...] = jnp.zeros_like(kn_ref)
+            vn_ref[...] = jnp.zeros_like(vn_ref)
+
     start = jnp.clip(QTILES * group - 2, 0, TCOLS - KCOLS) * TILE
     key_refs = (kp_ref, k_ref, kn_ref)
     value_refs = (vp_ref, v_ref, vn_ref)
@@ -109,22 +182,26 @@
     o_ref[...] = acc.astype(o_ref.dtype)
 
 
-def attend(q, kp, k, kn, vp, v, vn, bias):
+def attend(q, k, v, bias):
     tokens = q.shape[0]
     full = pl.BlockSpec((tokens, HEAD_DIM), lambda r, g: (0, 0))
+    frame_kv = pltpu.VMEM((tokens, HEAD_DIM), jnp.bfloat16)
     return pl.pallas_call(
         attention_kernel,
         grid=(TROWS, GROUPS),
         in_specs=[pl.BlockSpec((BLOCK_Q, HEAD_DIM), lambda r, g: (r * GROUPS + g, 0))]
-        + [full] * 6
+        + [full] * 2
         + [pl.BlockSpec((1, QTILES, ROW_K), lambda r, g: (r * GROUPS + g, 0, 0))],
         out_specs=pl.BlockSpec((BLOCK_Q, HEAD_DIM), lambda r, g: (r * GROUPS + g, 0)),
         out_shape=jax.ShapeDtypeStruct((tokens, HEAD_DIM), jnp.bfloat16),
-        scratch_shapes=[
+        scratch_shapes=[frame_kv] * 4 + [
             pltpu.VMEM((BLOCK_Q, ROW_K), jnp.float32),
             pltpu.VMEM((BLOCK_Q, ROW_K), jnp.bfloat16),
+            pltpu.SemaphoreType.DMA((4,)),
+            pltpu.SemaphoreType.DMA((4,)),
         ],
-    )(q, kp, k, kn, vp, v, vn, bias)
+        compiler_params=pltpu.CompilerParams(collective_id=1, has_side_effects=True),
+    )(q, k, v, bias)
 
 
 def exchange_kernel(x_ref, o_ref, send_sem, recv_sem):
@@ -175,13 +252,9 @@
     count = lax.axis_size("frame")
     frames_total = frames_here * count
     frame = lax.axis_index("frame") * frames_here
-    forward = [(i, i + 1) for i in range(count - 1)]
-    backward = [(t, s) for s, t in forward]
-    prev = [lax.ppermute(x, "frame", forward) for x in (keys, values)]
-    nxt = [lax.ppermute(x, "frame", backward) for x in (keys, values)]
     mask_rows = block_mask.reshape(TROWS * TCOLS, WIN)
     bias = window_bias(mask_rows, frame, frames_total)
-    attention = attend(queries, prev[0], keys, nxt[0], prev[1], values, nxt[1], bias)
+    attention = attend(queries, keys, values, bias)
     core = lax.axis_index("frame") % 2
     side = lax.axis_index("hy")
     sides = lax.axis_size("hy")

time: 116 us -> 112 us (0.966)
  the two profiles are of different devices: /device:TPU:6 before, /device:TPU:17 now
where the time goes in v9:
time: 112 us; the launch traced here: 110 us
  Pallas kernels  56.3 us (50%)
  between operations  13.5 us (12%)
  waiting for transfers between devices  13.4 us (12%)
  matrix products  9.3 us (8%)
  starting transfers between devices  7.95 us (7%)
  local copies, waits for them, and re-layouts  6.85 us (6%)
  other arithmetic  2.82 us (3%)
    pallas_call x1, Pallas kernels, attend(): pl.pallas_call(attention_kernel, grid=(TROWS, GROUPS), in_specs=[pl.Block...  37.9 us
    pallas_call x1, Pallas kernels, exchange(): pl.pallas_call(exchange_kernel, out_shape=jax.ShapeDtypeStruct(x.shape, x...  18.4 us
    dot_general x4, matrix products, project(): return jnp.dot(rows, weight_half, preferred_element_type=jnp.float32)  8.25 us
    ppermute x1, waiting for transfers between devices, on_device(): lax.ppermute(project(theirs, 1 - side).astype(jnp.bfloat16), 'hy', flip)  6.13 us
    ppermute x1, waiting for transfers between devices, on_device(): lax.ppermute(project(mine, 1 - side).astype(jnp.bfloat16), 'hy', flip)  5.73 us
    ppermute x1, starting transfers between devices, on_device(): theirs = lax.ppermute(mine, 'frame', partners)  4.24 us
  transfers between devices with their start and end apart: 5, of which 3 were waited for; matrix products, arithmetic and copies ran while one was open for 12% of the time, Pallas kernels for 51%

profile of v9, /device:TPU:17, one launch (start us, length us, event | category | flops | bytes accessed | tf_op | source)
XLA Modules:
  0.0 110.2 jit_solution(697441517181092836)
XLA Ops:
  6.5 0.0 copy-start
  6.5 0.0 all-gather.2.cloned.1.call-start
  6.5 1.1 %copy-done = bf16[128,3072]{1,0:T(8,128)(2,1)S(1)} copy-done((bf16[128,3072]{1,0:T(8,128)(2,1)S(1)}, bf16[128,3072]{1,0:T(8,128)(2,1)}, u32[]{:S(2)}) %copy-start) | copy-done | bytes 786456
  7.7 0.8 constant_dynamic-slice_fusion
  8.5 0.0 all-gather.2.cloned.1.call-update
  8.5 0.7 convert_bitcast_fusion
  9.2 1.0 fusion.3
  10.3 0.1 reshape.27
  10.4 1.0 fusion.13
  11.5 0.4 broadcast_in_dim.16
  11.8 0.3 reshape.20
  12.1 1.0 copy.15.bias_ref
  13.1 37.9 %shard_map.91 = bf16[2048,128]{1,0:T(8,128)(2,1)} custom-call(bf16[2048,128]{1,0:T(8,128)(2,1)} %q_ref.1, bf16[2048,128]{1,0:T(8,128)(2,1)} %k_ref.1, bf16[2048,128]{1,0:T(8,128)(2,1)} %v_ref.1, f32[16,2,3456]{2,1,0:T(2,128)} %copy.15.bias_ref), custom_call_target="tpu_custom_call" | custom-call | tf_op jit(solution)/shard_map/pallas_call | solution.py:189
  51.1 1.9 %copy.16 = bf16[2,8,128,128]{3,2,0,1:T(8,128)(2,1)} copy(bf16[2,8,128,128]{3,2,1,0:T(8,128)(2,1)} %bitcast.20) | data formatting | bytes 1048576 | tf_op jit(solution)/shard_map/reshape | solution.py:265
  53.0 18.4 %shard_map.92 = bf16[8,256,128]{2,1,0:T(8,128)(2,1)} custom-call(bf16[8,256,128]{2,1,0:T(8,128)(2,1)} %bitcast.21), custom_call_target="tpu_custom_call" | custom-call | tf_op jit(solution)/shard_map/pallas_call | solution.py:238
  71.4 1.2 %copy.17 = bf16[256,8,128]{0,2,1:T(8,128)(2,1)S(1)} copy(bf16[256,8,128]{2,0,1:T(8,128)(2,1)} %bitcast.22) | data formatting | bytes 1048576 | tf_op jit(solution)/shard_map/transpose | solution.py:268
  72.6 4.2 %collective-permute-start.1 = (bf16[256,1024]{0,1:T(8,128)(2,1)S(1)}, bf16[256,1024]{0,1:T(8,128)(2,1)S(1)}, u32[]{:S(2)}, u32[]{:S(2)}) collective-permute-start(bf16[256,1024]{0,1:T(8,128)(2,1)S(1)} %bitcast.17), channel_id=1, source_target_pairs={{0,16},{16,0},{32,48},{48,32},{64,80},{80,64},{96,112},{112,96},{1... | collective-permute-start | bytes 1572872 | tf_op jit(solution)/shard_map/ppermute | solution.py:269
  76.9 1.5 %collective-permute-done.1 = bf16[256,1024]{0,1:T(8,128)(2,1)S(1)} collective-permute-done((bf16[256,1024]{0,1:T(8,128)(2,1)S(1)}, bf16[256,1024]{0,1:T(8,128)(2,1)S(1)}, u32[]{:S(2)}, u32[]{:S(2)}) %collective-permute-start.1) | collective-permute-done | bytes 524320 | tf_op jit(solution)/shard_map/ppermute | solution.py:269
  78.4 0.0 all-gather.2.cloned.1.call-done
  78.4 2.5 %convolution_convert_fusion = bf16[128,1536]{1,0:T(8,128)(2,1)S(1)} fusion(bf16[1024,1536]{1,0:T(8,128)(2,1)} %all-gather.2.cloned.1.call-done, bf16[256,1024]{0,1:T(8,128)(2,1)S(1)} %collective-permute-done.1, s32[]{:T(128)S(6)} %select_n.35), kind=kOutput, calls=%fused_computation.2 | convolution fusion | flops 402849792 | bytes 3801092 | tf_op jit(solution)/shard_map/dot_general | solution.py:274
  80.9 1.1 collective-permute-start.2
  82.0 0.0 copy-start.1
  82.0 2.6 %convolution_convert_fusion.1 = bf16[128,1536]{1,0:T(8,128)(2,1)S(1)} fusion(bf16[1024,1536]{1,0:T(8,128)(2,1)} %all-gather.2.cloned.1.call-done, bf16[256,1024]{0,1:T(8,128)(2,1)S(1)} %bitcast.18, s32[]{:T(128)S(6)} %select_n.35), kind=kOutput, calls=%fused_computation.3 | convolution fusion | flops 402849792 | bytes 3801092 | tf_op jit(solution)/shard_map/dot_general | solution.py:274
  84.6 0.6 collective-permute-start
  85.2 6.1 %collective-permute-done.2 = bf16[128,1536]{1,0:T(8,128)(2,1)S(1)} collective-permute-done((bf16[128,1536]{1,0:T(8,128)(2,1)S(1)}, bf16[128,1536]{1,0:T(8,128)(2,1)S(1)}, u32[]{:S(2)}, u32[]{:S(2)}) %collective-permute-start.2) | collective-permute-done | bytes 393248 | tf_op jit(solution)/shard_map/ppermute | solution.py:278
  91.3 0.0 copy-done.1
  91.3 0.6 fusion
  91.9 2.1 %collective-permute-start.3 = (bf16[128,1536]{1,0:T(8,128)(2,1)S(1)}, bf16[128,1536]{1,0:T(8,128)(2,1)S(1)}, u32[]{:S(2)}, u32[]{:S(2)}) collective-permute-start(bf16[128,1536]{1,0:T(8,128)(2,1)S(1)} %fusion), channel_id=1, source_target_pairs={{0,16},{16,0},{32,48},{48,32},{64,80},{80,64},{96,112},{112,96},{1... | collective-permute-start | bytes 1179656 | tf_op jit(solution)/shard_map/ppermute | solution.py:280
  94.0 5.7 %collective-permute-done = bf16[128,1536]{1,0:T(8,128)(2,1)S(1)} collective-permute-done((bf16[128,1536]{1,0:T(8,128)(2,1)S(1)}, bf16[128,1536]{1,0:T(8,128)(2,1)S(1)}, u32[]{:S(2)}, u32[]{:S(2)}) %collective-permute-start) | collective-permute-done | bytes 393248 | tf_op jit(solution)/shard_map/ppermute | solution.py:277
  99.7 2.5 %add_convert_fusion = bf16[128,1536]{1,0:T(8,128)(2,1)S(1)} fusion(bf16[128,1536]{1,0:T(8,128)(2,1)S(1)} %collective-permute-done, bf16[1024,1536]{1,0:T(8,128)(2,1)} %all-gather.2.cloned.1.call-done, bf16[256,1024]{0,1:T(8,128)(2,1)S(1)} %bitcast.19, s32[]{:T(128)S(6)} %select_n.33), kind=kOutput, calls=%fused_computation.9 | convolution fusion | flops 403243008 | bytes 4194308 | tf_op jit(solution)/shard_map/dot_general | solution.py:274
  102.2 0.0 collective-permute-done.3
  102.3 1.1 maximum_select_fusion
  (2 shorter events, 0.0 us)
Async XLA Ops:
  6.5 1.1 %copy-start = (bf16[128,3072]{1,0:T(8,128)(2,1)S(1)}, bf16[128,3072]{1,0:T(8,128)(2,1)}, u32[]{:S(2)}) copy-start(bf16[128,3072]{1,0:T(8,128)(2,1)} %param.13) | copy-start | bytes 2359300
  6.5 71.9 %all-gather.2.cloned.1.call-start = ((), (), s32[]{:S(2)}) async-start(), calls=%async_computation | async-start | bytes 3538944 | tf_op jit(solution)/shard_map/all_gather | solution.py:264
  72.6 5.8 %collective-permute-start.1 = (bf16[256,1024]{0,1:T(8,128)(2,1)S(1)}, bf16[256,1024]{0,1:T(8,128)(2,1)S(1)}, u32[]{:S(2)}, u32[]{:S(2)}) collective-permute-start(bf16[256,1024]{0,1:T(8,128)(2,1)S(1)} %bitcast.17), channel_id=1, source_target_pairs={{0,16},{16,0},{32,48},{48,32},{64,80},{80,64},{96,112},{112,96},{1... | collective-permute-start | bytes 1572872 | tf_op jit(solution)/shard_map/ppermute | solution.py:269
  80.9 10.4 %collective-permute-start.2 = (bf16[128,1536]{1,0:T(8,128)(2,1)S(1)}, bf16[128,1536]{1,0:T(8,128)(2,1)S(1)}, u32[]{:S(2)}, u32[]{:S(2)}) collective-permute-start(bf16[128,1536]{1,0:T(8,128)(2,1)S(1)} %convolution_convert_fusion), channel_id=1, source_target_pairs={{0,8},{8,0},{1,9},{9,1},{2,10},{10,2},{3,11},{11,3},{4,12},{12,4},... | collective-permute-start | bytes 1179656 | tf_op jit(solution)/shard_map/ppermute | solution.py:278
  82.0 9.3 %copy-start.1 = (bf16[1024,1536]{1,0:T(8,128)(2,1)S(1)}, bf16[1024,1536]{1,0:T(8,128)(2,1)}, u32[]{:S(2)}) copy-start(bf16[1024,1536]{1,0:T(8,128)(2,1)} %all-gather.2.cloned.1.call-done) | copy-start | bytes 9437188
  84.6 15.1 %collective-permute-start = (bf16[128,1536]{1,0:T(8,128)(2,1)S(1)}, bf16[128,1536]{1,0:T(8,128)(2,1)S(1)}, u32[]{:S(2)}, u32[]{:S(2)}) collective-permute-start(bf16[128,1536]{1,0:T(8,128)(2,1)S(1)} %convolution_convert_fusion.1), channel_id=1, source_target_pairs={{0,8},{8,0},{1,9},{9,1},{2,10},{10,2},{3,11},{11,3},{4,12},{12,4},... | collective-permute-start | bytes 1179656 | tf_op jit(solution)/shard_map/ppermute | solution.py:277
  91.9 10.3 %collective-permute-start.3 = (bf16[128,1536]{1,0:T(8,128)(2,1)S(1)}, bf16[128,1536]{1,0:T(8,128)(2,1)S(1)}, u32[]{:S(2)}, u32[]{:S(2)}) collective-permute-start(bf16[128,1536]{1,0:T(8,128)(2,1)S(1)} %fusion), channel_id=1, source_target_pairs={{0,16},{16,0},{32,48},{48,32},{64,80},{80,64},{96,112},{112,96},{1... | collective-permute-start | bytes 1179656 | tf_op jit(solution)/shard_map/ppermute | solution.py:280
Sparse Core Ops, SparseCore 0:
  9.1 47.4 all-gather.1

commit v10 on v9

--- a/solution.py
+++ b/solution.py
@@ -75,17 +75,20 @@
 
 
 def attention_kernel(q_ref, k_ref, v_ref, bias_ref, o_ref,
-                     kp_ref, kn_ref, vp_ref, vn_ref, s_ref, p_ref, send_sem, recv_sem):
+                     kp_ref, kn_ref, vp_ref, vn_ref, s_ref, p_ref, att_ref, got_ref,
+                     send_sem, recv_sem, out_send, out_recv):
     row = pl.program_id(0)
     group = pl.program_id(1)
+    frame = lax.axis_index("frame")
+    side = lax.axis_index("hy")
+    me = lax.axis_index("hz")
+    peers = lax.axis_size("hz")
+    mesh = pl.DeviceIdType.MESH
 
     @pl.when((row == 0) & (group == 0))
     def _():
-        frame = lax.axis_index("frame")
         count = lax.axis_size("frame")
-        side = lax.axis_index("hy")
-        peer = lax.axis_index("hz")
-        mesh = pl.DeviceIdType.MESH
+        peer = me
         has_prev = frame > 0
         has_next = frame < count - 1
         prev_dev = (frame - 1, side, peer)
@@ -100,13 +103,17 @@
         def _():
             pl.semaphore_signal(barrier, inc=1, device_id=next_dev, device_id_type=mesh)
 
+        for i in range(1, peers):
+            other = (frame, side, lax.rem(me + i, peers))
+            pl.semaphore_signal(barrier, inc=1, device_id=other, device_id_type=mesh)
+
         @pl.when(has_prev & has_next)
         def _():
-            pl.semaphore_wait(barrier, 2)
+            pl.semaphore_wait(barrier, peers + 1)
 
         @pl.when(has_prev != has_next)
         def _():
-            pl.semaphore_wait(barrier, 1)
+            pl.semaphore_wait(barrier, peers)
 
         def push(src, dst, slot, device):
             return pltpu.make_async_remote_copy(
@@ -179,70 +186,62 @@
         v = value_refs[df][pl.ds(bases[seg], SEG_K), :]
         acc += jnp.dot(p_ref[:, seg * SEG_K:(seg + 1) * SEG_K], v,
                        preferred_element_type=jnp.float32)
-    o_ref[...] = acc.astype(o_ref.dtype)
+    att_ref[pl.ds(pl.multiple_of((row * GROUPS + group) * BLOCK_Q, BLOCK_Q), BLOCK_Q), :] = (
+        acc.astype(att_ref.dtype))
+
+    @pl.when((row == TROWS - 1) & (group == GROUPS - 1))
+    def _():
+        chunk = got_ref.shape[1] // 2
+        copies = []
+        for i in range(1, peers):
+            peer = lax.rem(me + i, peers)
+            for part in range(2):
+                src = pl.multiple_of((part * peers + peer) * chunk, chunk)
+                copy = pltpu.make_async_remote_copy(
+                    src_ref=att_ref.at[pl.ds(src, chunk)],
+                    dst_ref=got_ref.at[me, pl.ds(part * chunk, chunk)],
+                    send_sem=out_send.at[2 * i + part],
+                    recv_sem=out_recv.at[2 * i + part],
+                    device_id=(frame, side, peer),
+                    device_id_type=mesh,
+                )
+                copy.start()
+                copies.append(copy)
+        for part in range(2):
+            src = pl.multiple_of((part * peers + me) * chunk, chunk)
+            got_ref[me, pl.ds(part * chunk, chunk), :] = att_ref[pl.ds(src, chunk), :]
+        for copy in copies:
+            copy.wait()
+        o_ref[...] = got_ref[...]
 
 
 def attend(q, k, v, bias):
     tokens = q.shape[0]
     full = pl.BlockSpec((tokens, HEAD_DIM), lambda r, g: (0, 0))
     frame_kv = pltpu.VMEM((tokens, HEAD_DIM), jnp.bfloat16)
+    peers = lax.axis_size("hz")
+    got_shape = (peers, tokens // peers, HEAD_DIM)
+    got = pltpu.VMEM(got_shape, jnp.bfloat16)
     return pl.pallas_call(
         attention_kernel,
         grid=(TROWS, GROUPS),
         in_specs=[pl.BlockSpec((BLOCK_Q, HEAD_DIM), lambda r, g: (r * GROUPS + g, 0))]
         + [full] * 2
         + [pl.BlockSpec((1, QTILES, ROW_K), lambda r, g: (r * GROUPS + g, 0, 0))],
-        out_specs=pl.BlockSpec((BLOCK_Q, HEAD_DIM), lambda r, g: (r * GROUPS + g, 0)),
-        out_shape=jax.ShapeDtypeStruct((tokens, HEAD_DIM), jnp.bfloat16),
+        out_specs=pl.BlockSpec(got_shape, lambda r, g: (0, 0, 0)),
+        out_shape=jax.ShapeDtypeStruct(got_shape, jnp.bfloat16),
         scratch_shapes=[frame_kv] * 4 + [
             pltpu.VMEM((BLOCK_Q, ROW_K), jnp.float32),
             pltpu.VMEM((BLOCK_Q, ROW_K), jnp.bfloat16),
+            frame_kv,
+            got,
             pltpu.SemaphoreType.DMA((4,)),
             pltpu.SemaphoreType.DMA((4,)),
+            pltpu.SemaphoreType.DMA((2 * peers,)),
+            pltpu.SemaphoreType.DMA((2 * peers,)),
         ],
         compiler_params=pltpu.CompilerParams(collective_id=1, has_side_effects=True),
     )(q, k, v, bias)
-
-
-def exchange_kernel(x_ref, o_ref, send_sem, recv_sem):
-    me = lax.axis_index("hz")
-    peers = lax.axis_size("hz")
-    frame = lax.axis_index("frame")
-    side = lax.axis_index("hy")
-    mesh = pl.DeviceIdType.MESH
-    barrier = pltpu.get_barrier_semaphore()
-    for i in range(1, peers):
-        peer = lax.rem(me + i, peers)
-        pl.semaphore_signal(barrier, inc=1, device_id=(frame, side, peer), device_id_type=mesh)
-    pl.semaphore_wait(barrier, peers - 1)
-    copies = []
-    for i in range(1, peers):
-        peer = lax.rem(me + i, peers)
-        copy = pltpu.make_async_remote_copy(
-            src_ref=x_ref.at[peer],
-            dst_ref=o_ref.at[me],
-            send_sem=send_sem.at[i],
-            recv_sem=recv_sem.at[i],
-            device_id=(frame, side, peer),
-            device_id_type=mesh,
-        )
-        copy.start()
-        copies.append(copy)
-    o_ref[me] = x_ref[me]
-    for copy in copies:
-        copy.wait()
-
-
-def exchange(x):
-    peers = x.shape[0]
-    return pl.pallas_call(
-        exchange_kernel,
-        out_shape=jax.ShapeDtypeStruct(x.shape, x.dtype),
-        in_specs=[pl.BlockSpec(memory_space=pltpu.VMEM)],
-        out_specs=pl.BlockSpec(memory_space=pltpu.VMEM),
-        scratch_shapes=[pltpu.SemaphoreType.DMA((peers,)), pltpu.SemaphoreType.DMA((peers,))],
-        compiler_params=pltpu.CompilerParams(collective_id=0, has_side_effects=True),
-    )(x)
 
 
 def on_device(queries, keys, values, block_mask, out_weight):
@@ -254,7 +253,7 @@
     frame = lax.axis_index("frame") * frames_here
     mask_rows = block_mask.reshape(TROWS * TCOLS, WIN)
     bias = window_bias(mask_rows, frame, frames_total)
-    attention = attend(queries, keys, values, bias)
+    got = attend(queries, keys, values, bias)
     core = lax.axis_index("frame") % 2
     side = lax.axis_index("hy")
     sides = lax.axis_size("hy")
@@ -262,10 +261,8 @@
     partners = [(i, i ^ 1) for i in range(count)]
     weight_half = lax.dynamic_slice_in_dim(out_weight, core * half, half, axis=1)
     weight_half = lax.all_gather(weight_half, "hz", axis=0, tiled=True)
-    chunks = attention.reshape(sides, -1, tok_dev // (sides * lax.axis_size("hz")), HEAD_DIM)
     peers = lax.axis_size("hz")
-    chunks = chunks.transpose(1, 0, 2, 3).reshape(peers, tok_dev // peers, HEAD_DIM)
-    mine = exchange(chunks).transpose(1, 0, 2).reshape(tok_dev // peers, peers * HEAD_DIM)
+    mine = got.transpose(1, 0, 2).reshape(tok_dev // peers, peers * HEAD_DIM)
     theirs = lax.ppermute(mine, "frame", partners)
     block = mine.shape[0] // sides
 

time: 112 us -> 108 us (0.964)
  starting transfers between devices: 7.95 us -> 4.5 us
  Pallas kernels: 56.3 us -> 58.8 us
  local copies, waits for them, and re-layouts: 6.85 us -> 4.96 us
    pallas_call x1, Pallas kernels: 37.9 us -> 58.8 us  [attend(): pl.pallas_call(attention_kernel, grid=(TROWS, GROUPS), in_specs=[pl.Block...]
    pallas_call x1 -> x0, Pallas kernels: 18.4 us -> none  [exchange(): pl.pallas_call(exchange_kernel, out_shape=jax.ShapeDtypeStruct(x.shape, x...]
    ppermute x1, starting transfers between devices: 4.24 us -> 0.78 us  [on_device(): theirs = lax.ppermute(mine, 'frame', partners)]
    reshape x1 -> x0, local copies, waits for them, and re-layouts: 1.89 us -> none  [on_device(): attention.reshape(sides, -1, tok_dev // (sides * lax.axis_size('hz')), HE...]
  transfers between devices with their start and end apart: 5 -> 5, of which waited for: 3 -> 3; matrix products, arithmetic and copies ran while one was open for 12% -> 11% of each run, Pallas kernels for 51% -> 55%
where the time goes in v10:
time: 108 us; the launch traced here: 107 us
  Pallas kernels  58.8 us (54%)
  between operations  13.5 us (12%)
  waiting for transfers between devices  13.4 us (12%)
  matrix products  9.3 us (9%)
  local copies, waits for them, and re-layouts  4.96 us (5%)
  starting transfers between devices  4.5 us (4%)
  other arithmetic  2.82 us (3%)
    pallas_call x1, Pallas kernels, attend(): pl.pallas_call(attention_kernel, grid=(TROWS, GROUPS), in_specs=[pl.Block...  58.8 us
    dot_general x4, matrix products, project(): return jnp.dot(rows, weight_half, preferred_element_type=jnp.float32)  8.25 us
    ppermute x1, waiting for transfers between devices, on_device(): lax.ppermute(project(theirs, 1 - side).astype(jnp.bfloat16), 'hy', flip)  6.13 us
    ppermute x1, waiting for transfers between devices, on_device(): lax.ppermute(project(mine, 1 - side).astype(jnp.bfloat16), 'hy', flip)  5.71 us
  transfers between devices with their start and end apart: 5, of which 3 were waited for; matrix products, arithmetic and copies ran while one was open for 11% of the time, Pallas kernels for 55%

profile of v10, /device:TPU:17, one launch (start us, length us, event | category | flops | bytes accessed | tf_op | source)
XLA Modules:
  0.0 107.3 jit_solution(13987302719529322294)
XLA Ops:
  6.5 0.0 copy-start
  6.5 0.0 all-gather.2.cloned.1.call-start
  6.5 1.1 %copy-done = bf16[128,3072]{1,0:T(8,128)(2,1)S(1)} copy-done((bf16[128,3072]{1,0:T(8,128)(2,1)S(1)}, bf16[128,3072]{1,0:T(8,128)(2,1)}, u32[]{:S(2)}) %copy-start) | copy-done | bytes 786456
  7.7 0.8 constant_dynamic-slice_fusion
  8.5 0.0 all-gather.2.cloned.1.call-update
  8.5 0.7 convert_bitcast_fusion
  9.2 1.0 fusion.3
  10.3 0.1 reshape.19
  10.4 1.0 fusion.13
  11.5 0.4 broadcast_in_dim.16
  11.8 0.3 reshape.14
  12.1 1.0 copy.14.bias_ref
  13.1 58.8 %shard_map.91 = bf16[8,256,128]{2,1,0:T(8,128)(2,1)} custom-call(bf16[2048,128]{1,0:T(8,128)(2,1)} %q_ref.1, bf16[2048,128]{1,0:T(8,128)(2,1)} %k_ref.1, bf16[2048,128]{1,0:T(8,128)(2,1)} %v_ref.1, f32[16,2,3456]{2,1,0:T(2,128)} %copy.14.bias_ref), custom_call_target="tpu_custom_call" | custom-call | tf_op jit(solution)/shard_map/pallas_call | solution.py:225
  71.9 1.2 %copy.15 = bf16[256,8,128]{0,2,1:T(8,128)(2,1)S(1)} copy(bf16[256,8,128]{2,0,1:T(8,128)(2,1)} %bitcast.16) | data formatting | bytes 1048576 | tf_op jit(solution)/shard_map/transpose | solution.py:265
  73.2 0.8 collective-permute-start.1
  74.0 1.5 %collective-permute-done.1 = bf16[256,1024]{0,1:T(8,128)(2,1)S(1)} collective-permute-done((bf16[256,1024]{0,1:T(8,128)(2,1)S(1)}, bf16[256,1024]{0,1:T(8,128)(2,1)S(1)}, u32[]{:S(2)}, u32[]{:S(2)}) %collective-permute-start.1) | collective-permute-done | bytes 524320 | tf_op jit(solution)/shard_map/ppermute | solution.py:266
  75.5 0.0 all-gather.2.cloned.1.call-done
  75.5 2.5 %convolution_convert_fusion = bf16[128,1536]{1,0:T(8,128)(2,1)S(1)} fusion(bf16[1024,1536]{1,0:T(8,128)(2,1)} %all-gather.2.cloned.1.call-done, bf16[256,1024]{0,1:T(8,128)(2,1)S(1)} %collective-permute-done.1, s32[]{:T(128)S(6)} %select_n.35), kind=kOutput, calls=%fused_computation.2 | convolution fusion | flops 402849792 | bytes 3801092 | tf_op jit(solution)/shard_map/dot_general | solution.py:271
  78.0 1.1 %collective-permute-start.2 = (bf16[128,1536]{1,0:T(8,128)(2,1)S(1)}, bf16[128,1536]{1,0:T(8,128)(2,1)S(1)}, u32[]{:S(2)}, u32[]{:S(2)}) collective-permute-start(bf16[128,1536]{1,0:T(8,128)(2,1)S(1)} %convolution_convert_fusion), channel_id=1, source_target_pairs={{0,8},{8,0},{1,9},{9,1},{2,10},{10,2},{3,11},{11,3},{4,12},{12,4},... | collective-permute-start | bytes 1179656 | tf_op jit(solution)/shard_map/ppermute | solution.py:275
  79.1 0.0 copy-start.1
  79.1 2.6 %convolution_convert_fusion.1 = bf16[128,1536]{1,0:T(8,128)(2,1)S(1)} fusion(bf16[1024,1536]{1,0:T(8,128)(2,1)} %all-gather.2.cloned.1.call-done, bf16[256,1024]{0,1:T(8,128)(2,1)S(1)} %bitcast.14, s32[]{:T(128)S(6)} %select_n.35), kind=kOutput, calls=%fused_computation.3 | convolution fusion | flops 402849792 | bytes 3801092 | tf_op jit(solution)/shard_map/dot_general | solution.py:271
  81.7 0.5 collective-permute-start
  82.3 6.1 %collective-permute-done.2 = bf16[128,1536]{1,0:T(8,128)(2,1)S(1)} collective-permute-done((bf16[128,1536]{1,0:T(8,128)(2,1)S(1)}, bf16[128,1536]{1,0:T(8,128)(2,1)S(1)}, u32[]{:S(2)}, u32[]{:S(2)}) %collective-permute-start.2) | collective-permute-done | bytes 393248 | tf_op jit(solution)/shard_map/ppermute | solution.py:275
  88.4 0.0 copy-done.1
  88.4 0.6 fusion
  89.0 2.1 %collective-permute-start.3 = (bf16[128,1536]{1,0:T(8,128)(2,1)S(1)}, bf16[128,1536]{1,0:T(8,128)(2,1)S(1)}, u32[]{:S(2)}, u32[]{:S(2)}) collective-permute-start(bf16[128,1536]{1,0:T(8,128)(2,1)S(1)} %fusion), channel_id=1, source_target_pairs={{0,16},{16,0},{32,48},{48,32},{64,80},{80,64},{96,112},{112,96},{1... | collective-permute-start | bytes 1179656 | tf_op jit(solution)/shard_map/ppermute | solution.py:277
  91.1 5.7 %collective-permute-done = bf16[128,1536]{1,0:T(8,128)(2,1)S(1)} collective-permute-done((bf16[128,1536]{1,0:T(8,128)(2,1)S(1)}, bf16[128,1536]{1,0:T(8,128)(2,1)S(1)}, u32[]{:S(2)}, u32[]{:S(2)}) %collective-permute-start) | collective-permute-done | bytes 393248 | tf_op jit(solution)/shard_map/ppermute | solution.py:274
  96.8 2.5 %add_convert_fusion = bf16[128,1536]{1,0:T(8,128)(2,1)S(1)} fusion(bf16[128,1536]{1,0:T(8,128)(2,1)S(1)} %collective-permute-done, bf16[1024,1536]{1,0:T(8,128)(2,1)} %all-gather.2.cloned.1.call-done, bf16[256,1024]{0,1:T(8,128)(2,1)S(1)} %bitcast.15, s32[]{:T(128)S(6)} %select_n.33), kind=kOutput, calls=%fused_computation.9 | convolution fusion | flops 403243008 | bytes 4194308 | tf_op jit(solution)/shard_map/dot_general | solution.py:271
  99.3 0.0 collective-permute-done.3
  99.4 1.1 maximum_select_fusion
  (2 shorter events, 0.0 us)
Async XLA Ops:
  6.5 1.1 %copy-start = (bf16[128,3072]{1,0:T(8,128)(2,1)S(1)}, bf16[128,3072]{1,0:T(8,128)(2,1)}, u32[]{:S(2)}) copy-start(bf16[128,3072]{1,0:T(8,128)(2,1)} %param.13) | copy-start | bytes 2359300
  6.5 69.0 %all-gather.2.cloned.1.call-start = ((), (), s32[]{:S(2)}) async-start(), calls=%async_computation | async-start | bytes 3538944 | tf_op jit(solution)/shard_map/all_gather | solution.py:263
  73.2 2.3 %collective-permute-start.1 = (bf16[256,1024]{0,1:T(8,128)(2,1)S(1)}, bf16[256,1024]{0,1:T(8,128)(2,1)S(1)}, u32[]{:S(2)}, u32[]{:S(2)}) collective-permute-start(bf16[256,1024]{0,1:T(8,128)(2,1)S(1)} %bitcast.13), channel_id=1, source_target_pairs={{0,16},{16,0},{32,48},{48,32},{64,80},{80,64},{96,112},{112,96},{1... | collective-permute-start | bytes 1572872 | tf_op jit(solution)/shard_map/ppermute | solution.py:266
  78.0 10.4 %collective-permute-start.2 = (bf16[128,1536]{1,0:T(8,128)(2,1)S(1)}, bf16[128,1536]{1,0:T(8,128)(2,1)S(1)}, u32[]{:S(2)}, u32[]{:S(2)}) collective-permute-start(bf16[128,1536]{1,0:T(8,128)(2,1)S(1)} %convolution_convert_fusion), channel_id=1, source_target_pairs={{0,8},{8,0},{1,9},{9,1},{2,10},{10,2},{3,11},{11,3},{4,12},{12,4},... | collective-permute-start | bytes 1179656 | tf_op jit(solution)/shard_map/ppermute | solution.py:275
  79.1 9.3 %copy-start.1 = (bf16[1024,1536]{1,0:T(8,128)(2,1)S(1)}, bf16[1024,1536]{1,0:T(8,128)(2,1)}, u32[]{:S(2)}) copy-start(bf16[1024,1536]{1,0:T(8,128)(2,1)} %all-gather.2.cloned.1.call-done) | copy-start | bytes 9437188
  81.7 15.1 %collective-permute-start = (bf16[128,1536]{1,0:T(8,128)(2,1)S(1)}, bf16[128,1536]{1,0:T(8,128)(2,1)S(1)}, u32[]{:S(2)}, u32[]{:S(2)}) collective-permute-start(bf16[128,1536]{1,0:T(8,128)(2,1)S(1)} %convolution_convert_fusion.1), channel_id=1, source_target_pairs={{0,8},{8,0},{1,9},{9,1},{2,10},{10,2},{3,11},{11,3},{4,12},{12,4},... | collective-permute-start | bytes 1179656 | tf_op jit(solution)/shard_map/ppermute | solution.py:274
  89.0 10.3 %collective-permute-start.3 = (bf16[128,1536]{1,0:T(8,128)(2,1)S(1)}, bf16[128,1536]{1,0:T(8,128)(2,1)S(1)}, u32[]{:S(2)}, u32[]{:S(2)}) collective-permute-start(bf16[128,1536]{1,0:T(8,128)(2,1)S(1)} %fusion), channel_id=1, source_target_pairs={{0,16},{16,0},{32,48},{48,32},{64,80},{80,64},{96,112},{112,96},{1... | collective-permute-start | bytes 1179656 | tf_op jit(solution)/shard_map/ppermute | solution.py:277
Sparse Core Ops, SparseCore 0:
  9.1 47.5 all-gather.1

commit v11 on v10

--- a/solution.py
+++ b/solution.py
@@ -263,7 +263,6 @@
     weight_half = lax.all_gather(weight_half, "hz", axis=0, tiled=True)
     peers = lax.axis_size("hz")
     mine = got.transpose(1, 0, 2).reshape(tok_dev // peers, peers * HEAD_DIM)
-    theirs = lax.ppermute(mine, "frame", partners)
     block = mine.shape[0] // sides
 
     def project(x, which):
@@ -271,11 +270,16 @@
         return jnp.dot(rows, weight_half, preferred_element_type=jnp.float32)
 
     flip = [(0, 1), (1, 0)]
-    sent_mine = lax.ppermute(project(mine, 1 - side).astype(jnp.bfloat16), "hy", flip)
+    partial_mine = project(mine, 1 - side).astype(jnp.bfloat16)
+    partial_mine, mine = lax.optimization_barrier((partial_mine, mine))
+    sent_mine = lax.ppermute(partial_mine, "hy", flip)
+    theirs = lax.ppermute(mine, "frame", partners)
     sent_theirs = lax.ppermute(project(theirs, 1 - side).astype(jnp.bfloat16), "hy", flip)
-    other = (project(theirs, side) + sent_theirs.astype(jnp.float32)).astype(jnp.bfloat16)
+    own_mine = lax.optimization_barrier(project(mine, side))
+    own_theirs = lax.optimization_barrier(project(theirs, side))
+    other = (own_theirs + sent_theirs.astype(jnp.float32)).astype(jnp.bfloat16)
     other_half = lax.ppermute(other, "frame", partners)
-    own_half = (project(mine, side) + sent_mine.astype(jnp.float32)).astype(jnp.bfloat16)
+    own_half = (own_mine + sent_mine.astype(jnp.float32)).astype(jnp.bfloat16)
     return jnp.where(
         core == 0,
         jnp.concatenate([own_half, other_half], axis=1),

time: 108 us -> 108 us (level)
  matrix products: 9.3 us -> 7.27 us
  waiting for transfers between devices: 13.4 us -> 15.4 us
    dot_general x4, matrix products: 8.25 us -> 6.22 us  [project(): return jnp.dot(rows, weight_half, preferred_element_type=jnp.float32)]
    ppermute x1, waiting for transfers between devices: 6.13 us -> 7.54 us  [on_device(): lax.ppermute(project(theirs, 1 - side).astype(jnp.bfloat16), 'hy', flip)]
  transfers between devices with their start and end apart: 5 -> 5, of which waited for: 3 -> 3; matrix products, arithmetic and copies ran while one was open for 11% -> 7% of each run, Pallas kernels for 55% -> 55%
where the time goes in v11:
time: 108 us; the launch traced here: 107 us
  Pallas kernels  58.8 us (54%)
  waiting for transfers between devices  15.4 us (14%)
  between operations  13.5 us (12%)
  matrix products  7.27 us (7%)
  local copies, waits for them, and re-layouts  4.96 us (5%)
  starting transfers between devices  4.51 us (4%)
  other arithmetic  2.96 us (3%)
    pallas_call x1, Pallas kernels, attend(): pl.pallas_call(attention_kernel, grid=(TROWS, GROUPS), in_specs=[pl.Block...  58.8 us
    ppermute x1, waiting for transfers between devices, on_device(): lax.ppermute(project(theirs, 1 - side).astype(jnp.bfloat16), 'hy', flip)  7.54 us
    ppermute x1, waiting for transfers between devices, on_device(): sent_mine = lax.ppermute(partial_mine, 'hy', flip)  6.28 us
    dot_general x4, matrix products, project(): return jnp.dot(rows, weight_half, preferred_element_type=jnp.float32)  6.22 us
  transfers between devices with their start and end apart: 5, of which 3 were waited for; matrix products, arithmetic and copies ran while one was open for 7% of the time, Pallas kernels for 55%

profile of v11, /device:TPU:17, one launch (start us, length us, event | category | flops | bytes accessed | tf_op | source)
XLA Modules:
  0.0 107.4 jit_solution(13029002123147491244)
XLA Ops:
  6.5 0.0 copy-start
  6.5 0.0 all-gather.2.cloned.1.call-start
  6.5 1.1 %copy-done = bf16[128,3072]{1,0:T(8,128)(2,1)S(1)} copy-done((bf16[128,3072]{1,0:T(8,128)(2,1)S(1)}, bf16[128,3072]{1,0:T(8,128)(2,1)}, u32[]{:S(2)}) %copy-start) | copy-done | bytes 786456
  7.7 0.8 constant_dynamic-slice_fusion
  8.5 0.0 all-gather.2.cloned.1.call-update
  8.5 0.7 convert_bitcast_fusion
  9.2 1.0 fusion.2
  10.3 0.1 reshape.19
  10.4 1.0 fusion.11
  11.5 0.4 broadcast_in_dim.16
  11.9 0.3 reshape.14
  12.1 1.0 copy.14.bias_ref
  13.1 58.8 %shard_map.91 = bf16[8,256,128]{2,1,0:T(8,128)(2,1)} custom-call(bf16[2048,128]{1,0:T(8,128)(2,1)} %q_ref.1, bf16[2048,128]{1,0:T(8,128)(2,1)} %k_ref.1, bf16[2048,128]{1,0:T(8,128)(2,1)} %v_ref.1, f32[16,2,3456]{2,1,0:T(2,128)} %copy.14.bias_ref), custom_call_target="tpu_custom_call" | custom-call | tf_op jit(solution)/shard_map/pallas_call | solution.py:225
  71.9 1.2 %copy.15 = bf16[256,8,128]{0,2,1:T(8,128)(2,1)S(1)} copy(bf16[256,8,128]{2,0,1:T(8,128)(2,1)} %bitcast.16) | data formatting | bytes 1048576 | tf_op jit(solution)/shard_map/transpose | solution.py:265
  73.2 0.0 all-gather.2.cloned.1.call-done
  73.2 2.5 %convolution_convert_fusion.1 = bf16[128,1536]{1,0:T(8,128)(2,1)S(1)} fusion(bf16[1024,1536]{1,0:T(8,128)(2,1)} %all-gather.2.cloned.1.call-done, bf16[256,1024]{0,1:T(8,128)(2,1)S(1)} %bitcast.13, s32[]{:T(128)S(6)} %select_n.33), kind=kOutput, calls=%fused_computation.1 | convolution fusion | flops 402849792 | bytes 3801092 | tf_op jit(solution)/shard_map/dot_general | solution.py:270
  75.7 0.8 collective-permute-start.1
  76.5 0.0 copy-start.1
  76.5 1.5 %collective-permute-done.1 = bf16[256,1024]{0,1:T(8,128)(2,1)S(1)} collective-permute-done((bf16[256,1024]{0,1:T(8,128)(2,1)S(1)}, bf16[256,1024]{0,1:T(8,128)(2,1)S(1)}, u32[]{:S(2)}, u32[]{:S(2)}) %collective-permute-start.1) | collective-permute-done | bytes 524320 | tf_op jit(solution)/shard_map/ppermute | solution.py:276
  78.0 2.5 %convolution_convert_fusion = bf16[128,1536]{1,0:T(8,128)(2,1)S(1)} fusion(bf16[1024,1536]{1,0:T(8,128)(2,1)} %all-gather.2.cloned.1.call-done, bf16[256,1024]{0,1:T(8,128)(2,1)S(1)} %collective-permute-done.1, s32[]{:T(128)S(6)} %select_n.33), kind=kOutput, calls=%fused_computation | convolution fusion | flops 402849792 | bytes 3801092 | tf_op jit(solution)/shard_map/dot_general | solution.py:270
  80.5 1.1 collective-permute-start.2
  81.6 0.0 copy-done.1
  81.6 0.6 fusion.6
  82.2 0.6 collective-permute-start
  82.8 0.6 fusion.4
  83.4 7.5 %collective-permute-done.2 = bf16[128,1536]{1,0:T(8,128)(2,1)S(1)} collective-permute-done((bf16[128,1536]{1,0:T(8,128)(2,1)S(1)}, bf16[128,1536]{1,0:T(8,128)(2,1)S(1)}, u32[]{:S(2)}, u32[]{:S(2)}) %collective-permute-start.2) | collective-permute-done | bytes 393248 | tf_op jit(solution)/shard_map/ppermute | solution.py:277
  91.0 0.1 add_convert_fusion
  91.0 2.1 %collective-permute-start.3 = (bf16[128,1536]{1,0:T(8,128)(2,1)S(1)}, bf16[128,1536]{1,0:T(8,128)(2,1)S(1)}, u32[]{:S(2)}, u32[]{:S(2)}) collective-permute-start(bf16[128,1536]{1,0:T(8,128)(2,1)S(1)} %add_convert_fusion), channel_id=1, source_target_pairs={{0,16},{16,0},{32,48},{48,32},{64,80},{80,64},{96,112},{112,96},{1... | collective-permute-start | bytes 1179656 | tf_op jit(solution)/shard_map/ppermute | solution.py:281
  93.1 6.3 %collective-permute-done = bf16[128,1536]{1,0:T(8,128)(2,1)S(1)} collective-permute-done((bf16[128,1536]{1,0:T(8,128)(2,1)S(1)}, bf16[128,1536]{1,0:T(8,128)(2,1)S(1)}, u32[]{:S(2)}, u32[]{:S(2)}) %collective-permute-start) | collective-permute-done | bytes 393248 | tf_op jit(solution)/shard_map/ppermute | solution.py:275
  99.4 0.1 add_convert_fusion.1
  99.5 0.0 collective-permute-done.3
  99.5 1.1 maximum_select_fusion
  (2 shorter events, 0.0 us)
Async XLA Ops:
  6.5 1.1 %copy-start = (bf16[128,3072]{1,0:T(8,128)(2,1)S(1)}, bf16[128,3072]{1,0:T(8,128)(2,1)}, u32[]{:S(2)}) copy-start(bf16[128,3072]{1,0:T(8,128)(2,1)} %param.13) | copy-start | bytes 2359300
  6.5 66.7 %all-gather.2.cloned.1.call-start = ((), (), s32[]{:S(2)}) async-start(), calls=%async_computation | async-start | bytes 3538944 | tf_op jit(solution)/shard_map/all_gather | solution.py:263
  75.7 2.3 %collective-permute-start.1 = (bf16[256,1024]{0,1:T(8,128)(2,1)S(1)}, bf16[256,1024]{0,1:T(8,128)(2,1)S(1)}, u32[]{:S(2)}, u32[]{:S(2)}) collective-permute-start(bf16[256,1024]{0,1:T(8,128)(2,1)S(1)} %bitcast.14), channel_id=1, source_target_pairs={{0,16},{16,0},{32,48},{48,32},{64,80},{80,64},{96,112},{112,96},{1... | collective-permute-start | bytes 1572872 | tf_op jit(solution)/shard_map/ppermute | solution.py:276
  76.5 5.1 %copy-start.1 = (bf16[1024,1536]{1,0:T(8,128)(2,1)S(1)}, bf16[1024,1536]{1,0:T(8,128)(2,1)}, u32[]{:S(2)}) copy-start(bf16[1024,1536]{1,0:T(8,128)(2,1)} %all-gather.2.cloned.1.call-done) | copy-start | bytes 9437188
  80.5 10.4 %collective-permute-start.2 = (bf16[128,1536]{1,0:T(8,128)(2,1)S(1)}, bf16[128,1536]{1,0:T(8,128)(2,1)S(1)}, u32[]{:S(2)}, u32[]{:S(2)}) collective-permute-start(bf16[128,1536]{1,0:T(8,128)(2,1)S(1)} %convolution_convert_fusion), channel_id=1, source_target_pairs={{0,8},{8,0},{1,9},{9,1},{2,10},{10,2},{3,11},{11,3},{4,12},{12,4},... | collective-permute-start | bytes 1179656 | tf_op jit(solution)/shard_map/ppermute | solution.py:277
  82.2 17.2 %collective-permute-start = (bf16[128,1536]{1,0:T(8,128)(2,1)S(1)}, bf16[128,1536]{1,0:T(8,128)(2,1)S(1)}, u32[]{:S(2)}, u32[]{:S(2)}) collective-permute-start(bf16[128,1536]{1,0:T(8,128)(2,1)S(1)} %convolution_convert_fusion.1), channel_id=1, source_target_pairs={{0,8},{8,0},{1,9},{9,1},{2,10},{10,2},{3,11},{11,3},{4,12},{12,4},... | collective-permute-start | bytes 1179656 | tf_op jit(solution)/shard_map/ppermute | solution.py:275
  91.0 8.4 %collective-permute-start.3 = (bf16[128,1536]{1,0:T(8,128)(2,1)S(1)}, bf16[128,1536]{1,0:T(8,128)(2,1)S(1)}, u32[]{:S(2)}, u32[]{:S(2)}) collective-permute-start(bf16[128,1536]{1,0:T(8,128)(2,1)S(1)} %add_convert_fusion), channel_id=1, source_target_pairs={{0,16},{16,0},{32,48},{48,32},{64,80},{80,64},{96,112},{112,96},{1... | collective-permute-start | bytes 1179656 | tf_op jit(solution)/shard_map/ppermute | solution.py:281
Sparse Core Ops, SparseCore 0:
  9.1 47.5 all-gather.1

commit v12 on v11

--- a/solution.py
+++ b/solution.py
@@ -74,9 +74,9 @@
     return bias.reshape(TROWS * GROUPS, QTILES, ROW_K)
 
 
-def attention_kernel(q_ref, k_ref, v_ref, bias_ref, o_ref,
-                     kp_ref, kn_ref, vp_ref, vn_ref, s_ref, p_ref, att_ref, got_ref,
-                     send_sem, recv_sem, out_send, out_recv):
+def attention_kernel(q_ref, k_ref, v_ref, bias_ref, o_ref, o2_ref,
+                     kp_ref, kn_ref, vp_ref, vn_ref, s_ref, p_ref, att_ref, got_ref, their_ref,
+                     send_sem, recv_sem, out_send, out_recv, pair_send, pair_recv):
     row = pl.program_id(0)
     group = pl.program_id(1)
     frame = lax.axis_index("frame")
@@ -84,6 +84,7 @@
     me = lax.axis_index("hz")
     peers = lax.axis_size("hz")
     mesh = pl.DeviceIdType.MESH
+    partner = frame + 1 - 2 * (frame % 2)
 
     @pl.when((row == 0) & (group == 0))
     def _():
@@ -106,14 +107,17 @@
         for i in range(1, peers):
             other = (frame, side, lax.rem(me + i, peers))
             pl.semaphore_signal(barrier, inc=1, device_id=other, device_id_type=mesh)
+        for j in range(peers):
+            other = (partner, side, j)
+            pl.semaphore_signal(barrier, inc=1, device_id=other, device_id_type=mesh)
 
         @pl.when(has_prev & has_next)
         def _():
-            pl.semaphore_wait(barrier, peers + 1)
+            pl.semaphore_wait(barrier, 2 * peers + 1)
 
         @pl.when(has_prev != has_next)
         def _():
-            pl.semaphore_wait(barrier, peers)
+            pl.semaphore_wait(barrier, 2 * peers)
 
         def push(src, dst, slot, device):
             return pltpu.make_async_remote_copy(
@@ -207,12 +211,27 @@
                 )
                 copy.start()
                 copies.append(copy)
+        for i in range(peers):
+            peer = lax.rem(me + i, peers)
+            for part in range(2):
+                src = pl.multiple_of((part * peers + peer) * chunk, chunk)
+                copy = pltpu.make_async_remote_copy(
+                    src_ref=att_ref.at[pl.ds(src, chunk)],
+                    dst_ref=their_ref.at[me, pl.ds(part * chunk, chunk)],
+                    send_sem=pair_send.at[2 * i + part],
+                    recv_sem=pair_recv.at[2 * i + part],
+                    device_id=(partner, side, peer),
+                    device_id_type=mesh,
+                )
+                copy.start()
+                copies.append(copy)
         for part in range(2):
             src = pl.multiple_of((part * peers + me) * chunk, chunk)
             got_ref[me, pl.ds(part * chunk, chunk), :] = att_ref[pl.ds(src, chunk), :]
         for copy in copies:
             copy.wait()
         o_ref[...] = got_ref[...]
+        o2_ref[...] = their_ref[...]
 
 
 def attend(q, k, v, bias):
@@ -228,15 +247,18 @@
         in_specs=[pl.BlockSpec((BLOCK_Q, HEAD_DIM), lambda r, g: (r * GROUPS + g, 0))]
         + [full] * 2
         + [pl.BlockSpec((1, QTILES, ROW_K), lambda r, g: (r * GROUPS + g, 0, 0))],
-        out_specs=pl.BlockSpec(got_shape, lambda r, g: (0, 0, 0)),
-        out_shape=jax.ShapeDtypeStruct(got_shape, jnp.bfloat16),
+        out_specs=[pl.BlockSpec(got_shape, lambda r, g: (0, 0, 0))] * 2,
+        out_shape=[jax.ShapeDtypeStruct(got_shape, jnp.bfloat16)] * 2,
         scratch_shapes=[frame_kv] * 4 + [
             pltpu.VMEM((BLOCK_Q, ROW_K), jnp.float32),
             pltpu.VMEM((BLOCK_Q, ROW_K), jnp.bfloat16),
             frame_kv,
             got,
+            got,
             pltpu.SemaphoreType.DMA((4,)),
             pltpu.SemaphoreType.DMA((4,)),
+            pltpu.SemaphoreType.DMA((2 * peers,)),
+            pltpu.SemaphoreType.DMA((2 * peers,)),
             pltpu.SemaphoreType.DMA((2 * peers,)),
             pltpu.SemaphoreType.DMA((2 * peers,)),
         ],
@@ -253,7 +275,7 @@
     frame = lax.axis_index("frame") * frames_here
     mask_rows = block_mask.reshape(TROWS * TCOLS, WIN)
     bias = window_bias(mask_rows, frame, frames_total)
-    got = attend(queries, keys, values, bias)
+    got, got_theirs = attend(queries, keys, values, bias)
     core = lax.axis_index("frame") % 2
     side = lax.axis_index("hy")
     sides = lax.axis_size("hy")
@@ -273,7 +295,7 @@
     partial_mine = project(mine, 1 - side).astype(jnp.bfloat16)
     partial_mine, mine = lax.optimization_barrier((partial_mine, mine))
     sent_mine = lax.ppermute(partial_mine, "hy", flip)
-    theirs = lax.ppermute(mine, "frame", partners)
+    theirs = got_theirs.transpose(1, 0, 2).reshape(tok_dev // peers, peers * HEAD_DIM)
     sent_theirs = lax.ppermute(project(theirs, 1 - side).astype(jnp.bfloat16), "hy", flip)
     own_mine = lax.optimization_barrier(project(mine, side))
     own_theirs = lax.optimization_barrier(project(theirs, side))

time: 108 us -> 117 us (1.083)
  Pallas kernels: 58.8 us -> 70.6 us
  matrix products: 7.27 us -> 5.55 us
  waiting for transfers between devices: 15.4 us -> 13.9 us
  starting transfers between devices: 4.51 us -> 3.25 us
  local copies, waits for them, and re-layouts: 4.96 us -> 6.19 us
    pallas_call x1, Pallas kernels: 58.8 us -> 70.6 us  [attend(): pl.pallas_call(attention_kernel, grid=(TROWS, GROUPS), in_specs=[pl.Block...]
    dot_general x4, matrix products: 6.22 us -> 4.5 us  [project(): return jnp.dot(rows, weight_half, preferred_element_type=jnp.float32)]
    ppermute x1 -> x0, waiting for transfers between devices: 1.53 us -> none  [on_device(): theirs = lax.ppermute(mine, 'frame', partners)]
    transpose x0 -> x1, local copies, waits for them, and re-layouts: none -> 1.25 us  [on_device(): got_theirs.transpose(1, 0, 2).reshape(tok_dev // peers, peers * HEAD_DIM)]
  transfers between devices with their start and end apart: 5 -> 4, of which waited for: 3 -> 2; matrix products, arithmetic and copies ran while one was open for 7% -> 8% of each run, Pallas kernels for 55% -> 61%
where the time goes in v12:
time: 117 us; the launch traced here: 116 us
  Pallas kernels  70.6 us (60%)
  waiting for transfers between devices  13.9 us (12%)
  between operations  13.5 us (12%)
  local copies, waits for them, and re-layouts  6.19 us (5%)
  matrix products  5.55 us (5%)
  starting transfers between devices  3.25 us (3%)
  other arithmetic  2.97 us (3%)
    pallas_call x1, Pallas kernels, attend(): pl.pallas_call(attention_kernel, grid=(TROWS, GROUPS), in_specs=[pl.Block...  70.6 us
    ppermute x1, waiting for transfers between devices, on_device(): lax.ppermute(project(theirs, 1 - side).astype(jnp.bfloat16), 'hy', flip)  7.14 us
    ppermute x1, waiting for transfers between devices, on_device(): sent_mine = lax.ppermute(partial_mine, 'hy', flip)  6.75 us
    dot_general x4, matrix products, project(): return jnp.dot(rows, weight_half, preferred_element_type=jnp.float32)  4.5 us
  transfers between devices with their start and end apart: 4, of which 2 were waited for; matrix products, arithmetic and copies ran while one was open for 8% of the time, Pallas kernels for 61%

profile of v12, /device:TPU:17, one launch (start us, length us, event | category | flops | bytes accessed | tf_op | source)
XLA Modules:
  0.0 116.0 jit_solution(8278680752857774374)
XLA Ops:
  6.5 0.0 copy-start
  6.5 0.0 all-gather.2.cloned.1.call-start
  6.5 1.1 copy-done
  7.7 0.8 constant_dynamic-slice_fusion
  8.4 0.0 all-gather.2.cloned.1.call-update
  8.5 0.7 convert_bitcast_fusion
  9.2 1.0 fusion.2
  10.3 0.1 reshape.23
  10.4 1.0 fusion.11
  11.5 0.4 broadcast_in_dim.16
  11.8 0.3 reshape.17
  12.1 1.0 copy.14.bias_ref
  13.1 70.6 %shard_map.91 = (bf16[8,256,128]{2,1,0:T(8,128)(2,1)}, bf16[8,256,128]{2,1,0:T(8,128)(2,1)}) custom-call(bf16[2048,128]{1,0:T(8,128)(2,1)} %q_ref.1, bf16[2048,128]{1,0:T(8,128)(2,1)} %k_ref.1, bf16[2048,128]{1,0:T(8,128)(2,1)} %v_ref.1, f32[16,2,3456]{2,1,0:T(2,128)} %copy.14.bias_ref), custom_call_target="tpu_custom_call" | custom-call | tf_op jit(solution)/shard_map/pallas_call | solution.py:244
  83.7 1.2 %copy.16 = bf16[256,8,128]{0,2,1:T(8,128)(2,1)S(1)} copy(bf16[256,8,128]{2,0,1:T(8,128)(2,1)} %bitcast.20) | data formatting | bytes 1048576 | tf_op jit(solution)/shard_map/transpose | solution.py:298
  84.9 1.2 %copy.15 = bf16[256,8,128]{0,2,1:T(8,128)(2,1)S(1)} copy(bf16[256,8,128]{2,0,1:T(8,128)(2,1)} %bitcast.19) | data formatting | bytes 1048576 | tf_op jit(solution)/shard_map/transpose | solution.py:287
  86.2 0.0 all-gather.2.cloned.1.call-done
  86.2 0.0 copy-start.1
  86.2 2.6 %convolution_convert_fusion = bf16[128,1536]{1,0:T(8,128)(2,1)S(1)} fusion(bf16[1024,1536]{1,0:T(8,128)(2,1)} %all-gather.2.cloned.1.call-done, bf16[256,1024]{0,1:T(8,128)(2,1)S(1)} %bitcast.17, s32[]{:T(128)S(6)} %select_n.33), kind=kOutput, calls=%fused_computation | convolution fusion | flops 402849792 | bytes 3801092 | tf_op jit(solution)/shard_map/dot_general | solution.py:292
  88.9 1.1 collective-permute-start.1
  90.0 0.0 copy-done.1
  90.0 0.6 fusion.4
  90.6 0.6 convolution_convert_fusion.1
  91.2 0.6 fusion.6
  91.8 0.5 collective-permute-start
  92.4 7.1 %collective-permute-done.1 = bf16[128,1536]{1,0:T(8,128)(2,1)S(1)} collective-permute-done((bf16[128,1536]{1,0:T(8,128)(2,1)S(1)}, bf16[128,1536]{1,0:T(8,128)(2,1)S(1)}, u32[]{:S(2)}, u32[]{:S(2)}) %collective-permute-start.1) | collective-permute-done | bytes 393248 | tf_op jit(solution)/shard_map/ppermute | solution.py:299
  99.5 0.1 add_convert_fusion
  99.6 1.6 %collective-permute-start.2 = (bf16[128,1536]{1,0:T(8,128)(2,1)S(1)}, bf16[128,1536]{1,0:T(8,128)(2,1)S(1)}, u32[]{:S(2)}, u32[]{:S(2)}) collective-permute-start(bf16[128,1536]{1,0:T(8,128)(2,1)S(1)} %add_convert_fusion), channel_id=1, source_target_pairs={{0,16},{16,0},{32,48},{48,32},{64,80},{80,64},{96,112},{112,96},{1... | collective-permute-start | bytes 1179656 | tf_op jit(solution)/shard_map/ppermute | solution.py:303
  101.2 6.7 %collective-permute-done = bf16[128,1536]{1,0:T(8,128)(2,1)S(1)} collective-permute-done((bf16[128,1536]{1,0:T(8,128)(2,1)S(1)}, bf16[128,1536]{1,0:T(8,128)(2,1)S(1)}, u32[]{:S(2)}, u32[]{:S(2)}) %collective-permute-start) | collective-permute-done | bytes 393248 | tf_op jit(solution)/shard_map/ppermute | solution.py:297
  108.0 0.1 add_convert_fusion.1
  108.0 0.0 collective-permute-done.2
  108.1 1.1 maximum_select_fusion
  (2 shorter events, 0.0 us)
Async XLA Ops:
  6.5 1.1 copy-start
  6.5 79.7 %all-gather.2.cloned.1.call-start = ((), (), s32[]{:S(2)}) async-start(), calls=%async_computation | async-start | bytes 3538944 | tf_op jit(solution)/shard_map/all_gather | solution.py:285
  86.2 3.8 %copy-start.1 = (bf16[1024,1536]{1,0:T(8,128)(2,1)S(1)}, bf16[1024,1536]{1,0:T(8,128)(2,1)}, u32[]{:S(2)}) copy-start(bf16[1024,1536]{1,0:T(8,128)(2,1)} %all-gather.2.cloned.1.call-done) | copy-start | bytes 9437188
  88.9 10.7 %collective-permute-start.1 = (bf16[128,1536]{1,0:T(8,128)(2,1)S(1)}, bf16[128,1536]{1,0:T(8,128)(2,1)S(1)}, u32[]{:S(2)}, u32[]{:S(2)}) collective-permute-start(bf16[128,1536]{1,0:T(8,128)(2,1)S(1)} %convolution_convert_fusion), channel_id=1, source_target_pairs={{0,8},{8,0},{1,9},{9,1},{2,10},{10,2},{3,11},{11,3},{4,12},{12,4},... | collective-permute-start | bytes 1179656 | tf_op jit(solution)/shard_map/ppermute | solution.py:299
  91.8 16.1 %collective-permute-start = (bf16[128,1536]{1,0:T(8,128)(2,1)S(1)}, bf16[128,1536]{1,0:T(8,128)(2,1)S(1)}, u32[]{:S(2)}, u32[]{:S(2)}) collective-permute-start(bf16[128,1536]{1,0:T(8,128)(2,1)S(1)} %convolution_convert_fusion.1), channel_id=1, source_target_pairs={{0,8},{8,0},{1,9},{9,1},{2,10},{10,2},{3,11},{11,3},{4,12},{12,4},... | collective-permute-start | bytes 1179656 | tf_op jit(solution)/shard_map/ppermute | solution.py:297
  99.6 8.4 %collective-permute-start.2 = (bf16[128,1536]{1,0:T(8,128)(2,1)S(1)}, bf16[128,1536]{1,0:T(8,128)(2,1)S(1)}, u32[]{:S(2)}, u32[]{:S(2)}) collective-permute-start(bf16[128,1536]{1,0:T(8,128)(2,1)S(1)} %add_convert_fusion), channel_id=1, source_target_pairs={{0,16},{16,0},{32,48},{48,32},{64,80},{80,64},{96,112},{112,96},{1... | collective-permute-start | bytes 1179656 | tf_op jit(solution)/shard_map/ppermute | solution.py:303
Sparse Core Ops, SparseCore 0:
  9.1 47.5 all-gather.1

commit v13 on v11

--- a/solution.py
+++ b/solution.py
@@ -270,11 +270,9 @@
         return jnp.dot(rows, weight_half, preferred_element_type=jnp.float32)
 
     flip = [(0, 1), (1, 0)]
-    partial_mine = project(mine, 1 - side).astype(jnp.bfloat16)
-    partial_mine, mine = lax.optimization_barrier((partial_mine, mine))
-    sent_mine = lax.ppermute(partial_mine, "hy", flip)
     theirs = lax.ppermute(mine, "frame", partners)
-    sent_theirs = lax.ppermute(project(theirs, 1 - side).astype(jnp.bfloat16), "hy", flip)
+    partials = jnp.stack([project(mine, 1 - side), project(theirs, 1 - side)]).astype(jnp.bfloat16)
+    sent_mine, sent_theirs = lax.ppermute(partials, "hy", flip)
     own_mine = lax.optimization_barrier(project(mine, side))
     own_theirs = lax.optimization_barrier(project(theirs, side))
     other = (own_theirs + sent_theirs.astype(jnp.float32)).astype(jnp.bfloat16)

time: 108 us -> 107 us (level)
  starting transfers between devices: 4.51 us -> 2.77 us
    ppermute x1, waiting for transfers between devices: 1.53 us -> 0.01 us  [on_device(): theirs = lax.ppermute(mine, 'frame', partners)]
    ppermute x1, waiting for transfers between devices: 0.01 us -> 1.35 us  [on_device(): other_half = lax.ppermute(other, 'frame', partners)]
    ppermute x1, starting transfers between devices: 2.08 us -> 0.92 us  [on_device(): other_half = lax.ppermute(other, 'frame', partners)]
    ppermute x2 -> x1, waiting for transfers between devices: 13.8 us -> 14.7 us  [on_device(): sent_mine, sent_theirs = lax.ppermute(partials, 'hy', flip)]
  transfers between devices with their start and end apart: 5 -> 4, of which waited for: 3 -> 2; matrix products, arithmetic and copies ran while one was open for 7% -> 11% of each run, Pallas kernels for 55% -> 55%
where the time goes in v13:
time: 107 us
  Pallas kernels  58.8 us (55%)
  waiting for transfers between devices  16.1 us (15%)
  between operations  13.5 us (13%)
  matrix products  7.56 us (7%)
  local copies, waits for them, and re-layouts  5.31 us (5%)
  other arithmetic  3.07 us (3%)
  starting transfers between devices  2.77 us (3%)
    pallas_call x1, Pallas kernels, attend(): pl.pallas_call(attention_kernel, grid=(TROWS, GROUPS), in_specs=[pl.Block...  58.8 us
    ppermute x1, waiting for transfers between devices, on_device(): sent_mine, sent_theirs = lax.ppermute(partials, 'hy', flip)  14.7 us
    dot_general x4, matrix products, project(): return jnp.dot(rows, weight_half, preferred_element_type=jnp.float32)  6.51 us
  transfers between devices with their start and end apart: 4, of which 2 were waited for; matrix products, arithmetic and copies ran while one was open for 11% of the time, Pallas kernels for 55%

profile of v13, /device:TPU:17, one launch (start us, length us, event | category | flops | bytes accessed | tf_op | source)
XLA Modules:
  0.0 107.1 jit_solution(6589204041972098605)
XLA Ops:
  6.5 0.0 copy-start
  6.5 0.0 all-gather.2.cloned.1.call-start
  6.5 1.1 %copy-done = bf16[128,3072]{1,0:T(8,128)(2,1)S(1)} copy-done((bf16[128,3072]{1,0:T(8,128)(2,1)S(1)}, bf16[128,3072]{1,0:T(8,128)(2,1)}, u32[]{:S(2)}) %copy-start) | copy-done | bytes 786456
  7.7 0.8 constant_dynamic-slice_fusion
  8.4 0.0 all-gather.2.cloned.1.call-update
  8.5 0.7 convert_bitcast_fusion
  9.2 1.0 fusion.4
  10.3 0.1 reshape.25
  10.4 1.0 fusion.15
  11.5 0.4 broadcast_in_dim.16
  11.8 0.3 reshape.18
  12.1 1.0 copy.14.bias_ref
  13.1 58.8 %shard_map.91 = bf16[8,256,128]{2,1,0:T(8,128)(2,1)} custom-call(bf16[2048,128]{1,0:T(8,128)(2,1)} %q_ref.1, bf16[2048,128]{1,0:T(8,128)(2,1)} %k_ref.1, bf16[2048,128]{1,0:T(8,128)(2,1)} %v_ref.1, f32[16,2,3456]{2,1,0:T(2,128)} %copy.14.bias_ref), custom_call_target="tpu_custom_call" | custom-call | tf_op jit(solution)/shard_map/pallas_call | solution.py:225
  71.9 1.2 %copy.15 = bf16[256,8,128]{0,2,1:T(8,128)(2,1)S(1)} copy(bf16[256,8,128]{2,0,1:T(8,128)(2,1)} %bitcast.30) | data formatting | bytes 1048576 | tf_op jit(solution)/shard_map/transpose | solution.py:265
  73.2 0.8 collective-permute-start
  73.9 0.0 all-gather.2.cloned.1.call-done
  73.9 0.0 copy-start.1
  73.9 2.6 %fusion = bf16[1,128,1536]{2,1,0:T(8,128)(2,1)S(1)} fusion(bf16[1024,1536]{1,0:T(8,128)(2,1)} %all-gather.2.cloned.1.call-done, bf16[256,1024]{0,1:T(8,128)(2,1)S(1)} %bitcast.28, s32[]{:T(128)S(6)} %select_n.35), kind=kOutput, calls=%fused_computation.2 | convolution fusion | flops 402849792 | bytes 3801092 | tf_op jit(solution)/shard_map/dot_general | solution.py:270
  76.6 0.0 collective-permute-done
  76.6 0.2 copy-done.1
  76.8 0.6 fusion.1
  77.4 0.1 pad_maximum_fusion
  77.5 1.1 %collective-permute-start.1 = (bf16[2,128,1536]{2,1,0:T(8,128)(2,1)S(1)}, bf16[2,128,1536]{2,1,0:T(8,128)(2,1)S(1)}, u32[]{:S(2)}, u32[]{:S(2)}) collective-permute-start(bf16[2,128,1536]{2,1,0:T(8,128)(2,1)S(1)} %pad_maximum_fusion), channel_id=1, source_target_pairs={{0,8},{8,0},{1,9},{9,1},{2,10},{10,2},{3,11},{11,3},{4,12},{12,4},... | collective-permute-start | bytes 2359304 | tf_op jit(solution)/shard_map/ppermute | solution.py:275
  78.6 0.0 copy-start.2
  78.6 2.6 %fusion.11 = f32[128,1536]{1,0:T(8,128)S(1)} fusion(bf16[1024,1536]{1,0:T(8,128)(2,1)} %all-gather.2.cloned.1.call-done, bf16[256,1024]{0,1:T(8,128)(2,1)S(1)} %bitcast.29, s32[]{:T(128)S(6)} %select_n.33), kind=kOutput, calls=%fused_computation.22 | convolution fusion | flops 402653184 | bytes 4194308 | tf_op jit(solution)/shard_map/dot_general | solution.py:270
  81.2 0.2 copy-done.2
  81.4 0.6 fusion.7
  82.0 14.7 %collective-permute-done.1 = bf16[2,128,1536]{2,1,0:T(8,128)(2,1)S(1)} collective-permute-done((bf16[2,128,1536]{2,1,0:T(8,128)(2,1)S(1)}, bf16[2,128,1536]{2,1,0:T(8,128)(2,1)S(1)}, u32[]{:S(2)}, u32[]{:S(2)}) %collective-permute-start.1) | collective-permute-done | bytes 786464 | tf_op jit(solution)/shard_map/ppermute | solution.py:275
  96.7 0.2 fusion.6
  96.9 0.9 collective-permute-start.2
  97.8 1.3 %collective-permute-done.2 = bf16[128,1536]{1,0:T(8,128)(2,1)S(1)} collective-permute-done((bf16[128,1536]{1,0:T(8,128)(2,1)S(1)}, bf16[128,1536]{1,0:T(8,128)(2,1)S(1)}, u32[]{:S(2)}, u32[]{:S(2)}) %collective-permute-start.2) | collective-permute-done | bytes 393248 | tf_op jit(solution)/shard_map/ppermute | solution.py:279
  99.2 1.1 maximum_select_fusion
  (2 shorter events, 0.0 us)
Async XLA Ops:
  6.5 1.1 %copy-start = (bf16[128,3072]{1,0:T(8,128)(2,1)S(1)}, bf16[128,3072]{1,0:T(8,128)(2,1)}, u32[]{:S(2)}) copy-start(bf16[128,3072]{1,0:T(8,128)(2,1)} %param.13) | copy-start | bytes 2359300
  6.5 67.4 %all-gather.2.cloned.1.call-start = ((), (), s32[]{:S(2)}) async-start(), calls=%async_computation | async-start | bytes 3538944 | tf_op jit(solution)/shard_map/all_gather | solution.py:263
  73.2 3.4 %collective-permute-start = (bf16[256,1024]{0,1:T(8,128)(2,1)S(1)}, bf16[256,1024]{0,1:T(8,128)(2,1)S(1)}, u32[]{:S(2)}, u32[]{:S(2)}) collective-permute-start(bf16[256,1024]{0,1:T(8,128)(2,1)S(1)} %bitcast.27), channel_id=1, source_target_pairs={{0,16},{16,0},{32,48},{48,32},{64,80},{80,64},{96,112},{112,96},{1... | collective-permute-start | bytes 1572872 | tf_op jit(solution)/shard_map/ppermute | solution.py:273
  73.9 2.8 %copy-start.1 = (bf16[1024,1536]{1,0:T(8,128)(2,1)S(1)}, bf16[1024,1536]{1,0:T(8,128)(2,1)}, u32[]{:S(2)}) copy-start(bf16[1024,1536]{1,0:T(8,128)(2,1)} %all-gather.2.cloned.1.call-done) | copy-start | bytes 9437188
  77.5 19.2 %collective-permute-start.1 = (bf16[2,128,1536]{2,1,0:T(8,128)(2,1)S(1)}, bf16[2,128,1536]{2,1,0:T(8,128)(2,1)S(1)}, u32[]{:S(2)}, u32[]{:S(2)}) collective-permute-start(bf16[2,128,1536]{2,1,0:T(8,128)(2,1)S(1)} %pad_maximum_fusion), channel_id=1, source_target_pairs={{0,8},{8,0},{1,9},{9,1},{2,10},{10,2},{3,11},{11,3},{4,12},{12,4},... | collective-permute-start | bytes 2359304 | tf_op jit(solution)/shard_map/ppermute | solution.py:275
  78.6 2.8 %copy-start.2 = (bf16[1024,1536]{1,0:T(8,128)(2,1)S(1)}, bf16[1024,1536]{1,0:T(8,128)(2,1)}, u32[]{:S(2)}) copy-start(bf16[1024,1536]{1,0:T(8,128)(2,1)} %all-gather.2.cloned.1.call-done) | copy-start | bytes 9437188
  96.9 2.3 %collective-permute-start.2 = (bf16[128,1536]{1,0:T(8,128)(2,1)S(1)}, bf16[128,1536]{1,0:T(8,128)(2,1)S(1)}, u32[]{:S(2)}, u32[]{:S(2)}) collective-permute-start(bf16[128,1536]{1,0:T(8,128)(2,1)S(1)} %get-tuple-element.6), channel_id=1, source_target_pairs={{0,16},{16,0},{32,48},{48,32},{64,80},{80,64},{96,112},{112,96},{1... | collective-permute-start | bytes 1179656 | tf_op jit(solution)/shard_map/ppermute | solution.py:279
Sparse Core Ops, SparseCore 0:
  9.1 47.6 all-gather.1

commit v14 on v13

--- a/solution.py
+++ b/solution.py
@@ -173,19 +173,21 @@
             q, k, (((1,), (1,)), ((), ())), preferred_element_type=jnp.float32
         )
     scale = 1.0 / math.sqrt(HEAD_DIM)
+    inverse = []
     for a in range(QTILES):
         rows = slice(a * TILE, (a + 1) * TILE)
-        scores = s_ref[rows, :] * scale + bias_ref[0, a:a + 1, :]
+        scores = s_ref[rows, :] + bias_ref[0, a:a + 1, :]
         peak = jnp.max(scores, axis=1, keepdims=True)
-        expos = jnp.exp(scores - peak)
-        total = jnp.sum(expos, axis=1, keepdims=True)
-        p_ref[rows, :] = (expos * (1.0 / total)).astype(jnp.bfloat16)
+        expos = jnp.exp((scores - peak) * scale)
+        inverse.append(1.0 / jnp.sum(expos, axis=1, keepdims=True))
+        p_ref[rows, :] = expos.astype(jnp.bfloat16)
     acc = jnp.zeros((BLOCK_Q, HEAD_DIM), jnp.float32)
     for seg in range(SEGS):
         df, dr = divmod(seg, 3)
         v = value_refs[df][pl.ds(bases[seg], SEG_K), :]
         acc += jnp.dot(p_ref[:, seg * SEG_K:(seg + 1) * SEG_K], v,
                        preferred_element_type=jnp.float32)
+    acc = acc * jnp.concatenate(inverse, axis=0)
     att_ref[pl.ds(pl.multiple_of((row * GROUPS + group) * BLOCK_Q, BLOCK_Q), BLOCK_Q), :] = (
         acc.astype(att_ref.dtype))
 

time: 107 us -> 107 us (level)
  no operation moved by 1% of the time
where the time goes in v14:
time: 107 us
  Pallas kernels  58.7 us (55%)
  waiting for transfers between devices  16.1 us (15%)
  between operations  13.5 us (13%)
  matrix products  7.56 us (7%)
  local copies, waits for them, and re-layouts  5.31 us (5%)
  other arithmetic  3.07 us (3%)
  starting transfers between devices  2.77 us (3%)
    pallas_call x1, Pallas kernels, attend(): pl.pallas_call(attention_kernel, grid=(TROWS, GROUPS), in_specs=[pl.Block...  58.7 us
    ppermute x1, waiting for transfers between devices, on_device(): sent_mine, sent_theirs = lax.ppermute(partials, 'hy', flip)  14.7 us
    dot_general x4, matrix products, project(): return jnp.dot(rows, weight_half, preferred_element_type=jnp.float32)  6.52 us
  transfers between devices with their start and end apart: 4, of which 2 were waited for; matrix products, arithmetic and copies ran while one was open for 11% of the time, Pallas kernels for 55%

profile of v14, /device:TPU:17, one launch (start us, length us, event | category | flops | bytes accessed | tf_op | source)
XLA Modules:
  0.0 107.0 jit_solution(11447908228526232680)
XLA Ops:
  6.5 0.0 copy-start
  6.5 0.0 all-gather.2.cloned.1.call-start
  6.5 1.1 %copy-done = bf16[128,3072]{1,0:T(8,128)(2,1)S(1)} copy-done((bf16[128,3072]{1,0:T(8,128)(2,1)S(1)}, bf16[128,3072]{1,0:T(8,128)(2,1)}, u32[]{:S(2)}) %copy-start) | copy-done | bytes 786456
  7.7 0.8 constant_dynamic-slice_fusion
  8.4 0.0 all-gather.2.cloned.1.call-update
  8.5 0.7 convert_bitcast_fusion
  9.2 1.0 fusion.4
  10.3 0.1 reshape.25
  10.4 1.0 fusion.15
  11.5 0.4 broadcast_in_dim.16
  11.8 0.3 reshape.18
  12.1 1.0 copy.14.bias_ref
  13.1 58.7 %shard_map.91 = bf16[8,256,128]{2,1,0:T(8,128)(2,1)} custom-call(bf16[2048,128]{1,0:T(8,128)(2,1)} %q_ref.1, bf16[2048,128]{1,0:T(8,128)(2,1)} %k_ref.1, bf16[2048,128]{1,0:T(8,128)(2,1)} %v_ref.1, f32[16,2,3456]{2,1,0:T(2,128)} %copy.14.bias_ref), custom_call_target="tpu_custom_call" | custom-call | tf_op jit(solution)/shard_map/pallas_call | solution.py:227
  71.8 1.2 %copy.15 = bf16[256,8,128]{0,2,1:T(8,128)(2,1)S(1)} copy(bf16[256,8,128]{2,0,1:T(8,128)(2,1)} %bitcast.30) | data formatting | bytes 1048576 | tf_op jit(solution)/shard_map/transpose | solution.py:267
  73.1 0.8 collective-permute-start
  73.8 0.0 all-gather.2.cloned.1.call-done
  73.8 0.0 copy-start.1
  73.8 2.6 %fusion = bf16[1,128,1536]{2,1,0:T(8,128)(2,1)S(1)} fusion(bf16[1024,1536]{1,0:T(8,128)(2,1)} %all-gather.2.cloned.1.call-done, bf16[256,1024]{0,1:T(8,128)(2,1)S(1)} %bitcast.28, s32[]{:T(128)S(6)} %select_n.35), kind=kOutput, calls=%fused_computation.2 | convolution fusion | flops 402849792 | bytes 3801092 | tf_op jit(solution)/shard_map/dot_general | solution.py:272
  76.5 0.0 collective-permute-done
  76.5 0.2 copy-done.1
  76.7 0.6 fusion.1
  77.3 0.1 pad_maximum_fusion
  77.4 1.1 %collective-permute-start.1 = (bf16[2,128,1536]{2,1,0:T(8,128)(2,1)S(1)}, bf16[2,128,1536]{2,1,0:T(8,128)(2,1)S(1)}, u32[]{:S(2)}, u32[]{:S(2)}) collective-permute-start(bf16[2,128,1536]{2,1,0:T(8,128)(2,1)S(1)} %pad_maximum_fusion), channel_id=1, source_target_pairs={{0,8},{8,0},{1,9},{9,1},{2,10},{10,2},{3,11},{11,3},{4,12},{12,4},... | collective-permute-start | bytes 2359304 | tf_op jit(solution)/shard_map/ppermute | solution.py:277
  78.5 0.0 copy-start.2
  78.5 2.6 %fusion.11 = f32[128,1536]{1,0:T(8,128)S(1)} fusion(bf16[1024,1536]{1,0:T(8,128)(2,1)} %all-gather.2.cloned.1.call-done, bf16[256,1024]{0,1:T(8,128)(2,1)S(1)} %bitcast.29, s32[]{:T(128)S(6)} %select_n.33), kind=kOutput, calls=%fused_computation.22 | convolution fusion | flops 402653184 | bytes 4194308 | tf_op jit(solution)/shard_map/dot_general | solution.py:272
  81.1 0.2 copy-done.2
  81.3 0.6 fusion.7
  81.9 14.7 %collective-permute-done.1 = bf16[2,128,1536]{2,1,0:T(8,128)(2,1)S(1)} collective-permute-done((bf16[2,128,1536]{2,1,0:T(8,128)(2,1)S(1)}, bf16[2,128,1536]{2,1,0:T(8,128)(2,1)S(1)}, u32[]{:S(2)}, u32[]{:S(2)}) %collective-permute-start.1) | collective-permute-done | bytes 786464 | tf_op jit(solution)/shard_map/ppermute | solution.py:277
  96.6 0.2 fusion.6
  96.8 0.9 collective-permute-start.2
  97.7 1.3 %collective-permute-done.2 = bf16[128,1536]{1,0:T(8,128)(2,1)S(1)} collective-permute-done((bf16[128,1536]{1,0:T(8,128)(2,1)S(1)}, bf16[128,1536]{1,0:T(8,128)(2,1)S(1)}, u32[]{:S(2)}, u32[]{:S(2)}) %collective-permute-start.2) | collective-permute-done | bytes 393248 | tf_op jit(solution)/shard_map/ppermute | solution.py:281
  99.1 1.1 maximum_select_fusion
  (2 shorter events, 0.0 us)
Async XLA Ops:
  6.5 1.1 %copy-start = (bf16[128,3072]{1,0:T(8,128)(2,1)S(1)}, bf16[128,3072]{1,0:T(8,128)(2,1)}, u32[]{:S(2)}) copy-start(bf16[128,3072]{1,0:T(8,128)(2,1)} %param.13) | copy-start | bytes 2359300
  6.5 67.3 %all-gather.2.cloned.1.call-start = ((), (), s32[]{:S(2)}) async-start(), calls=%async_computation | async-start | bytes 3538944 | tf_op jit(solution)/shard_map/all_gather | solution.py:265
  73.1 3.4 %collective-permute-start = (bf16[256,1024]{0,1:T(8,128)(2,1)S(1)}, bf16[256,1024]{0,1:T(8,128)(2,1)S(1)}, u32[]{:S(2)}, u32[]{:S(2)}) collective-permute-start(bf16[256,1024]{0,1:T(8,128)(2,1)S(1)} %bitcast.27), channel_id=1, source_target_pairs={{0,16},{16,0},{32,48},{48,32},{64,80},{80,64},{96,112},{112,96},{1... | collective-permute-start | bytes 1572872 | tf_op jit(solution)/shard_map/ppermute | solution.py:275
  73.8 2.8 %copy-start.1 = (bf16[1024,1536]{1,0:T(8,128)(2,1)S(1)}, bf16[1024,1536]{1,0:T(8,128)(2,1)}, u32[]{:S(2)}) copy-start(bf16[1024,1536]{1,0:T(8,128)(2,1)} %all-gather.2.cloned.1.call-done) | copy-start | bytes 9437188
  77.4 19.2 %collective-permute-start.1 = (bf16[2,128,1536]{2,1,0:T(8,128)(2,1)S(1)}, bf16[2,128,1536]{2,1,0:T(8,128)(2,1)S(1)}, u32[]{:S(2)}, u32[]{:S(2)}) collective-permute-start(bf16[2,128,1536]{2,1,0:T(8,128)(2,1)S(1)} %pad_maximum_fusion), channel_id=1, source_target_pairs={{0,8},{8,0},{1,9},{9,1},{2,10},{10,2},{3,11},{11,3},{4,12},{12,4},... | collective-permute-start | bytes 2359304 | tf_op jit(solution)/shard_map/ppermute | solution.py:277
  78.5 2.8 %copy-start.2 = (bf16[1024,1536]{1,0:T(8,128)(2,1)S(1)}, bf16[1024,1536]{1,0:T(8,128)(2,1)}, u32[]{:S(2)}) copy-start(bf16[1024,1536]{1,0:T(8,128)(2,1)} %all-gather.2.cloned.1.call-done) | copy-start | bytes 9437188
  96.8 2.3 %collective-permute-start.2 = (bf16[128,1536]{1,0:T(8,128)(2,1)S(1)}, bf16[128,1536]{1,0:T(8,128)(2,1)S(1)}, u32[]{:S(2)}, u32[]{:S(2)}) collective-permute-start(bf16[128,1536]{1,0:T(8,128)(2,1)S(1)} %get-tuple-element.6), channel_id=1, source_target_pairs={{0,16},{16,0},{32,48},{48,32},{64,80},{80,64},{96,112},{112,96},{1... | collective-permute-start | bytes 1179656 | tf_op jit(solution)/shard_map/ppermute | solution.py:281
Sparse Core Ops, SparseCore 0:
  9.1 47.5 all-gather.1

commit v15 on v14

--- a/solution.py
+++ b/solution.py
@@ -188,32 +188,40 @@
         acc += jnp.dot(p_ref[:, seg * SEG_K:(seg + 1) * SEG_K], v,
                        preferred_element_type=jnp.float32)
     acc = acc * jnp.concatenate(inverse, axis=0)
-    att_ref[pl.ds(pl.multiple_of((row * GROUPS + group) * BLOCK_Q, BLOCK_Q), BLOCK_Q), :] = (
+    block = row * GROUPS + group
+    att_ref[pl.ds(pl.multiple_of(block * BLOCK_Q, BLOCK_Q), BLOCK_Q), :] = (
         acc.astype(att_ref.dtype))
+    chunk = got_ref.shape[1] // 2
+    assert chunk == BLOCK_Q
+    part = block // peers
+    owner = block % peers
+    distance = (owner - me + peers) % peers
+    src = att_ref.at[pl.ds(pl.multiple_of(block * BLOCK_Q, BLOCK_Q), chunk)]
+
+    def send(i, which, peer, source):
+        return pltpu.make_async_remote_copy(
+            src_ref=source,
+            dst_ref=got_ref.at[me, pl.ds(pl.multiple_of(which * chunk, chunk), chunk)],
+            send_sem=out_send.at[2 * i + which],
+            recv_sem=out_recv.at[2 * i + which],
+            device_id=(frame, side, peer),
+            device_id_type=mesh,
+        )
+
+    @pl.when(distance == 0)
+    def _():
+        got_ref[me, pl.ds(pl.multiple_of(part * chunk, chunk), chunk), :] = src[...]
+
+    @pl.when(distance != 0)
+    def _():
+        send(distance, part, owner, src).start()
 
     @pl.when((row == TROWS - 1) & (group == GROUPS - 1))
     def _():
-        chunk = got_ref.shape[1] // 2
-        copies = []
         for i in range(1, peers):
             peer = lax.rem(me + i, peers)
-            for part in range(2):
-                src = pl.multiple_of((part * peers + peer) * chunk, chunk)
-                copy = pltpu.make_async_remote_copy(
-                    src_ref=att_ref.at[pl.ds(src, chunk)],
-                    dst_ref=got_ref.at[me, pl.ds(part * chunk, chunk)],
-                    send_sem=out_send.at[2 * i + part],
-                    recv_sem=out_recv.at[2 * i + part],
-                    device_id=(frame, side, peer),
-                    device_id_type=mesh,
-                )
-                copy.start()
-                copies.append(copy)
-        for part in range(2):
-            src = pl.multiple_of((part * peers + me) * chunk, chunk)
-            got_ref[me, pl.ds(part * chunk, chunk), :] = att_ref[pl.ds(src, chunk), :]
-        for copy in copies:
-            copy.wait()
+            for which in range(2):
+                send(i, which, peer, src).wait()
         o_ref[...] = got_ref[...]
 
 

time: 107 us -> 104 us (0.972); the launches traced: 107 us -> 102 us
  Pallas kernels: 58.7 us -> 50.7 us
  starting transfers between devices: 2.77 us -> 6.03 us
    pallas_call x1, Pallas kernels: 58.7 us -> 50.7 us  [attend(): pl.pallas_call(attention_kernel, grid=(TROWS, GROUPS), in_specs=[pl.Block...]
    all_gather x1, waiting for transfers between devices: 0.01 us -> 2.8 us  [on_device(): weight_half = lax.all_gather(weight_half, 'hz', axis=0, tiled=True)]
    ppermute x1, waiting for transfers between devices: 14.7 us -> 12 us  [on_device(): sent_mine, sent_theirs = lax.ppermute(partials, 'hy', flip)]
    ppermute x1, starting transfers between devices: 0.92 us -> 3.41 us  [on_device(): other_half = lax.ppermute(other, 'frame', partners)]
  transfers between devices with their start and end apart: 4 -> 4, of which waited for: 2 -> 3; matrix products, arithmetic and copies ran while one was open for 11% -> 11% of each run, Pallas kernels for 55% -> 50%
where the time goes in v15:
time: 104 us; the launch traced here: 102 us
  Pallas kernels  50.7 us (49%)
  waiting for transfers between devices  16.2 us (16%)
  between operations  13.5 us (13%)
  matrix products  7.55 us (7%)
  starting transfers between devices  6.03 us (6%)
  local copies, waits for them, and re-layouts  5.33 us (5%)
  other arithmetic  3.07 us (3%)
    pallas_call x1, Pallas kernels, attend(): pl.pallas_call(attention_kernel, grid=(TROWS, GROUPS), in_specs=[pl.Block...  50.7 us
    ppermute x1, waiting for transfers between devices, on_device(): sent_mine, sent_theirs = lax.ppermute(partials, 'hy', flip)  12 us
    dot_general x4, matrix products, project(): return jnp.dot(rows, weight_half, preferred_element_type=jnp.float32)  6.5 us
    ppermute x1, starting transfers between devices, on_device(): other_half = lax.ppermute(other, 'frame', partners)  3.41 us
    all_gather x1, waiting for transfers between devices, on_device(): weight_half = lax.all_gather(weight_half, 'hz', axis=0, tiled=True)  2.8 us
  transfers between devices with their start and end apart: 4, of which 3 were waited for; matrix products, arithmetic and copies ran while one was open for 11% of the time, Pallas kernels for 50%

profile of v15, /device:TPU:17, one launch (start us, length us, event | category | flops | bytes accessed | tf_op | source)
XLA Modules:
  0.0 102.3 jit_solution(10804121483714874732)
XLA Ops:
  6.5 0.0 copy-start
  6.5 0.0 all-gather.2.cloned.1.call-start
  6.5 1.1 %copy-done = bf16[128,3072]{1,0:T(8,128)(2,1)S(1)} copy-done((bf16[128,3072]{1,0:T(8,128)(2,1)S(1)}, bf16[128,3072]{1,0:T(8,128)(2,1)}, u32[]{:S(2)}) %copy-start) | copy-done | bytes 786456
  7.7 0.8 constant_dynamic-slice_fusion
  8.4 0.0 all-gather.2.cloned.1.call-update
  8.5 0.7 convert_bitcast_fusion
  9.2 1.0 %fusion.4 = pred[4,8,54]{2,0,1:T(4,128)(4,1)S(1)} fusion(pred[8,54,4]{1,2,0:T(4,128)(4,1)} %constant.59, pred[8,54,4]{1,2,0:T(4,128)(4,1)} %constant.57, bf16[8,45,54]{2,1,0:T(8,128)(2,1)} %constant.82, bf16[4,8,45]{2,1,0:T(8,128)(2,1)S(1)} %convert_bitcast_fusion), kind=kOutput, calls=%fused_computation.7 | convolution fusion | flops 160704 | bytes 46944 | tf_op jit(solution)/shard_map/rcw,cwk->rck/dot_general | solution.py:67
  10.3 0.1 reshape.25
  10.4 1.0 %fusion.15 = f32[16,2,9,6]{3,2,1,0:T(8,128)S(1)} fusion(pred[16,2,9,6]{3,2,1,0:T(8,128)(4,1)S(1)} %reshape.25, s32[16,2,9,6]{3,2,1,0:T(8,128)} %constant.52.clone, s32[]{:T(128)S(6)} %axis_index.29), kind=kLoop, calls=%fused_computation.26 | loop fusion | flops 10368 | bytes 15556 | tf_op jit(solution)/shard_map/jit(_where)/select_n | solution.py:72
  11.5 0.4 broadcast_in_dim.16
  11.8 0.3 reshape.18
  12.1 1.0 copy.14.bias_ref
  13.1 50.7 %shard_map.91 = bf16[8,256,128]{2,1,0:T(8,128)(2,1)} custom-call(bf16[2048,128]{1,0:T(8,128)(2,1)} %q_ref.1, bf16[2048,128]{1,0:T(8,128)(2,1)} %k_ref.1, bf16[2048,128]{1,0:T(8,128)(2,1)} %v_ref.1, f32[16,2,3456]{2,1,0:T(2,128)} %copy.14.bias_ref), custom_call_target="tpu_custom_call" | custom-call | tf_op jit(solution)/shard_map/pallas_call | solution.py:235
  63.8 1.3 %copy.15 = bf16[256,8,128]{0,2,1:T(8,128)(2,1)S(1)} copy(bf16[256,8,128]{2,0,1:T(8,128)(2,1)} %bitcast.30) | data formatting | bytes 1048576 | tf_op jit(solution)/shard_map/transpose | solution.py:275
  65.1 1.4 %collective-permute-start = (bf16[256,1024]{0,1:T(8,128)(2,1)S(1)}, bf16[256,1024]{0,1:T(8,128)(2,1)S(1)}, u32[]{:S(2)}, u32[]{:S(2)}) collective-permute-start(bf16[256,1024]{0,1:T(8,128)(2,1)S(1)} %bitcast.27), channel_id=1, source_target_pairs={{0,16},{16,0},{32,48},{48,32},{64,80},{80,64},{96,112},{112,96},{1... | collective-permute-start | bytes 1572872 | tf_op jit(solution)/shard_map/ppermute | solution.py:283
  66.4 2.8 %all-gather.2.cloned.1.call-done = bf16[1024,1536]{1,0:T(8,128)(2,1)} async-done(((bf16[128,1536]{1,0:T(8,128)(2,1)}), bf16[1024,1536]{1,0:T(8,128)(2,1)}) %all-gather.2.cloned.1.call-update) | async-done | bytes 3145744 | tf_op jit(solution)/shard_map/all_gather | solution.py:273
  69.2 0.0 copy-start.1
  69.2 2.6 %fusion = bf16[1,128,1536]{2,1,0:T(8,128)(2,1)S(1)} fusion(bf16[1024,1536]{1,0:T(8,128)(2,1)} %all-gather.2.cloned.1.call-done, bf16[256,1024]{0,1:T(8,128)(2,1)S(1)} %bitcast.28, s32[]{:T(128)S(6)} %select_n.35), kind=kOutput, calls=%fused_computation.2 | convolution fusion | flops 402849792 | bytes 3801092 | tf_op jit(solution)/shard_map/dot_general | solution.py:280
  71.9 0.0 collective-permute-done
  71.9 0.2 copy-done.1
  72.0 0.6 fusion.1
  72.7 0.1 pad_maximum_fusion
  72.7 1.3 %collective-permute-start.1 = (bf16[2,128,1536]{2,1,0:T(8,128)(2,1)S(1)}, bf16[2,128,1536]{2,1,0:T(8,128)(2,1)S(1)}, u32[]{:S(2)}, u32[]{:S(2)}) collective-permute-start(bf16[2,128,1536]{2,1,0:T(8,128)(2,1)S(1)} %pad_maximum_fusion), channel_id=1, source_target_pairs={{0,8},{8,0},{1,9},{9,1},{2,10},{10,2},{3,11},{11,3},{4,12},{12,4},... | collective-permute-start | bytes 2359304 | tf_op jit(solution)/shard_map/ppermute | solution.py:285
  74.0 0.0 copy-start.2
  74.0 2.6 %fusion.11 = f32[128,1536]{1,0:T(8,128)S(1)} fusion(bf16[1024,1536]{1,0:T(8,128)(2,1)} %all-gather.2.cloned.1.call-done, bf16[256,1024]{0,1:T(8,128)(2,1)S(1)} %bitcast.29, s32[]{:T(128)S(6)} %select_n.33), kind=kOutput, calls=%fused_computation.22 | convolution fusion | flops 402653184 | bytes 4194308 | tf_op jit(solution)/shard_map/dot_general | solution.py:280
  76.7 0.2 copy-done.2
  76.8 0.6 fusion.7
  77.5 12.0 %collective-permute-done.1 = bf16[2,128,1536]{2,1,0:T(8,128)(2,1)S(1)} collective-permute-done((bf16[2,128,1536]{2,1,0:T(8,128)(2,1)S(1)}, bf16[2,128,1536]{2,1,0:T(8,128)(2,1)S(1)}, u32[]{:S(2)}, u32[]{:S(2)}) %collective-permute-start.1) | collective-permute-done | bytes 786464 | tf_op jit(solution)/shard_map/ppermute | solution.py:285
  89.5 0.2 fusion.6
  89.7 3.4 %collective-permute-start.2 = (bf16[128,1536]{1,0:T(8,128)(2,1)S(1)}, bf16[128,1536]{1,0:T(8,128)(2,1)S(1)}, u32[]{:S(2)}, u32[]{:S(2)}) collective-permute-start(bf16[128,1536]{1,0:T(8,128)(2,1)S(1)} %get-tuple-element.6), channel_id=1, source_target_pairs={{0,16},{16,0},{32,48},{48,32},{64,80},{80,64},{96,112},{112,96},{1... | collective-permute-start | bytes 1179656 | tf_op jit(solution)/shard_map/ppermute | solution.py:289
  93.1 1.3 %collective-permute-done.2 = bf16[128,1536]{1,0:T(8,128)(2,1)S(1)} collective-permute-done((bf16[128,1536]{1,0:T(8,128)(2,1)S(1)}, bf16[128,1536]{1,0:T(8,128)(2,1)S(1)}, u32[]{:S(2)}, u32[]{:S(2)}) %collective-permute-start.2) | collective-permute-done | bytes 393248 | tf_op jit(solution)/shard_map/ppermute | solution.py:289
  94.4 1.1 %maximum_select_fusion = bf16[128,3072]{1,0:T(8,128)(2,1)} fusion(bf16[128,1536]{1,0:T(8,128)(2,1)S(1)} %collective-permute-done.2, bf16[128,1536]{1,0:T(8,128)(2,1)S(1)} %get-tuple-element.5, pred[]{:T(512)S(6)} %eq.5), kind=kLoop, calls=%fused_computation.9 | loop fusion | flops 3538944 | bytes 1572865 | tf_op jit(solution)/shard_map/jit(_where)/select_n | solution.py:291
  (2 shorter events, 0.0 us)
Async XLA Ops:
  6.5 1.1 %copy-start = (bf16[128,3072]{1,0:T(8,128)(2,1)S(1)}, bf16[128,3072]{1,0:T(8,128)(2,1)}, u32[]{:S(2)}) copy-start(bf16[128,3072]{1,0:T(8,128)(2,1)} %param.13) | copy-start | bytes 2359300
  6.5 62.7 %all-gather.2.cloned.1.call-start = ((), (), s32[]{:S(2)}) async-start(), calls=%async_computation | async-start | bytes 3538944 | tf_op jit(solution)/shard_map/all_gather | solution.py:273
  65.1 6.8 %collective-permute-start = (bf16[256,1024]{0,1:T(8,128)(2,1)S(1)}, bf16[256,1024]{0,1:T(8,128)(2,1)S(1)}, u32[]{:S(2)}, u32[]{:S(2)}) collective-permute-start(bf16[256,1024]{0,1:T(8,128)(2,1)S(1)} %bitcast.27), channel_id=1, source_target_pairs={{0,16},{16,0},{32,48},{48,32},{64,80},{80,64},{96,112},{112,96},{1... | collective-permute-start | bytes 1572872 | tf_op jit(solution)/shard_map/ppermute | solution.py:283
  69.2 2.8 %copy-start.1 = (bf16[1024,1536]{1,0:T(8,128)(2,1)S(1)}, bf16[1024,1536]{1,0:T(8,128)(2,1)}, u32[]{:S(2)}) copy-start(bf16[1024,1536]{1,0:T(8,128)(2,1)} %all-gather.2.cloned.1.call-done) | copy-start | bytes 9437188
  72.7 16.7 %collective-permute-start.1 = (bf16[2,128,1536]{2,1,0:T(8,128)(2,1)S(1)}, bf16[2,128,1536]{2,1,0:T(8,128)(2,1)S(1)}, u32[]{:S(2)}, u32[]{:S(2)}) collective-permute-start(bf16[2,128,1536]{2,1,0:T(8,128)(2,1)S(1)} %pad_maximum_fusion), channel_id=1, source_target_pairs={{0,8},{8,0},{1,9},{9,1},{2,10},{10,2},{3,11},{11,3},{4,12},{12,4},... | collective-permute-start | bytes 2359304 | tf_op jit(solution)/shard_map/ppermute | solution.py:285
  74.0 2.8 %copy-start.2 = (bf16[1024,1536]{1,0:T(8,128)(2,1)S(1)}, bf16[1024,1536]{1,0:T(8,128)(2,1)}, u32[]{:S(2)}) copy-start(bf16[1024,1536]{1,0:T(8,128)(2,1)} %all-gather.2.cloned.1.call-done) | copy-start | bytes 9437188
  89.7 4.8 %collective-permute-start.2 = (bf16[128,1536]{1,0:T(8,128)(2,1)S(1)}, bf16[128,1536]{1,0:T(8,128)(2,1)S(1)}, u32[]{:S(2)}, u32[]{:S(2)}) collective-permute-start(bf16[128,1536]{1,0:T(8,128)(2,1)S(1)} %get-tuple-element.6), channel_id=1, source_target_pairs={{0,16},{16,0},{32,48},{48,32},{64,80},{80,64},{96,112},{112,96},{1... | collective-permute-start | bytes 1179656 | tf_op jit(solution)/shard_map/ppermute | solution.py:289
Sparse Core Ops, SparseCore 0:
  9.1 60.0 all-gather.1

commit v16 on v15

--- a/solution.py
+++ b/solution.py
@@ -269,25 +269,33 @@
     sides = lax.axis_size("hy")
     half = out_weight.shape[1] // 2
     partners = [(i, i ^ 1) for i in range(count)]
-    weight_half = lax.dynamic_slice_in_dim(out_weight, core * half, half, axis=1)
-    weight_half = lax.all_gather(weight_half, "hz", axis=0, tiled=True)
+    quarter = half // 2
+    weights = [
+        lax.all_gather(
+            lax.dynamic_slice_in_dim(out_weight, core * half + k * quarter, quarter, axis=1),
+            "hz", axis=0, tiled=True)
+        for k in range(2)
+    ]
     peers = lax.axis_size("hz")
     mine = got.transpose(1, 0, 2).reshape(tok_dev // peers, peers * HEAD_DIM)
     block = mine.shape[0] // sides
 
-    def project(x, which):
+    def project(x, which, weight):
         rows = lax.dynamic_slice_in_dim(x, which * block, block, axis=0)
-        return jnp.dot(rows, weight_half, preferred_element_type=jnp.float32)
+        return jnp.dot(rows, weight, preferred_element_type=jnp.float32)
 
     flip = [(0, 1), (1, 0)]
     theirs = lax.ppermute(mine, "frame", partners)
-    partials = jnp.stack([project(mine, 1 - side), project(theirs, 1 - side)]).astype(jnp.bfloat16)
-    sent_mine, sent_theirs = lax.ppermute(partials, "hy", flip)
-    own_mine = lax.optimization_barrier(project(mine, side))
-    own_theirs = lax.optimization_barrier(project(theirs, side))
-    other = (own_theirs + sent_theirs.astype(jnp.float32)).astype(jnp.bfloat16)
-    other_half = lax.ppermute(other, "frame", partners)
-    own_half = (own_mine + sent_mine.astype(jnp.float32)).astype(jnp.bfloat16)
+    own_parts, other_parts = [], []
+    for weight in weights:
+        partials = jnp.stack([project(mine, 1 - side, weight), project(theirs, 1 - side, weight)])
+        sent_mine, sent_theirs = lax.ppermute(partials.astype(jnp.bfloat16), "hy", flip)
+        own_mine = lax.optimization_barrier(project(mine, side, weight))
+        own_theirs = lax.optimization_barrier(project(theirs, side, weight))
+        other_parts.append((own_theirs + sent_theirs.astype(jnp.float32)).astype(jnp.bfloat16))
+        own_parts.append((own_mine + sent_mine.astype(jnp.float32)).astype(jnp.bfloat16))
+    other_half = lax.ppermute(jnp.concatenate(other_parts, axis=1), "frame", partners)
+    own_half = jnp.concatenate(own_parts, axis=1)
     return jnp.where(
         core == 0,
         jnp.concatenate([own_half, other_half], axis=1),

time: 104 us -> 124 us (1.19)
  waiting for transfers between devices: 16.2 us -> 35.8 us
  starting transfers between devices: 6.03 us -> 9.13 us
  Pallas kernels: 50.7 us -> 49.4 us
    all_gather x1 -> x2, waiting for transfers between devices: 2.8 us -> 29.7 us  [on_device(): lax.all_gather(lax.dynamic_slice_in_dim(out_weight, core * half + k * qua...]
    ppermute x2 -> x3, waiting for transfers between devices: 13.4 us -> 5.36 us  [the longest x2 4.01 us: on_device(): lax.ppermute(partials.astype(jnp.bfloat16), 'hy', flip)]
    ppermute x2 -> x3, starting transfers between devices: 4.67 us -> 8.35 us  [the longest x1 5.94 us: on_device(): lax.ppermute(jnp.concatenate(other_parts, axis=1), 'frame', partners)]
    unnamed x6, local copies, waits for them, and re-layouts: 1.5 us -> 0.01 us
    pallas_call x1, Pallas kernels: 50.7 us -> 49.4 us  [attend(): pl.pallas_call(attention_kernel, grid=(TROWS, GROUPS), in_specs=[pl.Block...]
    dot_general x4 -> x8, matrix products: 6.5 us -> 6.38 us  [project(): return jnp.dot(rows, weight, preferred_element_type=jnp.float32)]
  transfers between devices with their start and end apart: 4 -> 6, of which waited for: 3 -> 3; matrix products, arithmetic and copies ran while one was open for 11% -> 9% of each run, Pallas kernels for 50% -> 40%
where the time goes in v16:
time: 124 us; the launch traced here: 122 us
  Pallas kernels  49.4 us (40%)
  waiting for transfers between devices  35.8 us (29%)
  between operations  13.6 us (11%)
  starting transfers between devices  9.13 us (7%)
  matrix products  7.43 us (6%)
  local copies, waits for them, and re-layouts  4.88 us (4%)
  other arithmetic  2.11 us (2%)
    pallas_call x1, Pallas kernels, attend(): pl.pallas_call(attention_kernel, grid=(TROWS, GROUPS), in_specs=[pl.Block...  49.4 us
    all_gather x2, waiting for transfers between devices, on_device(): lax.all_gather(lax.dynamic_slice_in_dim(out_weight, core * half + k * qua...  29.7 us
    dot_general x8, matrix products, project(): return jnp.dot(rows, weight, preferred_element_type=jnp.float32)  6.38 us
    ppermute x1, starting transfers between devices, on_device(): lax.ppermute(jnp.concatenate(other_parts, axis=1), 'frame', partners)  5.94 us
    ppermute x2, waiting for transfers between devices, on_device(): lax.ppermute(partials.astype(jnp.bfloat16), 'hy', flip)  4.01 us
  transfers between devices with their start and end apart: 6, of which 3 were waited for; matrix products, arithmetic and copies ran while one was open for 9% of the time, Pallas kernels for 40%

profile of v16, /device:TPU:17, one launch (start us, length us, event | category | flops | bytes accessed | tf_op | source)
XLA Modules:
  0.0 122.4 jit_solution(3724962881013961932)
XLA Ops:
  6.5 0.0 copy-start.2
  6.5 0.0 all-gather.3.cloned.1.call-start
  6.5 1.8 %constant_dynamic-slice_fusion.1 = (bf16[128,768]{1,0:T(8,128)(2,1)}, bf16[128,768]{1,0:T(8,128)(2,1)}) fusion(bf16[128,3072]{1,0:T(8,128)(2,1)} %param.13, s32[]{:T(128)S(6)} %select_n.41, s32[]{:T(128)S(6)} %select_n.43), kind=kLoop, calls=%fused_computation.55 | loop fusion | bytes 786440 | tf_op jit(solution)/shard_map/dynamic_slice | solution.py:275
  8.4 0.0 all-gather.3.cloned.1.call-update
  8.4 0.0 all-gather.5.cloned.1.call-start
  8.4 0.7 all-gather.5.cloned.1.call-update
  9.1 0.7 convert_bitcast_fusion
  9.9 1.0 fusion.6
  10.9 0.1 reshape.31
  11.1 0.0 copy-done.2
  11.1 0.1 fusion.13
  11.2 0.4 broadcast_in_dim.16
  11.6 0.3 reshape.22
  11.8 1.0 copy.14.bias_ref
  12.8 49.4 %shard_map.91 = bf16[8,256,128]{2,1,0:T(8,128)(2,1)} custom-call(bf16[2048,128]{1,0:T(8,128)(2,1)} %q_ref.1, bf16[2048,128]{1,0:T(8,128)(2,1)} %k_ref.1, bf16[2048,128]{1,0:T(8,128)(2,1)} %v_ref.1, f32[16,2,3456]{2,1,0:T(2,128)} %copy.14.bias_ref), custom_call_target="tpu_custom_call" | custom-call | tf_op jit(solution)/shard_map/pallas_call | solution.py:235
  62.3 1.2 %copy.15 = bf16[256,8,128]{0,2,1:T(8,128)(2,1)S(1)} copy(bf16[256,8,128]{2,0,1:T(8,128)(2,1)} %bitcast.50) | data formatting | bytes 1048576 | tf_op jit(solution)/shard_map/transpose | solution.py:280
  63.5 0.7 collective-permute-start
  64.3 0.0 all-gather.3.cloned.1.call-done
  64.3 0.0 copy-start
  64.3 1.9 %fusion = bf16[1,128,768]{2,1,0:T(8,128)(2,1)S(1)} fusion(bf16[1024,768]{1,0:T(8,128)(2,1)} %all-gather.3.cloned.1.call-done, bf16[256,1024]{0,1:T(8,128)(2,1)S(1)} %bitcast.46, s32[]{:T(128)S(6)} %select_n.42), kind=kOutput, calls=%fused_computation.4 | convolution fusion | flops 201424896 | bytes 2031620 | tf_op jit(solution)/shard_map/dot_general | solution.py:285
  66.2 0.0 collective-permute-done
  66.2 0.0 copy-done
  66.2 0.4 fusion.1
  66.7 1.5 %collective-permute-start.1 = (bf16[2,128,768]{2,1,0:T(8,128)(2,1)S(1)}, bf16[2,128,768]{2,1,0:T(8,128)(2,1)S(1)}, u32[]{:S(2)}, u32[]{:S(2)}) collective-permute-start(bf16[2,128,768]{2,1,0:T(8,128)(2,1)S(1)} %pad_maximum_fusion), channel_id=1, source_target_pairs={{0,8},{8,0},{1,9},{9,1},{2,10},{10,2},{3,11},{11,3},{4,12},{12,4},... | collective-permute-start | bytes 1179656 | tf_op jit(solution)/shard_map/ppermute | solution.py:292
  68.2 29.7 %all-gather.5.cloned.1.call-done = bf16[1024,768]{1,0:T(8,128)(2,1)} async-done(((bf16[128,768]{1,0:T(8,128)(2,1)}), bf16[1024,768]{1,0:T(8,128)(2,1)}) %all-gather.5.cloned.1.call-update) | async-done | bytes 1572880 | tf_op jit(solution)/shard_map/all_gather | solution.py:274
  97.9 0.0 copy-start.1
  97.9 1.9 %fusion.3 = bf16[1,128,768]{2,1,0:T(8,128)(2,1)S(1)} fusion(bf16[1024,768]{1,0:T(8,128)(2,1)} %all-gather.5.cloned.1.call-done, bf16[256,1024]{0,1:T(8,128)(2,1)S(1)} %collective-permute-done, s32[]{:T(128)S(6)} %select_n.42), kind=kOutput, calls=%fused_computation.7 | convolution fusion | flops 201424896 | bytes 2031620 | tf_op jit(solution)/shard_map/dot_general | solution.py:285
  99.9 0.0 copy-done.1
  99.9 0.4 fusion.2
  100.4 0.9 collective-permute-start.2
  101.3 0.4 fusion.16
  101.7 0.4 fusion.24
  102.1 0.4 fusion.14
  102.6 0.4 fusion.22
  103.0 0.0 collective-permute-done.1
  103.0 0.1 fusion.10
  103.1 4.0 %collective-permute-done.2 = bf16[2,128,768]{2,1,0:T(8,128)(2,1)S(1)} collective-permute-done((bf16[2,128,768]{2,1,0:T(8,128)(2,1)S(1)}, bf16[2,128,768]{2,1,0:T(8,128)(2,1)S(1)}, u32[]{:S(2)}, u32[]{:S(2)}) %collective-permute-start.2) | collective-permute-done | bytes 393248 | tf_op jit(solution)/shard_map/ppermute | solution.py:292
  107.1 0.1 fusion.9
  107.2 5.9 %collective-permute-start.3 = (bf16[128,1536]{1,0:T(8,128)(2,1)S(1)}, bf16[128,1536]{1,0:T(8,128)(2,1)S(1)}, u32[]{:S(2)}, u32[]{:S(2)}) collective-permute-start(bf16[128,1536]{1,0:T(8,128)(2,1)S(1)} %pad_maximum_fusion.2), channel_id=1, source_target_pairs={{0,16},{16,0},{32,48},{48,32},{64,80},{80,64},{96,112},{112,96},{1... | collective-permute-start | bytes 1179656 | tf_op jit(solution)/shard_map/ppermute | solution.py:297
  113.1 1.3 %collective-permute-done.3 = bf16[128,1536]{1,0:T(8,128)(2,1)S(1)} collective-permute-done((bf16[128,1536]{1,0:T(8,128)(2,1)S(1)}, bf16[128,1536]{1,0:T(8,128)(2,1)S(1)}, u32[]{:S(2)}, u32[]{:S(2)}) %collective-permute-start.3) | collective-permute-done | bytes 393248 | tf_op jit(solution)/shard_map/ppermute | solution.py:297
  114.5 1.1 maximum_select_fusion
  (5 shorter events, 0.1 us)
Async XLA Ops:
  6.5 4.5 %copy-start.2 = (s32[16,2,9,6]{3,2,1,0:T(8,128)S(1)}, s32[16,2,9,6]{3,2,1,0:T(8,128)}, u32[]{:S(2)}) copy-start(s32[16,2,9,6]{3,2,1,0:T(8,128)} %constant.56.clone) | copy-start | bytes 20740
  6.5 57.7 %all-gather.3.cloned.1.call-start = ((), (), s32[]{:S(2)}) async-start(), calls=%async_computation | async-start | bytes 1769472 | tf_op jit(solution)/shard_map/all_gather | solution.py:274
  8.4 89.5 %all-gather.5.cloned.1.call-start = ((), (), s32[]{:S(2)}) async-start(), calls=%async_computation.1 | async-start | bytes 1769472 | tf_op jit(solution)/shard_map/all_gather | solution.py:274
  63.5 2.7 %collective-permute-start = (bf16[256,1024]{0,1:T(8,128)(2,1)S(1)}, bf16[256,1024]{0,1:T(8,128)(2,1)S(1)}, u32[]{:S(2)}, u32[]{:S(2)}) collective-permute-start(bf16[256,1024]{0,1:T(8,128)(2,1)S(1)} %bitcast.45), channel_id=1, source_target_pairs={{0,16},{16,0},{32,48},{48,32},{64,80},{80,64},{96,112},{112,96},{1... | collective-permute-start | bytes 1572872 | tf_op jit(solution)/shard_map/ppermute | solution.py:288
  64.3 2.0 %copy-start = (bf16[1024,768]{1,0:T(8,128)(2,1)S(1)}, bf16[1024,768]{1,0:T(8,128)(2,1)}, u32[]{:S(2)}) copy-start(bf16[1024,768]{1,0:T(8,128)(2,1)} %all-gather.3.cloned.1.call-done) | copy-start | bytes 4718596
  66.7 36.3 %collective-permute-start.1 = (bf16[2,128,768]{2,1,0:T(8,128)(2,1)S(1)}, bf16[2,128,768]{2,1,0:T(8,128)(2,1)S(1)}, u32[]{:S(2)}, u32[]{:S(2)}) collective-permute-start(bf16[2,128,768]{2,1,0:T(8,128)(2,1)S(1)} %pad_maximum_fusion), channel_id=1, source_target_pairs={{0,8},{8,0},{1,9},{9,1},{2,10},{10,2},{3,11},{11,3},{4,12},{12,4},... | collective-permute-start | bytes 1179656 | tf_op jit(solution)/shard_map/ppermute | solution.py:292
  97.9 1.9 %copy-start.1 = (bf16[1024,768]{1,0:T(8,128)(2,1)S(1)}, bf16[1024,768]{1,0:T(8,128)(2,1)}, u32[]{:S(2)}) copy-start(bf16[1024,768]{1,0:T(8,128)(2,1)} %all-gather.5.cloned.1.call-done) | copy-start | bytes 4718596
  100.4 6.7 %collective-permute-start.2 = (bf16[2,128,768]{2,1,0:T(8,128)(2,1)S(1)}, bf16[2,128,768]{2,1,0:T(8,128)(2,1)S(1)}, u32[]{:S(2)}, u32[]{:S(2)}) collective-permute-start(bf16[2,128,768]{2,1,0:T(8,128)(2,1)S(1)} %pad_maximum_fusion.1), channel_id=1, source_target_pairs={{0,8},{8,0},{1,9},{9,1},{2,10},{10,2},{3,11},{11,3},{4,12},{12,4},... | collective-permute-start | bytes 1179656 | tf_op jit(solution)/shard_map/ppermute | solution.py:292
  107.2 7.3 %collective-permute-start.3 = (bf16[128,1536]{1,0:T(8,128)(2,1)S(1)}, bf16[128,1536]{1,0:T(8,128)(2,1)S(1)}, u32[]{:S(2)}, u32[]{:S(2)}) collective-permute-start(bf16[128,1536]{1,0:T(8,128)(2,1)S(1)} %pad_maximum_fusion.2), channel_id=1, source_target_pairs={{0,16},{16,0},{32,48},{48,32},{64,80},{80,64},{96,112},{112,96},{1... | collective-permute-start | bytes 1179656 | tf_op jit(solution)/shard_map/ppermute | solution.py:297
Sparse Core Ops, SparseCore 0:
  9.1 46.3 all-gather.2
  57.4 40.5 all-gather.4

commit v17 on v15

--- a/solution.py
+++ b/solution.py
@@ -74,9 +74,9 @@
     return bias.reshape(TROWS * GROUPS, QTILES, ROW_K)
 
 
-def attention_kernel(q_ref, k_ref, v_ref, bias_ref, o_ref,
-                     kp_ref, kn_ref, vp_ref, vn_ref, s_ref, p_ref, att_ref, got_ref,
-                     send_sem, recv_sem, out_send, out_recv):
+def attention_kernel(q_ref, k_ref, v_ref, bias_ref, w_ref, o_ref, ow_ref,
+                     kp_ref, kn_ref, vp_ref, vn_ref, s_ref, p_ref, att_ref, got_ref, wall_ref,
+                     send_sem, recv_sem, out_send, out_recv, w_send, w_recv):
     row = pl.program_id(0)
     group = pl.program_id(1)
     frame = lax.axis_index("frame")
@@ -84,6 +84,12 @@
     me = lax.axis_index("hz")
     peers = lax.axis_size("hz")
     mesh = pl.DeviceIdType.MESH
+
+    def weight_copy(i):
+        return pltpu.make_async_remote_copy(
+            src_ref=w_ref, dst_ref=wall_ref.at[me], send_sem=w_send.at[i], recv_sem=w_recv.at[i],
+            device_id=(frame, side, lax.rem(me + i, peers)), device_id_type=mesh,
+        )
 
     @pl.when((row == 0) & (group == 0))
     def _():
@@ -147,6 +153,10 @@
                 copy.wait_send()
             for copy in to_prev:
                 copy.wait_recv()
+
+        for i in range(1, peers):
+            weight_copy(i).start()
+        wall_ref[me] = w_ref[...]
 
         @pl.when(jnp.logical_not(has_prev))
         def _():
@@ -222,36 +232,46 @@
             peer = lax.rem(me + i, peers)
             for which in range(2):
                 send(i, which, peer, src).wait()
+        for i in range(1, peers):
+            weight_copy(i).wait()
         o_ref[...] = got_ref[...]
-
-
-def attend(q, k, v, bias):
+        ow_ref[...] = wall_ref[...]
+
+
+def attend(q, k, v, bias, weight):
     tokens = q.shape[0]
     full = pl.BlockSpec((tokens, HEAD_DIM), lambda r, g: (0, 0))
     frame_kv = pltpu.VMEM((tokens, HEAD_DIM), jnp.bfloat16)
     peers = lax.axis_size("hz")
     got_shape = (peers, tokens // peers, HEAD_DIM)
     got = pltpu.VMEM(got_shape, jnp.bfloat16)
+    wall_shape = (peers,) + weight.shape
     return pl.pallas_call(
         attention_kernel,
         grid=(TROWS, GROUPS),
         in_specs=[pl.BlockSpec((BLOCK_Q, HEAD_DIM), lambda r, g: (r * GROUPS + g, 0))]
         + [full] * 2
-        + [pl.BlockSpec((1, QTILES, ROW_K), lambda r, g: (r * GROUPS + g, 0, 0))],
-        out_specs=pl.BlockSpec(got_shape, lambda r, g: (0, 0, 0)),
-        out_shape=jax.ShapeDtypeStruct(got_shape, jnp.bfloat16),
+        + [pl.BlockSpec((1, QTILES, ROW_K), lambda r, g: (r * GROUPS + g, 0, 0)),
+           pl.BlockSpec(weight.shape, lambda r, g: (0, 0))],
+        out_specs=[pl.BlockSpec(got_shape, lambda r, g: (0, 0, 0)),
+                   pl.BlockSpec(wall_shape, lambda r, g: (0, 0, 0))],
+        out_shape=[jax.ShapeDtypeStruct(got_shape, jnp.bfloat16),
+                   jax.ShapeDtypeStruct(wall_shape, weight.dtype)],
         scratch_shapes=[frame_kv] * 4 + [
             pltpu.VMEM((BLOCK_Q, ROW_K), jnp.float32),
             pltpu.VMEM((BLOCK_Q, ROW_K), jnp.bfloat16),
             frame_kv,
             got,
+            pltpu.VMEM(wall_shape, weight.dtype),
             pltpu.SemaphoreType.DMA((4,)),
             pltpu.SemaphoreType.DMA((4,)),
             pltpu.SemaphoreType.DMA((2 * peers,)),
             pltpu.SemaphoreType.DMA((2 * peers,)),
+            pltpu.SemaphoreType.DMA((peers,)),
+            pltpu.SemaphoreType.DMA((peers,)),
         ],
         compiler_params=pltpu.CompilerParams(collective_id=1, has_side_effects=True),
-    )(q, k, v, bias)
+    )(q, k, v, bias, weight)
 
 
 def on_device(queries, keys, values, block_mask, out_weight):
@@ -263,14 +283,16 @@
     frame = lax.axis_index("frame") * frames_here
     mask_rows = block_mask.reshape(TROWS * TCOLS, WIN)
     bias = window_bias(mask_rows, frame, frames_total)
-    got = attend(queries, keys, values, bias)
+    core = lax.axis_index("frame") % 2
+    half = out_weight.shape[1] // 2
+    weight_rows = lax.dynamic_slice_in_dim(out_weight, core * half, half, axis=1)
+    got, weight_all = attend(queries, keys, values, bias, weight_rows)
     core = lax.axis_index("frame") % 2
     side = lax.axis_index("hy")
     sides = lax.axis_size("hy")
     half = out_weight.shape[1] // 2
     partners = [(i, i ^ 1) for i in range(count)]
-    weight_half = lax.dynamic_slice_in_dim(out_weight, core * half, half, axis=1)
-    weight_half = lax.all_gather(weight_half, "hz", axis=0, tiled=True)
+    weight_half = weight_all.reshape(-1, half)
     peers = lax.axis_size("hz")
     mine = got.transpose(1, 0, 2).reshape(tok_dev // peers, peers * HEAD_DIM)
     block = mine.shape[0] // sides

time: 104 us -> 140 us (1.35)
  Pallas kernels: 50.7 us -> 103 us
  between operations: 13.5 us -> 0.11 us
    pallas_call x1, Pallas kernels: 50.7 us -> 103 us  [attend(): pl.pallas_call(attention_kernel, grid=(TROWS, GROUPS), in_specs=[pl.Block...]
    all_gather x1 -> x0, waiting for transfers between devices: 2.8 us -> none  [on_device(): weight_half = lax.all_gather(weight_half, 'hz', axis=0, tiled=True)]
    ppermute x1, starting transfers between devices: 3.41 us -> 0.68 us  [on_device(): other_half = lax.ppermute(other, 'frame', partners)]
    ppermute x1, waiting for transfers between devices: 12 us -> 14.4 us  [on_device(): sent_mine, sent_theirs = lax.ppermute(partials, 'hy', flip)]
    ppermute x1, starting transfers between devices: 1.35 us -> 2.84 us  [on_device(): theirs = lax.ppermute(mine, 'frame', partners)]
  transfers between devices with their start and end apart: 4 -> 3, of which waited for: 3 -> 2; matrix products, arithmetic and copies ran while one was open for 11% -> 4% of each run, Pallas kernels for 50% -> 0%
where the time goes in v17:
time: 140 us; the launch traced here: 139 us
  Pallas kernels  103 us (74%)
  waiting for transfers between devices  15.8 us (11%)
  matrix products  7.57 us (5%)
  starting transfers between devices  5.53 us (4%)
  local copies, waits for them, and re-layouts  4.18 us (3%)
  other arithmetic  3.14 us (2%)
    pallas_call x1, Pallas kernels, attend(): pl.pallas_call(attention_kernel, grid=(TROWS, GROUPS), in_specs=[pl.Block...  103 us
    ppermute x1, waiting for transfers between devices, on_device(): sent_mine, sent_theirs = lax.ppermute(partials, 'hy', flip)  14.4 us
    dot_general x4, matrix products, project(): return jnp.dot(rows, weight_half, preferred_element_type=jnp.float32)  6.52 us
    ppermute x1, starting transfers between devices, on_device(): theirs = lax.ppermute(mine, 'frame', partners)  2.84 us
  transfers between devices with their start and end apart: 3, of which 2 were waited for; matrix products, arithmetic and copies ran while one was open for 4% of the time, Pallas kernels for 0%

profile of v17, /device:TPU:17, one launch (start us, length us, event | category | flops | bytes accessed | tf_op | source)
XLA Modules:
  0.0 138.9 jit_solution(17740949967112552917)
XLA Ops:
  0.0 0.0 copy-start
  0.0 0.8 convert_bitcast_fusion
  0.8 1.0 fusion.4
  1.9 0.1 reshape.29
  2.0 1.0 fusion.15
  3.1 0.4 broadcast_in_dim.16
  3.4 0.3 reshape.21
  3.7 1.0 copy.14.bias_ref
  4.7 0.0 copy-done
  4.7 0.8 constant_dynamic-slice_fusion.w_ref
  5.5 102.6 %shard_map.91 = (bf16[8,256,128]{2,1,0:T(8,128)(2,1)}, bf16[8,128,1536]{2,1,0:T(8,128)(2,1)}) custom-call(bf16[2048,128]{1,0:T(8,128)(2,1)} %q_ref.1, bf16[2048,128]{1,0:T(8,128)(2,1)} %k_ref.1, bf16[2048,128]{1,0:T(8,128)(2,1)} %v_ref.1, f32[16,2,3456]{2,1,0:T(2,128)} %copy.14.bias_ref, bf16[128,1536]{1,0:T(8,128)(2,1)} %constant_dynamic-slice_fusion.w_ref), custom_call_target="tpu_custom_call" | custom-call | tf_op jit(solution)/shard_map/pallas_call | solution.py:249
  108.1 1.2 copy.15
  109.4 2.8 %collective-permute-start = (bf16[256,1024]{0,1:T(8,128)(2,1)S(1)}, bf16[256,1024]{0,1:T(8,128)(2,1)S(1)}, u32[]{:S(2)}, u32[]{:S(2)}) collective-permute-start(bf16[256,1024]{0,1:T(8,128)(2,1)S(1)} %bitcast.32), channel_id=1, source_target_pairs={{0,16},{16,0},{32,48},{48,32},{64,80},{80,64},{96,112},{112,96},{1... | collective-permute-start | bytes 1572872 | tf_op jit(solution)/shard_map/ppermute | solution.py:305
  112.2 0.0 copy-start.1
  112.2 2.7 %fusion = bf16[1,128,1536]{2,1,0:T(8,128)(2,1)S(1)} fusion(bf16[1024,1536]{1,0:T(8,128)(2,1)} %bitcast.28, bf16[256,1024]{0,1:T(8,128)(2,1)S(1)} %bitcast.33, s32[]{:T(128)S(6)} %select_n.37), kind=kOutput, calls=%fused_computation.2 | convolution fusion | flops 402849792 | bytes 3801092 | tf_op jit(solution)/shard_map/dot_general | solution.py:302
  114.9 0.0 collective-permute-done
  114.9 0.2 copy-done.1
  115.0 0.6 fusion.1
  115.7 0.1 pad_maximum_fusion
  115.8 2.0 %collective-permute-start.1 = (bf16[2,128,1536]{2,1,0:T(8,128)(2,1)S(1)}, bf16[2,128,1536]{2,1,0:T(8,128)(2,1)S(1)}, u32[]{:S(2)}, u32[]{:S(2)}) collective-permute-start(bf16[2,128,1536]{2,1,0:T(8,128)(2,1)S(1)} %pad_maximum_fusion), channel_id=1, source_target_pairs={{0,8},{8,0},{1,9},{9,1},{2,10},{10,2},{3,11},{11,3},{4,12},{12,4},... | collective-permute-start | bytes 2359304 | tf_op jit(solution)/shard_map/ppermute | solution.py:307
  117.8 0.0 copy-start.2
  117.8 2.6 %fusion.11 = f32[128,1536]{1,0:T(8,128)S(1)} fusion(bf16[1024,1536]{1,0:T(8,128)(2,1)} %bitcast.29, bf16[256,1024]{0,1:T(8,128)(2,1)S(1)} %bitcast.34, s32[]{:T(128)S(6)} %select_n.36), kind=kOutput, calls=%fused_computation.22 | convolution fusion | flops 402653184 | bytes 4194308 | tf_op jit(solution)/shard_map/dot_general | solution.py:302
  120.4 0.2 copy-done.2
  120.6 0.6 fusion.7
  121.2 14.4 %collective-permute-done.1 = bf16[2,128,1536]{2,1,0:T(8,128)(2,1)S(1)} collective-permute-done((bf16[2,128,1536]{2,1,0:T(8,128)(2,1)S(1)}, bf16[2,128,1536]{2,1,0:T(8,128)(2,1)S(1)}, u32[]{:S(2)}, u32[]{:S(2)}) %collective-permute-start.1) | collective-permute-done | bytes 786464 | tf_op jit(solution)/shard_map/ppermute | solution.py:307
  135.7 0.2 fusion.6
  135.9 0.7 collective-permute-start.2
  136.5 1.3 collective-permute-done.2
  137.9 1.1 maximum_select_fusion
  (2 shorter events, 0.0 us)
Async XLA Ops:
  0.0 4.7 %copy-start = (bf16[128,3072]{1,0:T(8,128)(2,1)S(1)}, bf16[128,3072]{1,0:T(8,128)(2,1)}, u32[]{:S(2)}) copy-start(bf16[128,3072]{1,0:T(8,128)(2,1)} %param.13) | copy-start | bytes 2359300
  109.4 5.5 %collective-permute-start = (bf16[256,1024]{0,1:T(8,128)(2,1)S(1)}, bf16[256,1024]{0,1:T(8,128)(2,1)S(1)}, u32[]{:S(2)}, u32[]{:S(2)}) collective-permute-start(bf16[256,1024]{0,1:T(8,128)(2,1)S(1)} %bitcast.32), channel_id=1, source_target_pairs={{0,16},{16,0},{32,48},{48,32},{64,80},{80,64},{96,112},{112,96},{1... | collective-permute-start | bytes 1572872 | tf_op jit(solution)/shard_map/ppermute | solution.py:305
  112.2 2.8 %copy-start.1 = (bf16[8,128,1536]{2,1,0:T(8,128)(2,1)S(1)}, bf16[8,128,1536]{2,1,0:T(8,128)(2,1)}, u32[]{:S(2)}) copy-start(bf16[8,128,1536]{2,1,0:T(8,128)(2,1)} %get-tuple-element.8) | copy-start | bytes 9437188
  115.8 19.9 %collective-permute-start.1 = (bf16[2,128,1536]{2,1,0:T(8,128)(2,1)S(1)}, bf16[2,128,1536]{2,1,0:T(8,128)(2,1)S(1)}, u32[]{:S(2)}, u32[]{:S(2)}) collective-permute-start(bf16[2,128,1536]{2,1,0:T(8,128)(2,1)S(1)} %pad_maximum_fusion), channel_id=1, source_target_pairs={{0,8},{8,0},{1,9},{9,1},{2,10},{10,2},{3,11},{11,3},{4,12},{12,4},... | collective-permute-start | bytes 2359304 | tf_op jit(solution)/shard_map/ppermute | solution.py:307
  117.8 2.8 %copy-start.2 = (bf16[8,128,1536]{2,1,0:T(8,128)(2,1)S(1)}, bf16[8,128,1536]{2,1,0:T(8,128)(2,1)}, u32[]{:S(2)}) copy-start(bf16[8,128,1536]{2,1,0:T(8,128)(2,1)} %get-tuple-element.8) | copy-start | bytes 9437188
  135.9 2.0 %collective-permute-start.2 = (bf16[128,1536]{1,0:T(8,128)(2,1)S(1)}, bf16[128,1536]{1,0:T(8,128)(2,1)S(1)}, u32[]{:S(2)}, u32[]{:S(2)}) collective-permute-start(bf16[128,1536]{1,0:T(8,128)(2,1)S(1)} %get-tuple-element.10), channel_id=1, source_target_pairs={{0,16},{16,0},{32,48},{48,32},{64,80},{80,64},{96,112},{112,96},{1... | collective-permute-start | bytes 1179656 | tf_op jit(solution)/shard_map/ppermute | solution.py:311

commit v18 on v15

--- a/solution.py
+++ b/solution.py
@@ -281,12 +281,12 @@
 
     flip = [(0, 1), (1, 0)]
     theirs = lax.ppermute(mine, "frame", partners)
-    partials = jnp.stack([project(mine, 1 - side), project(theirs, 1 - side)]).astype(jnp.bfloat16)
-    sent_mine, sent_theirs = lax.ppermute(partials, "hy", flip)
+    sent_mine = lax.ppermute(project(mine, 1 - side).astype(jnp.bfloat16), "hy", flip)
+    diagonal = [(f * sides + h, (f ^ 1) * sides + (sides - 1 - h)) for f in range(count) for h in range(sides)]
+    sent_cross = lax.ppermute(project(theirs, 1 - side).astype(jnp.bfloat16), ("frame", "hy"), diagonal)
     own_mine = lax.optimization_barrier(project(mine, side))
-    own_theirs = lax.optimization_barrier(project(theirs, side))
-    other = (own_theirs + sent_theirs.astype(jnp.float32)).astype(jnp.bfloat16)
-    other_half = lax.ppermute(other, "frame", partners)
+    from_partner = lax.ppermute(project(theirs, side), "frame", partners)
+    other_half = (from_partner + sent_cross.astype(jnp.float32)).astype(jnp.bfloat16)
     own_half = (own_mine + sent_mine.astype(jnp.float32)).astype(jnp.bfloat16)
     return jnp.where(
         core == 0,

time: 104 us -> 101 us (0.971)
  matrix products: 7.55 us -> 5.52 us
    dot_general x4, matrix products: 6.5 us -> 4.48 us  [project(): return jnp.dot(rows, weight_half, preferred_element_type=jnp.float32)]
    ppermute x2 -> x3, starting transfers between devices: 4.67 us -> 4.33 us  [the longest x1 3.05 us: on_device(): from_partner = lax.ppermute(project(theirs, side), 'frame', partners)]
    ppermute x2 -> x3, waiting for transfers between devices: 13.4 us -> 13.1 us  [the longest x1 11 us: on_device(): lax.ppermute(project(theirs, 1 - side).astype(jnp.bfloat16), ('frame', 'h...]
  transfers between devices with their start and end apart: 4 -> 5, of which waited for: 3 -> 3; matrix products, arithmetic and copies ran while one was open for 11% -> 10% of each run, Pallas kernels for 50% -> 52%
where the time goes in v18:
time: 101 us; the launch traced here: 99.2 us
  Pallas kernels  51.2 us (51%)
  waiting for transfers between devices  15.9 us (16%)
  between operations  13.5 us (13%)
  matrix products  5.52 us (5%)
  starting transfers between devices  5.2 us (5%)
  local copies, waits for them, and re-layouts  4.96 us (5%)
  other arithmetic  2.97 us (3%)
    pallas_call x1, Pallas kernels, attend(): pl.pallas_call(attention_kernel, grid=(TROWS, GROUPS), in_specs=[pl.Block...  51.2 us
    ppermute x1, waiting for transfers between devices, on_device(): lax.ppermute(project(theirs, 1 - side).astype(jnp.bfloat16), ('frame', 'h...  11 us
    dot_general x4, matrix products, project(): return jnp.dot(rows, weight_half, preferred_element_type=jnp.float32)  4.48 us
    ppermute x1, starting transfers between devices, on_device(): from_partner = lax.ppermute(project(theirs, side), 'frame', partners)  3.05 us
    all_gather x1, waiting for transfers between devices, on_device(): weight_half = lax.all_gather(weight_half, 'hz', axis=0, tiled=True)  2.79 us
    ppermute x1, waiting for transfers between devices, on_device(): lax.ppermute(project(mine, 1 - side).astype(jnp.bfloat16), 'hy', flip)  2.1 us
  transfers between devices with their start and end apart: 5, of which 3 were waited for; matrix products, arithmetic and copies ran while one was open for 10% of the time, Pallas kernels for 52%

profile of v18, /device:TPU:17, one launch (start us, length us, event | category | flops | bytes accessed | tf_op | source)
XLA Modules:
  0.0 99.2 jit_solution(264395402486201298)
XLA Ops:
  6.5 0.0 copy-start
  6.5 0.0 all-gather.2.cloned.1.call-start
  6.5 1.1 %copy-done = bf16[128,3072]{1,0:T(8,128)(2,1)S(1)} copy-done((bf16[128,3072]{1,0:T(8,128)(2,1)S(1)}, bf16[128,3072]{1,0:T(8,128)(2,1)}, u32[]{:S(2)}) %copy-start) | copy-done | bytes 786456
  7.7 0.8 constant_dynamic-slice_fusion
  8.5 0.0 all-gather.2.cloned.1.call-update
  8.5 0.7 convert_bitcast_fusion
  9.2 1.0 %fusion.2 = pred[4,8,54]{2,0,1:T(4,128)(4,1)S(1)} fusion(pred[8,54,4]{1,2,0:T(4,128)(4,1)} %constant.59, pred[8,54,4]{1,2,0:T(4,128)(4,1)} %constant.57, bf16[8,45,54]{2,1,0:T(8,128)(2,1)} %constant.74, bf16[4,8,45]{2,1,0:T(8,128)(2,1)S(1)} %convert_bitcast_fusion), kind=kOutput, calls=%fused_computation.5 | convolution fusion | flops 160704 | bytes 46944 | tf_op jit(solution)/shard_map/rcw,cwk->rck/dot_general | solution.py:67
  10.3 0.1 reshape.19
  10.4 1.0 %fusion.11 = f32[16,2,9,6]{3,2,1,0:T(8,128)S(1)} fusion(pred[16,2,9,6]{3,2,1,0:T(8,128)(4,1)S(1)} %reshape.19, s32[16,2,9,6]{3,2,1,0:T(8,128)} %constant.52.clone, s32[]{:T(128)S(6)} %axis_index.29), kind=kLoop, calls=%fused_computation.19 | loop fusion | flops 10368 | bytes 15556 | tf_op jit(solution)/shard_map/jit(_where)/select_n | solution.py:72
  11.5 0.4 broadcast_in_dim.16
  11.8 0.3 reshape.14
  12.1 1.0 %copy.14.bias_ref = f32[16,2,3456]{2,1,0:T(2,128)} copy(f32[16,2,3456]{2,0,1:T(8,128)S(1)} %reshape.14) | data formatting | bytes 884736 | tf_op jit(solution)/shard_map/reshape | solution.py:74
  13.1 51.2 %shard_map.91 = bf16[8,256,128]{2,1,0:T(8,128)(2,1)} custom-call(bf16[2048,128]{1,0:T(8,128)(2,1)} %q_ref.1, bf16[2048,128]{1,0:T(8,128)(2,1)} %k_ref.1, bf16[2048,128]{1,0:T(8,128)(2,1)} %v_ref.1, f32[16,2,3456]{2,1,0:T(2,128)} %copy.14.bias_ref), custom_call_target="tpu_custom_call" | custom-call | tf_op jit(solution)/shard_map/pallas_call | solution.py:235
  64.3 1.2 %copy.15 = bf16[256,8,128]{0,2,1:T(8,128)(2,1)S(1)} copy(bf16[256,8,128]{2,0,1:T(8,128)(2,1)} %bitcast.16) | data formatting | bytes 1048576 | tf_op jit(solution)/shard_map/transpose | solution.py:275
  65.5 0.9 collective-permute-start.1
  66.4 2.8 %all-gather.2.cloned.1.call-done = bf16[1024,1536]{1,0:T(8,128)(2,1)} async-done(((bf16[128,1536]{1,0:T(8,128)(2,1)}), bf16[1024,1536]{1,0:T(8,128)(2,1)}) %all-gather.2.cloned.1.call-update) | async-done | bytes 3145744 | tf_op jit(solution)/shard_map/all_gather | solution.py:273
  69.2 0.0 copy-start.1
  69.2 2.6 %convolution_convert_fusion.1 = bf16[128,1536]{1,0:T(8,128)(2,1)S(1)} fusion(bf16[1024,1536]{1,0:T(8,128)(2,1)} %all-gather.2.cloned.1.call-done, bf16[256,1024]{0,1:T(8,128)(2,1)S(1)} %bitcast.14, s32[]{:T(128)S(6)} %select_n.35), kind=kOutput, calls=%fused_computation.1 | convolution fusion | flops 402849792 | bytes 3801092 | tf_op jit(solution)/shard_map/dot_general | solution.py:280
  71.9 0.5 collective-permute-start
  72.4 0.0 copy-done.1
  72.4 0.6 fusion.7
  73.0 0.0 collective-permute-done.1
  73.0 0.6 fusion.4
  73.6 3.0 %collective-permute-start.2 = (f32[128,1536]{1,0:T(8,128)S(1)}, f32[128,1536]{1,0:T(8,128)S(1)}, u32[]{:S(2)}, u32[]{:S(2)}) collective-permute-start(f32[128,1536]{1,0:T(8,128)S(1)} %fusion.4), channel_id=1, source_target_pairs={{0,16},{16,0},{32,48},{48,32},{64,80},{80,64},{96,112},{112,96},{1... | collective-permute-start | bytes 2359304 | tf_op jit(solution)/shard_map/ppermute | solution.py:288
  76.7 0.6 convolution_convert_fusion
  77.3 0.7 collective-permute-start.3
  78.1 2.1 %collective-permute-done = bf16[128,1536]{1,0:T(8,128)(2,1)S(1)} collective-permute-done((bf16[128,1536]{1,0:T(8,128)(2,1)S(1)}, bf16[128,1536]{1,0:T(8,128)(2,1)S(1)}, u32[]{:S(2)}, u32[]{:S(2)}) %collective-permute-start) | collective-permute-done | bytes 393248 | tf_op jit(solution)/shard_map/ppermute | solution.py:284
  80.2 0.1 add_convert_fusion.1
  80.2 11.0 %collective-permute-done.3 = bf16[128,1536]{1,0:T(8,128)(2,1)S(1)} collective-permute-done((bf16[128,1536]{1,0:T(8,128)(2,1)S(1)}, bf16[128,1536]{1,0:T(8,128)(2,1)S(1)}, u32[]{:S(2)}, u32[]{:S(2)}) %collective-permute-start.3) | collective-permute-done | bytes 393248 | tf_op jit(solution)/shard_map/ppermute | solution.py:286
  91.2 0.0 collective-permute-done.2
  91.2 0.1 add_convert_fusion
  91.3 1.1 %maximum_select_fusion = bf16[128,3072]{1,0:T(8,128)(2,1)} fusion(bf16[128,1536]{1,0:T(8,128)(2,1)S(1)} %add_convert_fusion, bf16[128,1536]{1,0:T(8,128)(2,1)S(1)} %add_convert_fusion.1, pred[]{:T(512)S(6)} %eq.5), kind=kLoop, calls=%fused_computation.6 | loop fusion | flops 3538944 | bytes 1572865 | tf_op jit(solution)/shard_map/jit(_where)/select_n | solution.py:291
  (2 shorter events, 0.0 us)
Async XLA Ops:
  6.5 1.1 %copy-start = (bf16[128,3072]{1,0:T(8,128)(2,1)S(1)}, bf16[128,3072]{1,0:T(8,128)(2,1)}, u32[]{:S(2)}) copy-start(bf16[128,3072]{1,0:T(8,128)(2,1)} %param.13) | copy-start | bytes 2359300
  6.5 62.7 %all-gather.2.cloned.1.call-start = ((), (), s32[]{:S(2)}) async-start(), calls=%async_computation | async-start | bytes 3538944 | tf_op jit(solution)/shard_map/all_gather | solution.py:273
  65.5 7.5 %collective-permute-start.1 = (bf16[256,1024]{0,1:T(8,128)(2,1)S(1)}, bf16[256,1024]{0,1:T(8,128)(2,1)S(1)}, u32[]{:S(2)}, u32[]{:S(2)}) collective-permute-start(bf16[256,1024]{0,1:T(8,128)(2,1)S(1)} %bitcast.13), channel_id=1, source_target_pairs={{0,16},{16,0},{32,48},{48,32},{64,80},{80,64},{96,112},{112,96},{1... | collective-permute-start | bytes 1572872 | tf_op jit(solution)/shard_map/ppermute | solution.py:283
  69.2 3.2 %copy-start.1 = (bf16[1024,1536]{1,0:T(8,128)(2,1)S(1)}, bf16[1024,1536]{1,0:T(8,128)(2,1)}, u32[]{:S(2)}) copy-start(bf16[1024,1536]{1,0:T(8,128)(2,1)} %all-gather.2.cloned.1.call-done) | copy-start | bytes 9437188
  71.9 8.3 %collective-permute-start = (bf16[128,1536]{1,0:T(8,128)(2,1)S(1)}, bf16[128,1536]{1,0:T(8,128)(2,1)S(1)}, u32[]{:S(2)}, u32[]{:S(2)}) collective-permute-start(bf16[128,1536]{1,0:T(8,128)(2,1)S(1)} %convolution_convert_fusion.1), channel_id=1, source_target_pairs={{0,8},{8,0},{1,9},{9,1},{2,10},{10,2},{3,11},{11,3},{4,12},{12,4},... | collective-permute-start | bytes 1179656 | tf_op jit(solution)/shard_map/ppermute | solution.py:284
  73.6 17.6 %collective-permute-start.2 = (f32[128,1536]{1,0:T(8,128)S(1)}, f32[128,1536]{1,0:T(8,128)S(1)}, u32[]{:S(2)}, u32[]{:S(2)}) collective-permute-start(f32[128,1536]{1,0:T(8,128)S(1)} %fusion.4), channel_id=1, source_target_pairs={{0,16},{16,0},{32,48},{48,32},{64,80},{80,64},{96,112},{112,96},{1... | collective-permute-start | bytes 2359304 | tf_op jit(solution)/shard_map/ppermute | solution.py:288
  77.3 13.9 %collective-permute-start.3 = (bf16[128,1536]{1,0:T(8,128)(2,1)S(1)}, bf16[128,1536]{1,0:T(8,128)(2,1)S(1)}, u32[]{:S(2)}, u32[]{:S(2)}) collective-permute-start(bf16[128,1536]{1,0:T(8,128)(2,1)S(1)} %convolution_convert_fusion), channel_id=1, source_target_pairs={{0,24},{8,16},{16,8},{24,0},{32,56},{40,48},{48,40},{56,32},{64,88... | collective-permute-start | bytes 1179656 | tf_op jit(solution)/shard_map/ppermute | solution.py:286
Sparse Core Ops, SparseCore 0:
  9.1 60.0 all-gather.1

commit v19 on v18

--- a/solution.py
+++ b/solution.py
@@ -254,6 +254,24 @@
     )(q, k, v, bias)
 
 
+def half_kernel(w_ref, o_ref, sem):
+    core = lax.axis_index("frame") % 2
+    half = o_ref.shape[1]
+    copy = pltpu.make_async_copy(w_ref.at[:, pl.ds(pl.multiple_of(core * half, 128), half)], o_ref, sem)
+    copy.start()
+    copy.wait()
+
+
+def column_half(w):
+    return pl.pallas_call(
+        half_kernel,
+        out_shape=jax.ShapeDtypeStruct((w.shape[0], w.shape[1] // 2), w.dtype),
+        in_specs=[pl.BlockSpec(memory_space=pl.ANY)],
+        out_specs=pl.BlockSpec(memory_space=pl.ANY),
+        scratch_shapes=[pltpu.SemaphoreType.DMA(())],
+    )(w)
+
+
 def on_device(queries, keys, values, block_mask, out_weight):
     tok_dev = queries.shape[0]
     frames_here = tok_dev // (TROWS * TCOLS * TILE)
@@ -269,7 +287,7 @@
     sides = lax.axis_size("hy")
     half = out_weight.shape[1] // 2
     partners = [(i, i ^ 1) for i in range(count)]
-    weight_half = lax.dynamic_slice_in_dim(out_weight, core * half, half, axis=1)
+    weight_half = column_half(out_weight)
     weight_half = lax.all_gather(weight_half, "hz", axis=0, tiled=True)
     peers = lax.axis_size("hz")
     mine = got.transpose(1, 0, 2).reshape(tok_dev // peers, peers * HEAD_DIM)

time: 101 us -> 114 us (1.13)
  Pallas kernels: 51.2 us -> 63.2 us
  local copies, waits for them, and re-layouts: 4.96 us -> 3.05 us
  waiting for transfers between devices: 15.9 us -> 17.8 us
  starting transfers between devices: 5.2 us -> 6.41 us
    pallas_call x0 -> x1, Pallas kernels: none -> 13 us  [column_half(): pl.pallas_call(half_kernel, out_shape=jax.ShapeDtypeStruct((w.shape[0], w...]
    ppermute x1, waiting for transfers between devices: 2.1 us -> 7.64 us  [on_device(): lax.ppermute(project(mine, 1 - side).astype(jnp.bfloat16), 'hy', flip)]
    all_gather x1, waiting for transfers between devices: 2.79 us -> 0.04 us  [on_device(): weight_half = lax.all_gather(weight_half, 'hz', axis=0, tiled=True)]
    ppermute x1, waiting for transfers between devices: 11 us -> 8.53 us  [on_device(): lax.ppermute(project(theirs, 1 - side).astype(jnp.bfloat16), ('frame', 'h...]
    ppermute x1, waiting for transfers between devices: 0.01 us -> 1.54 us  [on_device(): theirs = lax.ppermute(mine, 'frame', partners)]
  transfers between devices with their start and end apart: 5 -> 5, of which waited for: 3 -> 3; matrix products, arithmetic and copies ran while one was open for 10% -> 7% of each run, Pallas kernels for 52% -> 45%
where the time goes in v19:
time: 114 us; the launch traced here: 112 us
  Pallas kernels  63.2 us (55%)
  waiting for transfers between devices  17.8 us (16%)
  between operations  13.5 us (12%)
  starting transfers between devices  6.41 us (6%)
  matrix products  5.53 us (5%)
  local copies, waits for them, and re-layouts  3.05 us (3%)
  other arithmetic  2.96 us (3%)
    pallas_call x1, Pallas kernels, attend(): pl.pallas_call(attention_kernel, grid=(TROWS, GROUPS), in_specs=[pl.Block...  50.2 us
    pallas_call x1, Pallas kernels, column_half(): pl.pallas_call(half_kernel, out_shape=jax.ShapeDtypeStruct((w.shape[0], w...  13 us
    ppermute x1, waiting for transfers between devices, on_device(): lax.ppermute(project(theirs, 1 - side).astype(jnp.bfloat16), ('frame', 'h...  8.53 us
    ppermute x1, waiting for transfers between devices, on_device(): lax.ppermute(project(mine, 1 - side).astype(jnp.bfloat16), 'hy', flip)  7.64 us
    dot_general x4, matrix products, project(): return jnp.dot(rows, weight_half, preferred_element_type=jnp.float32)  4.48 us
    ppermute x1, starting transfers between devices, on_device(): from_partner = lax.ppermute(project(theirs, side), 'frame', partners)  2.95 us
  transfers between devices with their start and end apart: 5, of which 3 were waited for; matrix products, arithmetic and copies ran while one was open for 7% of the time, Pallas kernels for 45%

profile of v19, /device:TPU:17, one launch (start us, length us, event | category | flops | bytes accessed | tf_op | source)
XLA Modules:
  0.0 112.4 jit_solution(14997228117251186628)
XLA Ops:
  6.5 0.0 all-gather.2.cloned.1.call-start
  6.5 13.0 %shard_map.92 = bf16[128,1536]{1,0:T(8,128)(2,1)} custom-call(bf16[128,3072]{1,0:T(8,128)(2,1)} %w_ref.1), custom_call_target="tpu_custom_call" | custom-call | tf_op jit(solution)/shard_map/pallas_call | solution.py:266
  19.6 0.0 all-gather.2.cloned.1.call-update
  19.6 0.7 convert_bitcast_fusion
  20.3 1.0 fusion.2
  21.4 0.1 reshape.19
  21.5 1.0 fusion.11
  22.6 0.4 broadcast_in_dim.16
  23.0 0.3 reshape.14
  23.2 1.0 copy.14.bias_ref
  24.2 50.2 %shard_map.91 = bf16[8,256,128]{2,1,0:T(8,128)(2,1)} custom-call(bf16[2048,128]{1,0:T(8,128)(2,1)} %q_ref.1, bf16[2048,128]{1,0:T(8,128)(2,1)} %k_ref.1, bf16[2048,128]{1,0:T(8,128)(2,1)} %v_ref.1, f32[16,2,3456]{2,1,0:T(2,128)} %copy.14.bias_ref), custom_call_target="tpu_custom_call" | custom-call | tf_op jit(solution)/shard_map/pallas_call | solution.py:235
  74.4 1.3 %copy.15 = bf16[256,8,128]{0,2,1:T(8,128)(2,1)S(1)} copy(bf16[256,8,128]{2,0,1:T(8,128)(2,1)} %bitcast.16) | data formatting | bytes 1048576 | tf_op jit(solution)/shard_map/transpose | solution.py:293
  75.7 1.6 %collective-permute-start.1 = (bf16[256,1024]{0,1:T(8,128)(2,1)S(1)}, bf16[256,1024]{0,1:T(8,128)(2,1)S(1)}, u32[]{:S(2)}, u32[]{:S(2)}) collective-permute-start(bf16[256,1024]{0,1:T(8,128)(2,1)S(1)} %bitcast.13), channel_id=1, source_target_pairs={{0,16},{16,0},{32,48},{48,32},{64,80},{80,64},{96,112},{112,96},{1... | collective-permute-start | bytes 1572872 | tf_op jit(solution)/shard_map/ppermute | solution.py:301
  77.3 1.5 %collective-permute-done.1 = bf16[256,1024]{0,1:T(8,128)(2,1)S(1)} collective-permute-done((bf16[256,1024]{0,1:T(8,128)(2,1)S(1)}, bf16[256,1024]{0,1:T(8,128)(2,1)S(1)}, u32[]{:S(2)}, u32[]{:S(2)}) %collective-permute-start.1) | collective-permute-done | bytes 524320 | tf_op jit(solution)/shard_map/ppermute | solution.py:301
  78.8 0.0 all-gather.2.cloned.1.call-done
  78.8 0.0 copy-start
  78.8 2.6 %fusion.4 = f32[128,1536]{1,0:T(8,128)S(1)} fusion(bf16[1024,1536]{1,0:T(8,128)(2,1)} %all-gather.2.cloned.1.call-done, bf16[256,1024]{0,1:T(8,128)(2,1)S(1)} %collective-permute-done.1, s32[]{:T(128)S(6)} %select_n.30), kind=kOutput, calls=%fused_computation.12 | convolution fusion | flops 402653184 | bytes 4194308 | tf_op jit(solution)/shard_map/dot_general | solution.py:298
  81.5 2.9 %collective-permute-start.2 = (f32[128,1536]{1,0:T(8,128)S(1)}, f32[128,1536]{1,0:T(8,128)S(1)}, u32[]{:S(2)}, u32[]{:S(2)}) collective-permute-start(f32[128,1536]{1,0:T(8,128)S(1)} %fusion.4), channel_id=1, source_target_pairs={{0,16},{16,0},{32,48},{48,32},{64,80},{80,64},{96,112},{112,96},{1... | collective-permute-start | bytes 2359304 | tf_op jit(solution)/shard_map/ppermute | solution.py:306
  84.4 0.0 copy-done
  84.4 0.6 convolution_convert_fusion.1
  85.1 1.6 %collective-permute-start = (bf16[128,1536]{1,0:T(8,128)(2,1)S(1)}, bf16[128,1536]{1,0:T(8,128)(2,1)S(1)}, u32[]{:S(2)}, u32[]{:S(2)}) collective-permute-start(bf16[128,1536]{1,0:T(8,128)(2,1)S(1)} %convolution_convert_fusion.1), channel_id=1, source_target_pairs={{0,8},{8,0},{1,9},{9,1},{2,10},{10,2},{3,11},{11,3},{4,12},{12,4},... | collective-permute-start | bytes 1179656 | tf_op jit(solution)/shard_map/ppermute | solution.py:302
  86.6 0.6 convolution_convert_fusion
  87.3 0.3 collective-permute-start.3
  87.6 0.6 fusion.7
  88.2 7.6 %collective-permute-done = bf16[128,1536]{1,0:T(8,128)(2,1)S(1)} collective-permute-done((bf16[128,1536]{1,0:T(8,128)(2,1)S(1)}, bf16[128,1536]{1,0:T(8,128)(2,1)S(1)}, u32[]{:S(2)}, u32[]{:S(2)}) %collective-permute-start) | collective-permute-done | bytes 393248 | tf_op jit(solution)/shard_map/ppermute | solution.py:302
  95.8 0.1 add_convert_fusion.1
  95.9 8.5 %collective-permute-done.3 = bf16[128,1536]{1,0:T(8,128)(2,1)S(1)} collective-permute-done((bf16[128,1536]{1,0:T(8,128)(2,1)S(1)}, bf16[128,1536]{1,0:T(8,128)(2,1)S(1)}, u32[]{:S(2)}, u32[]{:S(2)}) %collective-permute-start.3) | collective-permute-done | bytes 393248 | tf_op jit(solution)/shard_map/ppermute | solution.py:304
  104.4 0.0 collective-permute-done.2
  104.4 0.1 add_convert_fusion
  104.5 1.1 maximum_select_fusion
  (2 shorter events, 0.0 us)
Async XLA Ops:
  6.5 72.3 %all-gather.2.cloned.1.call-start = ((), (), s32[]{:S(2)}) async-start(), calls=%async_computation | async-start | bytes 3538944 | tf_op jit(solution)/shard_map/all_gather | solution.py:291
  75.7 3.1 %collective-permute-start.1 = (bf16[256,1024]{0,1:T(8,128)(2,1)S(1)}, bf16[256,1024]{0,1:T(8,128)(2,1)S(1)}, u32[]{:S(2)}, u32[]{:S(2)}) collective-permute-start(bf16[256,1024]{0,1:T(8,128)(2,1)S(1)} %bitcast.13), channel_id=1, source_target_pairs={{0,16},{16,0},{32,48},{48,32},{64,80},{80,64},{96,112},{112,96},{1... | collective-permute-start | bytes 1572872 | tf_op jit(solution)/shard_map/ppermute | solution.py:301
  78.8 5.6 %copy-start = (bf16[1024,1536]{1,0:T(8,128)(2,1)S(1)}, bf16[1024,1536]{1,0:T(8,128)(2,1)}, u32[]{:S(2)}) copy-start(bf16[1024,1536]{1,0:T(8,128)(2,1)} %all-gather.2.cloned.1.call-done) | copy-start | bytes 9437188
  81.5 23.0 %collective-permute-start.2 = (f32[128,1536]{1,0:T(8,128)S(1)}, f32[128,1536]{1,0:T(8,128)S(1)}, u32[]{:S(2)}, u32[]{:S(2)}) collective-permute-start(f32[128,1536]{1,0:T(8,128)S(1)} %fusion.4), channel_id=1, source_target_pairs={{0,16},{16,0},{32,48},{48,32},{64,80},{80,64},{96,112},{112,96},{1... | collective-permute-start | bytes 2359304 | tf_op jit(solution)/shard_map/ppermute | solution.py:306
  85.1 10.8 %collective-permute-start = (bf16[128,1536]{1,0:T(8,128)(2,1)S(1)}, bf16[128,1536]{1,0:T(8,128)(2,1)S(1)}, u32[]{:S(2)}, u32[]{:S(2)}) collective-permute-start(bf16[128,1536]{1,0:T(8,128)(2,1)S(1)} %convolution_convert_fusion.1), channel_id=1, source_target_pairs={{0,8},{8,0},{1,9},{9,1},{2,10},{10,2},{3,11},{11,3},{4,12},{12,4},... | collective-permute-start | bytes 1179656 | tf_op jit(solution)/shard_map/ppermute | solution.py:302
  87.3 17.2 %collective-permute-start.3 = (bf16[128,1536]{1,0:T(8,128)(2,1)S(1)}, bf16[128,1536]{1,0:T(8,128)(2,1)S(1)}, u32[]{:S(2)}, u32[]{:S(2)}) collective-permute-start(bf16[128,1536]{1,0:T(8,128)(2,1)S(1)} %convolution_convert_fusion), channel_id=1, source_target_pairs={{0,24},{8,16},{16,8},{24,0},{32,56},{40,48},{48,40},{56,32},{64,88... | collective-permute-start | bytes 1179656 | tf_op jit(solution)/shard_map/ppermute | solution.py:304
Sparse Core Ops, SparseCore 0:
  19.7 59.0 all-gather.1

commit v20 on v18

--- a/solution.py
+++ b/solution.py
@@ -281,9 +281,12 @@
 
     flip = [(0, 1), (1, 0)]
     theirs = lax.ppermute(mine, "frame", partners)
-    sent_mine = lax.ppermute(project(mine, 1 - side).astype(jnp.bfloat16), "hy", flip)
+    away = lambda x: lax.dynamic_slice_in_dim(x, (1 - side) * block, block, axis=0)
+    both = jnp.dot(jnp.concatenate([away(mine), away(theirs)]), weight_half,
+                   preferred_element_type=jnp.float32).astype(jnp.bfloat16)
+    sent_mine = lax.ppermute(both[:block], "hy", flip)
     diagonal = [(f * sides + h, (f ^ 1) * sides + (sides - 1 - h)) for f in range(count) for h in range(sides)]
-    sent_cross = lax.ppermute(project(theirs, 1 - side).astype(jnp.bfloat16), ("frame", "hy"), diagonal)
+    sent_cross = lax.ppermute(both[block:], ("frame", "hy"), diagonal)
     own_mine = lax.optimization_barrier(project(mine, side))
     from_partner = lax.ppermute(project(theirs, side), "frame", partners)
     other_half = (from_partner + sent_cross.astype(jnp.float32)).astype(jnp.bfloat16)

time: 101 us -> 102 us (level)
    dot_general x4 -> x2, matrix products: 4.48 us -> 1.21 us  [project(): return jnp.dot(rows, weight_half, preferred_element_type=jnp.float32)]
    dot_general x0 -> x1, matrix products: none -> 3.03 us  [on_device(): jnp.dot(jnp.concatenate([away(mine), away(theirs)]), weight_half, preferr...]
    all_gather x1, waiting for transfers between devices: 2.79 us -> 1.24 us  [on_device(): weight_half = lax.all_gather(weight_half, 'hz', axis=0, tiled=True)]
    ppermute x1, waiting for transfers between devices: 0.01 us -> 1.52 us  [on_device(): theirs = lax.ppermute(mine, 'frame', partners)]
  transfers between devices with their start and end apart: 5 -> 5, of which waited for: 3 -> 4; matrix products, arithmetic and copies ran while one was open for 10% -> 7% of each run, Pallas kernels for 52% -> 51%
where the time goes in v20:
time: 102 us; the launch traced here: 99.7 us
  Pallas kernels  50.7 us (50%)
  waiting for transfers between devices  16.5 us (16%)
  between operations  13.5 us (13%)
  starting transfers between devices  5.68 us (6%)
  matrix products  5.29 us (5%)
  local copies, waits for them, and re-layouts  5.05 us (5%)
  other arithmetic  3 us (3%)
    pallas_call x1, Pallas kernels, attend(): pl.pallas_call(attention_kernel, grid=(TROWS, GROUPS), in_specs=[pl.Block...  50.7 us
    ppermute x1, waiting for transfers between devices, on_device(): sent_cross = lax.ppermute(both[block:], ('frame', 'hy'), diagonal)  11 us
    dot_general x1, matrix products, on_device(): jnp.dot(jnp.concatenate([away(mine), away(theirs)]), weight_half, preferr...  3.03 us
    ppermute x1, waiting for transfers between devices, on_device(): sent_mine = lax.ppermute(both[:block], 'hy', flip)  2.75 us
    ppermute x1, starting transfers between devices, on_device(): from_partner = lax.ppermute(project(theirs, side), 'frame', partners)  2.39 us
  transfers between devices with their start and end apart: 5, of which 4 were waited for; matrix products, arithmetic and copies ran while one was open for 7% of the time, Pallas kernels for 51%

profile of v20, /device:TPU:17, one launch (start us, length us, event | category | flops | bytes accessed | tf_op | source)
XLA Modules:
  0.0 99.7 jit_solution(12956470115440907206)
XLA Ops:
  6.5 0.0 copy-start
  6.5 0.0 all-gather.2.cloned.1.call-start
  6.5 1.1 %copy-done = bf16[128,3072]{1,0:T(8,128)(2,1)S(1)} copy-done((bf16[128,3072]{1,0:T(8,128)(2,1)S(1)}, bf16[128,3072]{1,0:T(8,128)(2,1)}, u32[]{:S(2)}) %copy-start) | copy-done | bytes 786456
  7.7 0.8 constant_dynamic-slice_fusion.2
  8.4 0.0 all-gather.2.cloned.1.call-update
  8.5 0.7 convert_bitcast_fusion
  9.2 1.0 %fusion.2 = pred[4,8,54]{2,0,1:T(4,128)(4,1)S(1)} fusion(pred[8,54,4]{1,2,0:T(4,128)(4,1)} %constant.59, pred[8,54,4]{1,2,0:T(4,128)(4,1)} %constant.57, bf16[8,45,54]{2,1,0:T(8,128)(2,1)} %constant.80, bf16[4,8,45]{2,1,0:T(8,128)(2,1)S(1)} %convert_bitcast_fusion), kind=kOutput, calls=%fused_computation.4 | convolution fusion | flops 160704 | bytes 46944 | tf_op jit(solution)/shard_map/rcw,cwk->rck/dot_general | solution.py:67
  10.3 0.1 reshape.19
  10.4 1.0 %fusion.12 = f32[16,2,9,6]{3,2,1,0:T(8,128)S(1)} fusion(pred[16,2,9,6]{3,2,1,0:T(8,128)(4,1)S(1)} %reshape.19, s32[16,2,9,6]{3,2,1,0:T(8,128)} %constant.52.clone, s32[]{:T(128)S(6)} %axis_index.29), kind=kLoop, calls=%fused_computation.19 | loop fusion | flops 10368 | bytes 15556 | tf_op jit(solution)/shard_map/jit(_where)/select_n | solution.py:72
  11.5 0.4 broadcast_in_dim.16
  11.8 0.3 reshape.14
  12.1 1.0 %copy.14.bias_ref = f32[16,2,3456]{2,1,0:T(2,128)} copy(f32[16,2,3456]{2,0,1:T(8,128)S(1)} %reshape.14) | data formatting | bytes 884736 | tf_op jit(solution)/shard_map/reshape | solution.py:74
  13.1 50.7 %shard_map.91 = bf16[8,256,128]{2,1,0:T(8,128)(2,1)} custom-call(bf16[2048,128]{1,0:T(8,128)(2,1)} %q_ref.1, bf16[2048,128]{1,0:T(8,128)(2,1)} %k_ref.1, bf16[2048,128]{1,0:T(8,128)(2,1)} %v_ref.1, f32[16,2,3456]{2,1,0:T(2,128)} %copy.14.bias_ref), custom_call_target="tpu_custom_call" | custom-call | tf_op jit(solution)/shard_map/pallas_call | solution.py:235
  63.8 1.3 %copy.15 = bf16[256,8,128]{0,2,1:T(8,128)(2,1)S(1)} copy(bf16[256,8,128]{2,0,1:T(8,128)(2,1)} %bitcast.15) | data formatting | bytes 1048576 | tf_op jit(solution)/shard_map/transpose | solution.py:275
  65.1 1.4 %collective-permute-start = (bf16[256,1024]{0,1:T(8,128)(2,1)S(1)}, bf16[256,1024]{0,1:T(8,128)(2,1)S(1)}, u32[]{:S(2)}, u32[]{:S(2)}) collective-permute-start(bf16[256,1024]{0,1:T(8,128)(2,1)S(1)} %bitcast.12), channel_id=1, source_target_pairs={{0,16},{16,0},{32,48},{48,32},{64,80},{80,64},{96,112},{112,96},{1... | collective-permute-start | bytes 1572872 | tf_op jit(solution)/shard_map/ppermute | solution.py:283
  66.4 1.5 %collective-permute-done = bf16[256,1024]{0,1:T(8,128)(2,1)S(1)} collective-permute-done((bf16[256,1024]{0,1:T(8,128)(2,1)S(1)}, bf16[256,1024]{0,1:T(8,128)(2,1)S(1)}, u32[]{:S(2)}, u32[]{:S(2)}) %collective-permute-start) | collective-permute-done | bytes 524320 | tf_op jit(solution)/shard_map/ppermute | solution.py:283
  68.0 1.2 %all-gather.2.cloned.1.call-done = bf16[1024,1536]{1,0:T(8,128)(2,1)} async-done(((bf16[128,1536]{1,0:T(8,128)(2,1)}), bf16[1024,1536]{1,0:T(8,128)(2,1)}) %all-gather.2.cloned.1.call-update) | async-done | bytes 3145744 | tf_op jit(solution)/shard_map/all_gather | solution.py:273
  69.2 0.0 copy-start.1
  69.2 3.0 %convolution_convert_fusion = bf16[256,1536]{1,0:T(8,128)(2,1)S(1)} fusion(bf16[1024,1536]{1,0:T(8,128)(2,1)} %all-gather.2.cloned.1.call-done, bf16[128,1024]{0,1:T(8,128)(2,1)S(1)} %constant_dynamic-slice_fusion, bf16[128,1024]{0,1:T(8,128)(2,1)S(1)} %constant_dynamic-slice_fusion.1), kind=kOutput, calls=%fused_computation | convolution fusion | flops 806748160 | bytes 4456448 | tf_op jit(solution)/shard_map/dot_general | solution.py:285
  72.2 0.1 fusion.17
  72.3 1.3 %collective-permute-start.1 = (bf16[128,1536]{1,0:T(8,128)(2,1)S(1)}, bf16[128,1536]{1,0:T(8,128)(2,1)S(1)}, u32[]{:S(2)}, u32[]{:S(2)}) collective-permute-start(bf16[128,1536]{1,0:T(8,128)(2,1)S(1)} %get-tuple-element.5), channel_id=1, source_target_pairs={{0,8},{8,0},{1,9},{9,1},{2,10},{10,2},{3,11},{11,3},{4,12},{12,4},... | collective-permute-start | bytes 1179656 | tf_op jit(solution)/shard_map/ppermute | solution.py:287
  73.6 0.0 copy-done.1
  73.6 0.6 fusion.6
  74.2 2.4 %collective-permute-start.2 = (f32[128,1536]{1,0:T(8,128)S(1)}, f32[128,1536]{1,0:T(8,128)S(1)}, u32[]{:S(2)}, u32[]{:S(2)}) collective-permute-start(f32[128,1536]{1,0:T(8,128)S(1)} %fusion.6), channel_id=1, source_target_pairs={{0,16},{16,0},{32,48},{48,32},{64,80},{80,64},{96,112},{112,96},{1... | collective-permute-start | bytes 2359304 | tf_op jit(solution)/shard_map/ppermute | solution.py:291
  76.6 0.6 fusion.8
  77.2 0.7 collective-permute-start.3
  77.9 2.7 %collective-permute-done.1 = bf16[128,1536]{1,0:T(8,128)(2,1)S(1)} collective-permute-done((bf16[128,1536]{1,0:T(8,128)(2,1)S(1)}, bf16[128,1536]{1,0:T(8,128)(2,1)S(1)}, u32[]{:S(2)}, u32[]{:S(2)}) %collective-permute-start.1) | collective-permute-done | bytes 393248 | tf_op jit(solution)/shard_map/ppermute | solution.py:287
  80.6 0.1 add_convert_fusion.1
  80.7 11.0 %collective-permute-done.3 = bf16[128,1536]{1,0:T(8,128)(2,1)S(1)} collective-permute-done((bf16[128,1536]{1,0:T(8,128)(2,1)S(1)}, bf16[128,1536]{1,0:T(8,128)(2,1)S(1)}, u32[]{:S(2)}, u32[]{:S(2)}) %collective-permute-start.3) | collective-permute-done | bytes 393248 | tf_op jit(solution)/shard_map/ppermute | solution.py:289
  91.7 0.0 collective-permute-done.2
  91.7 0.1 add_convert_fusion
  91.8 1.1 %maximum_select_fusion = bf16[128,3072]{1,0:T(8,128)(2,1)} fusion(bf16[128,1536]{1,0:T(8,128)(2,1)S(1)} %add_convert_fusion, bf16[128,1536]{1,0:T(8,128)(2,1)S(1)} %add_convert_fusion.1, pred[]{:T(512)S(6)} %eq.5), kind=kLoop, calls=%fused_computation.5 | loop fusion | flops 3538944 | bytes 1572865 | tf_op jit(solution)/shard_map/jit(_where)/select_n | solution.py:294
  (4 shorter events, 0.1 us)
Async XLA Ops:
  6.5 1.1 %copy-start = (bf16[128,3072]{1,0:T(8,128)(2,1)S(1)}, bf16[128,3072]{1,0:T(8,128)(2,1)}, u32[]{:S(2)}) copy-start(bf16[128,3072]{1,0:T(8,128)(2,1)} %param.13) | copy-start | bytes 2359300
  6.5 62.7 %all-gather.2.cloned.1.call-start = ((), (), s32[]{:S(2)}) async-start(), calls=%async_computation | async-start | bytes 3538944 | tf_op jit(solution)/shard_map/all_gather | solution.py:273
  65.1 2.9 %collective-permute-start = (bf16[256,1024]{0,1:T(8,128)(2,1)S(1)}, bf16[256,1024]{0,1:T(8,128)(2,1)S(1)}, u32[]{:S(2)}, u32[]{:S(2)}) collective-permute-start(bf16[256,1024]{0,1:T(8,128)(2,1)S(1)} %bitcast.12), channel_id=1, source_target_pairs={{0,16},{16,0},{32,48},{48,32},{64,80},{80,64},{96,112},{112,96},{1... | collective-permute-start | bytes 1572872 | tf_op jit(solution)/shard_map/ppermute | solution.py:283
  69.2 4.4 %copy-start.1 = (bf16[1024,1536]{1,0:T(8,128)(2,1)S(1)}, bf16[1024,1536]{1,0:T(8,128)(2,1)}, u32[]{:S(2)}) copy-start(bf16[1024,1536]{1,0:T(8,128)(2,1)} %all-gather.2.cloned.1.call-done) | copy-start | bytes 9437188
  72.3 8.3 %collective-permute-start.1 = (bf16[128,1536]{1,0:T(8,128)(2,1)S(1)}, bf16[128,1536]{1,0:T(8,128)(2,1)S(1)}, u32[]{:S(2)}, u32[]{:S(2)}) collective-permute-start(bf16[128,1536]{1,0:T(8,128)(2,1)S(1)} %get-tuple-element.5), channel_id=1, source_target_pairs={{0,8},{8,0},{1,9},{9,1},{2,10},{10,2},{3,11},{11,3},{4,12},{12,4},... | collective-permute-start | bytes 1179656 | tf_op jit(solution)/shard_map/ppermute | solution.py:287
  74.2 17.5 %collective-permute-start.2 = (f32[128,1536]{1,0:T(8,128)S(1)}, f32[128,1536]{1,0:T(8,128)S(1)}, u32[]{:S(2)}, u32[]{:S(2)}) collective-permute-start(f32[128,1536]{1,0:T(8,128)S(1)} %fusion.6), channel_id=1, source_target_pairs={{0,16},{16,0},{32,48},{48,32},{64,80},{80,64},{96,112},{112,96},{1... | collective-permute-start | bytes 2359304 | tf_op jit(solution)/shard_map/ppermute | solution.py:291
  77.2 14.5 %collective-permute-start.3 = (bf16[128,1536]{1,0:T(8,128)(2,1)S(1)}, bf16[128,1536]{1,0:T(8,128)(2,1)S(1)}, u32[]{:S(2)}, u32[]{:S(2)}) collective-permute-start(bf16[128,1536]{1,0:T(8,128)(2,1)S(1)} %get-tuple-element.6), channel_id=1, source_target_pairs={{0,24},{8,16},{16,8},{24,0},{32,56},{40,48},{48,40},{56,32},{64,88... | collective-permute-start | bytes 1179656 | tf_op jit(solution)/shard_map/ppermute | solution.py:289
Sparse Core Ops, SparseCore 0:
  9.1 60.0 all-gather.1
